TPU v7x, 32 devices: a whole 2x2x4 slice. The times are simulated.
32 devices in a mesh: dp: 8 (over z, x), tensor: 4 (over y, core).
Axes of the slice: x: 2, y: 2, z: 4, core: 2. Of those that a mesh axis runs over, the one named last changes fastest.
Arguments:
- hidden_in: bfloat16 [2, 2048, 2048], P(None, ('dp', 'tensor')), may hold values from -6 to 6
- attn_gain: bfloat16 [2, 2048], P(None, 'dp'), may hold values from 0.5 to 1.5
- query_weight: bfloat16 [2, 2048, 1536], P(None, 'dp', 'tensor'), may hold values from -0.125 to 0.125
- key_matrix: bfloat16 [2, 2048, 384], P(None, 'dp'), may hold values from -0.125 to 0.125
- value_matrix: bfloat16 [2, 2048, 384], P(None, 'dp'), may hold values from -0.125 to 0.125
- out_weight: bfloat16 [2, 1536, 2048], P(None, 'tensor', 'dp'), may hold values from -2.5 to 2.5
- ffn_gain: bfloat16 [2, 2048], P(None, 'dp'), may hold values from 0.5 to 1.5
- gate_weight: bfloat16 [2, 2048, 4608], P(None, 'dp', 'tensor'), may hold values from -0.125 to 0.125
- up_weight: bfloat16 [2, 2048, 4608], P(None, 'dp', 'tensor'), may hold values from -0.125 to 0.125
- down_weight: bfloat16 [2, 4608, 2048], P(None, 'tensor', 'dp'), may hold values from -0.09375 to 0.09375
- branch_at: int32 [2, 1, 8], replicated, may hold values from 512 to 1024, as said below
- cotangent: bfloat16 [2, 2048, 2048], P(None, ('dp', 'tensor')), may hold values from -6 to 6
Outputs:
- layer_out: float32 [2, 2048, 2048], P(None, ('dp', 'tensor'))
- input_grad: float32 [2, 2048, 2048], P(None, ('dp', 'tensor'))
- grad_attn_gain: float32 [2, 2048], P(None, 'dp')
- grad_query_weight: float32 [2, 2048, 1536], P(None, 'dp', 'tensor')
- grad_key_weight: float32 [2, 2048, 384], P(None, 'dp')
- grad_value_weight: float32 [2, 2048, 384], P(None, 'dp')
- grad_out_weight: float32 [2, 1536, 2048], P(None, 'tensor', 'dp')
- grad_ffn_gain: float32 [2, 2048], P(None, 'dp')
- grad_gate_weight: float32 [2, 2048, 4608], P(None, 'dp', 'tensor')
- grad_up_weight: float32 [2, 2048, 4608], P(None, 'dp', 'tensor')
- grad_down_weight: float32 [2, 4608, 2048], P(None, 'tensor', 'dp')
Inputs may be any that keep to these rules, and one draw needn't show every extreme that they name: `branch_at`: in each group of each micro-batch one continuation begins at 1024 and another at 512.
All inputs are finite; a program needn't handle non-finite values.
Results may differ from a plain program's by a relative error of at most 0.03.
Values may be sent and summed in bfloat16 or wider, within the bound.
No kernel may reach another device: no remote copies, remote signals or barrier semaphores. Data moves between devices by JAX's collectives and lax.ppermute only.
A program may use at most 256 MiB of HBM per device.

v0:
```python
import math

import jax
import jax.numpy as jnp
from jax import lax
from jax.sharding import PartitionSpec as P

QUERY_HEADS = 24
KEY_VALUE_HEADS = 6
HEAD_SIZE = 64
PROMPT = 1024
CONT = 128
NCONT = 8


norm_eps = 1e-06
rope_base = 10000.0
masked_score = -1000000000.0
swap_order = (2, 0, 1)
return_order = (1, 0, 2)


def partner(block, axis, distance):
    count = lax.axis_size(axis)
    route = []
    for low in range(count):
        high = low | 1 << distance
        if high != low and high < count:
            route += [(low, high), (high, low)]
    return lax.ppermute(block, axis, route)


def plain_product(left, right):
    return jnp.dot(left, right, preferred_element_type=jnp.float32)


def dot_left_t(left, right):
    return lax.dot_general(
        left, right, (((0,), (0,)), ((), ())), preferred_element_type=jnp.float32
    )


def dot_right_t(left, right):
    return lax.dot_general(
        left, right, (((1,), (1,)), ((), ())), preferred_element_type=jnp.float32
    )


def rms_forward(hidden, gain):
    inv_root = lax.rsqrt(jnp.mean(hidden * hidden, axis=-1, keepdims=True) + norm_eps)
    scaled = hidden * inv_root
    return (scaled * gain, scaled, inv_root)


def rms_backward(grad_normed, scaled, inv_root, gain):
    grad_gain = jnp.sum(grad_normed * scaled, axis=0)
    grad_scaled = grad_normed * gain
    centred = grad_scaled - scaled * jnp.mean(grad_scaled * scaled, axis=-1, keepdims=True)
    return (inv_root * centred, grad_gain)


def rope_tables(positions):
    half_size = HEAD_SIZE // 2
    inv_freq = rope_base ** (-(2.0 * jnp.arange(half_size, dtype=jnp.float32)) / HEAD_SIZE)
    angles = positions.astype(jnp.float32)[:, None] * inv_freq[None, :]
    return (jnp.cos(angles)[:, None, :], jnp.sin(angles)[:, None, :])


def apply_rotary(values, cosine_table, sine_table, direction):
    half_size = values.shape[-1] // 2
    first_half = values[..., :half_size]
    second_half = values[..., half_size:]
    return jnp.concatenate(
        [
            first_half * cosine_table - direction * second_half * sine_table,
            second_half * cosine_table + direction * first_half * sine_table,
        ],
        axis=-1,
    )


def gather_rows(rows_low):
    return lax.all_gather(rows_low, "tensor", axis=0, tiled=True)


def scatter_rows(partial_rows):
    return lax.psum_scatter(
        partial_rows.astype(jnp.bfloat16), "tensor", scatter_dimension=0, tiled=True
    ).astype(jnp.float32)


def gather_grads(rows_low):
    return lax.all_gather(rows_low, "tensor", axis=0, tiled=True)


def share_prompt(stacked, slot):
    held_part = stacked
    for bit_pos in swap_order:
        arrived = partner(held_part, "dp", bit_pos)
        if bit_pos == 2:
            held_part = jnp.where(slot >= 4, arrived, held_part)
        else:
            lower_side = slot // 2**bit_pos % 2 == 0
            held_part = jnp.where(
                lower_side,
                jnp.concatenate([held_part, arrived], axis=1),
                jnp.concatenate([arrived, held_part], axis=1),
            )
    return held_part


def return_prompt(stacked, slot):
    held_part = stacked
    for bit_pos in return_order:
        if bit_pos == 2:
            kept_part = held_part
            sent_part = held_part
        else:
            half_rows = held_part.shape[1] // 2
            lower_side = slot // 2**bit_pos % 2 == 0
            kept_part = jnp.where(lower_side, held_part[:, :half_rows], held_part[:, half_rows:])
            sent_part = jnp.where(lower_side, held_part[:, half_rows:], held_part[:, :half_rows])
        arrived = partner(sent_part.astype(jnp.bfloat16), "dp", bit_pos).astype(sent_part.dtype)
        if bit_pos == 2:
            held_part = jnp.where(slot < 4, kept_part + arrived, 0.0)
        else:
            held_part = kept_part + arrived
    return held_part


def micro_setup(branch_row, slot, rows_per_rank, own_start, local_row_block):
    local_index = jnp.arange(rows_per_rank, dtype=jnp.int32)
    is_prompt = slot < 4
    cont_offset = jnp.maximum((slot - 4) * rows_per_rank, 0) + local_index
    cont_index = cont_offset // CONT
    matches = cont_index[:, None] == jnp.arange(NCONT, dtype=jnp.int32)[None, :]
    start_pos = jnp.sum(jnp.where(matches, branch_row[None, :], 0), axis=1)
    positions = jnp.where(
        is_prompt, slot * rows_per_rank + local_index, start_pos + cont_offset % CONT
    )
    limits = jnp.where(is_prompt, slot * rows_per_rank, start_pos)
    seq_ids = jnp.where(is_prompt, slot, 4 + cont_index)
    prompt_pos = jnp.arange(PROMPT, dtype=jnp.int32)
    allowed = jnp.concatenate(
        [
            prompt_pos[None, :] < limits[:, None],
            (seq_ids[None, :] == seq_ids[:, None]) & (local_index[None, :] <= local_index[:, None]),
        ],
        axis=1,
    )
    cosine_table, sine_table = rope_tables(positions)
    local_cosine = lax.dynamic_slice_in_dim(cosine_table, own_start, local_row_block, 0)
    local_sine = lax.dynamic_slice_in_dim(sine_table, own_start, local_row_block, 0)
    return (cosine_table, sine_table, local_cosine, local_sine, allowed)


def attend_scores(query_rot, keys_sel, allowed):
    scale_factor = 1.0 / math.sqrt(HEAD_SIZE)
    scores = (
        jnp.einsum("qhd,khd->hqk", query_rot, keys_sel, preferred_element_type=jnp.float32)
        * scale_factor
    )
    return jnp.where(allowed[None], scores, masked_score)


def attend_forward(query_rot, every_key, every_value, allowed, key_head_for_query):
    keys_sel = jnp.take(every_key, key_head_for_query, axis=1)
    values_sel = jnp.take(every_value, key_head_for_query, axis=1)
    scores = attend_scores(query_rot, keys_sel, allowed)
    row_max = jnp.max(scores, axis=-1, keepdims=True)
    log_total = row_max + jnp.log(jnp.sum(jnp.exp(scores - row_max), axis=-1, keepdims=True))
    attn_probs = jnp.exp(scores - log_total).astype(jnp.bfloat16)
    attended = jnp.einsum(
        "hqk,khd->qhd", attn_probs, values_sel, preferred_element_type=jnp.float32
    )
    return (attended.astype(jnp.bfloat16), log_total)


def attend_backward(
    grad_attended,
    query_rot,
    every_key,
    every_value,
    allowed,
    key_head_for_query,
    head_indicator,
    log_total,
):
    scale_factor = 1.0 / math.sqrt(HEAD_SIZE)
    keys_sel = jnp.take(every_key, key_head_for_query, axis=1)
    values_sel = jnp.take(every_value, key_head_for_query, axis=1)
    scores = attend_scores(query_rot, keys_sel, allowed)
    attn_probs = jnp.exp(scores - log_total)
    probs_low = attn_probs.astype(jnp.bfloat16)
    grad_probs = jnp.einsum(
        "qhd,khd->hqk", grad_attended, values_sel, preferred_element_type=jnp.float32
    )
    grad_values_sel = jnp.einsum(
        "hqk,qhd->khd", probs_low, grad_attended, preferred_element_type=jnp.float32
    )
    grad_scores = attn_probs * (
        grad_probs - jnp.sum(attn_probs * grad_probs, axis=-1, keepdims=True)
    )
    grad_scores = grad_scores.astype(jnp.bfloat16)
    grad_query_rot = (
        jnp.einsum("hqk,khd->qhd", grad_scores, keys_sel, preferred_element_type=jnp.float32)
        * scale_factor
    )
    grad_keys_sel = (
        jnp.einsum("hqk,qhd->khd", grad_scores, query_rot, preferred_element_type=jnp.float32)
        * scale_factor
    )
    key_gradient = jnp.einsum(
        "khd,hg->kgd", grad_keys_sel, head_indicator, precision=lax.Precision.HIGHEST
    )
    value_gradient = jnp.einsum(
        "khd,hg->kgd", grad_values_sel, head_indicator, precision=lax.Precision.HIGHEST
    )
    return (grad_query_rot, key_gradient, value_gradient)


def forward_step(weights, hidden, setup, slot, key_head_for_query):
    (
        gain_attn,
        weight_q,
        key_projection,
        value_projection,
        weight_o,
        gain_ffn,
        weight_g,
        weight_u,
        weight_d,
    ) = weights
    cosine_table, sine_table, local_cosine, local_sine, allowed = setup
    normalized, scaled, inv_root = rms_forward(hidden, gain_attn.astype(jnp.float32))
    normalized_every = gather_rows(normalized.astype(jnp.bfloat16))
    rows_per_rank = normalized_every.shape[0]
    queries = plain_product(normalized_every, weight_q).reshape(rows_per_rank, -1, HEAD_SIZE)
    query_rot = apply_rotary(queries, cosine_table, sine_table, 1.0).astype(jnp.bfloat16)
    key_entries = plain_product(normalized_every, key_projection).reshape(
        rows_per_rank, KEY_VALUE_HEADS, HEAD_SIZE
    )
    rotary_keys = (
        apply_rotary(key_entries, cosine_table, sine_table, 1.0)
        .astype(jnp.bfloat16)
        .reshape(rows_per_rank, KEY_VALUE_HEADS * HEAD_SIZE)
    )
    value_row_block = plain_product(normalized_every, value_projection).astype(jnp.bfloat16)
    prompt_couple = share_prompt(jnp.stack([rotary_keys, value_row_block]), slot)
    every_key = jnp.concatenate([prompt_couple[0], rotary_keys], axis=0).reshape(
        -1, KEY_VALUE_HEADS, HEAD_SIZE
    )
    every_value = jnp.concatenate([prompt_couple[1], value_row_block], axis=0).reshape(
        -1, KEY_VALUE_HEADS, HEAD_SIZE
    )
    attended, log_total = attend_forward(
        query_rot, every_key, every_value, allowed, key_head_for_query
    )
    attended = attended.reshape(rows_per_rank, -1)
    middle = hidden + scatter_rows(plain_product(attended, weight_o))
    normed_ffn, scaled_ffn, inv_root_ffn = rms_forward(middle, gain_ffn.astype(jnp.float32))
    normed_ffn_all = gather_rows(normed_ffn.astype(jnp.bfloat16))
    gate_vals = plain_product(normed_ffn_all, weight_g)
    up_vals = plain_product(normed_ffn_all, weight_u)
    active = (jax.nn.silu(gate_vals) * up_vals).astype(jnp.bfloat16)
    output = middle + scatter_rows(plain_product(active, weight_d))
    saved = (
        scaled,
        inv_root,
        normalized_every,
        query_rot,
        every_key,
        every_value,
        log_total,
        attended,
        scaled_ffn,
        inv_root_ffn,
        normed_ffn_all,
        gate_vals,
        up_vals,
        active,
    )
    return (saved, output)


def backward_step(
    weights, grad_out, saved, setup, slot, key_head_for_query, head_indicator, own_start
):
    (
        gain_attn,
        weight_q,
        key_projection,
        value_projection,
        weight_o,
        gain_ffn,
        weight_g,
        weight_u,
        weight_d,
    ) = weights
    cosine_table, sine_table, local_cosine, local_sine, allowed = setup
    (
        scaled,
        inv_root,
        normalized_every,
        query_rot,
        every_key,
        every_value,
        log_total,
        attended,
        scaled_ffn,
        inv_root_ffn,
        normed_ffn_all,
        gate_vals,
        up_vals,
        active,
    ) = saved
    rows_per_rank = normalized_every.shape[0]
    local_row_block = grad_out.shape[0]
    grad_ffn_out = gather_grads(grad_out.astype(jnp.bfloat16))
    grad_active = dot_right_t(grad_ffn_out, weight_d)
    sig_gate = jax.nn.sigmoid(gate_vals)
    grad_gate = (grad_active * up_vals * sig_gate * (1.0 + gate_vals * (1.0 - sig_gate))).astype(
        jnp.bfloat16
    )
    grad_up = (grad_active * gate_vals * sig_gate).astype(jnp.bfloat16)
    grad_normed_ffn = lax.psum_scatter(
        (dot_right_t(grad_gate, weight_g) + dot_right_t(grad_up, weight_u)).astype(jnp.bfloat16),
        "tensor",
        scatter_dimension=0,
        tiled=True,
    ).astype(jnp.float32)
    grad_mid_norm, grad_gain_ffn = rms_backward(
        grad_normed_ffn, scaled_ffn, inv_root_ffn, gain_ffn.astype(jnp.float32)
    )
    grad_middle = grad_out + grad_mid_norm
    grad_attn_out = gather_grads(grad_middle.astype(jnp.bfloat16))
    grad_attended = (
        dot_right_t(grad_attn_out, weight_o)
        .astype(jnp.bfloat16)
        .reshape(rows_per_rank, -1, HEAD_SIZE)
    )
    grad_query_rot, key_gradient, value_gradient = attend_backward(
        grad_attended,
        query_rot,
        every_key,
        every_value,
        allowed,
        key_head_for_query,
        head_indicator,
        log_total,
    )
    grad_queries = (
        apply_rotary(grad_query_rot, cosine_table, sine_table, -1.0)
        .astype(jnp.bfloat16)
        .reshape(rows_per_rank, -1)
    )
    key_gradient = key_gradient.reshape(-1, KEY_VALUE_HEADS * HEAD_SIZE)
    value_gradient = value_gradient.reshape(-1, KEY_VALUE_HEADS * HEAD_SIZE)
    prompt_grads = return_prompt(jnp.stack([key_gradient[:PROMPT], value_gradient[:PROMPT]]), slot)
    row_part, key_row_block, value_row_block = (
        lax.psum_scatter(
            dot_right_t(grad_queries, weight_q).astype(jnp.bfloat16),
            "tensor",
            scatter_dimension=0,
            tiled=True,
        ).astype(jnp.float32),
        lax.psum_scatter(
            (key_gradient[PROMPT:] + prompt_grads[0]).astype(jnp.bfloat16),
            "tensor",
            scatter_dimension=0,
            tiled=True,
        ).astype(jnp.float32),
        lax.psum_scatter(
            (value_gradient[PROMPT:] + prompt_grads[1]).astype(jnp.bfloat16),
            "tensor",
            scatter_dimension=0,
            tiled=True,
        ).astype(jnp.float32),
    )
    key_row_block = apply_rotary(
        key_row_block.reshape(local_row_block, KEY_VALUE_HEADS, HEAD_SIZE),
        local_cosine,
        local_sine,
        -1.0,
    )
    key_row_block = key_row_block.reshape(local_row_block, KEY_VALUE_HEADS * HEAD_SIZE).astype(
        jnp.bfloat16
    )
    value_row_block = value_row_block.astype(jnp.bfloat16)
    own_normed = lax.dynamic_slice_in_dim(normalized_every, own_start, local_row_block, 0)
    grad_normed = (
        row_part
        + dot_right_t(key_row_block, key_projection)
        + dot_right_t(value_row_block, value_projection)
    )
    grad_hidden_norm, grad_gain_attn = rms_backward(
        grad_normed, scaled, inv_root, gain_attn.astype(jnp.float32)
    )
    operand_pairs = (
        (normalized_every, grad_queries),
        (own_normed, key_row_block),
        (own_normed, value_row_block),
        (attended, grad_attn_out),
        (normed_ffn_all, grad_gate),
        (normed_ffn_all, grad_up),
        (active, grad_ffn_out),
    )
    return (grad_middle + grad_hidden_norm, grad_gain_attn, grad_gain_ffn, operand_pairs)


def per_device(
    hidden_in,
    attn_gain,
    query_weight,
    key_matrix,
    value_matrix,
    out_weight,
    ffn_gain,
    gate_weight,
    up_weight,
    down_weight,
    branch_at,
    cotangent,
):
    tensor_count = lax.axis_size("tensor")
    rank_index = lax.axis_index("dp")
    tensor_index = lax.axis_index("tensor")
    slot = rank_index % 8
    group_index = rank_index // 8
    micro_count = hidden_in.shape[0]
    local_row_block = hidden_in.shape[1]
    rows_per_rank = local_row_block * tensor_count
    layer_count = attn_gain.shape[0]
    local_heads = query_weight.shape[2] // HEAD_SIZE
    own_start = tensor_index * local_row_block
    key_head_for_query = (
        tensor_index * local_heads + jnp.arange(local_heads, dtype=jnp.int32)
    ) // (QUERY_HEADS // KEY_VALUE_HEADS)
    head_indicator = (
        key_head_for_query[:, None] == jnp.arange(KEY_VALUE_HEADS, dtype=jnp.int32)[None, :]
    ).astype(jnp.float32)
    setups = []
    hidden_now = []
    grad_now = []
    for micro_idx in range(micro_count):
        branch_row = lax.dynamic_index_in_dim(branch_at[micro_idx], group_index, 0, keepdims=False)
        setups.append(micro_setup(branch_row, slot, rows_per_rank, own_start, local_row_block))
        hidden_now.append(hidden_in[micro_idx].astype(jnp.float32))
        grad_now.append(cotangent[micro_idx].astype(jnp.float32))
    gathered_all = []
    caches = []
    for layer_idx in range(layer_count):
        weights = (
            lax.all_gather(attn_gain[layer_idx], "dp", axis=0, tiled=True),
            lax.all_gather(query_weight[layer_idx], "dp", axis=0, tiled=True),
            lax.all_gather(key_matrix[layer_idx], "dp", axis=0, tiled=True),
            lax.all_gather(value_matrix[layer_idx], "dp", axis=0, tiled=True),
            lax.all_gather(out_weight[layer_idx], "dp", axis=1, tiled=True),
            lax.all_gather(ffn_gain[layer_idx], "dp", axis=0, tiled=True),
            lax.all_gather(gate_weight[layer_idx], "dp", axis=0, tiled=True),
            lax.all_gather(up_weight[layer_idx], "dp", axis=0, tiled=True),
            lax.all_gather(down_weight[layer_idx], "dp", axis=1, tiled=True),
        )
        gathered_all.append(weights)
        layer_saved = []
        for micro_idx in range(micro_count):
            saved, hidden_now[micro_idx] = forward_step(
                weights, hidden_now[micro_idx], setups[micro_idx], slot, key_head_for_query
            )
            layer_saved.append(saved)
        caches.append(layer_saved)
    grads_by_layer = [None] * layer_count
    for layer_idx in reversed(range(layer_count)):
        weights = (
            lax.all_gather(attn_gain[layer_idx], "dp", axis=0, tiled=True),
            lax.all_gather(query_weight[layer_idx], "dp", axis=0, tiled=True),
            lax.all_gather(key_matrix[layer_idx], "dp", axis=0, tiled=True),
            lax.all_gather(value_matrix[layer_idx], "dp", axis=0, tiled=True),
            lax.all_gather(out_weight[layer_idx], "dp", axis=1, tiled=True),
            lax.all_gather(ffn_gain[layer_idx], "dp", axis=0, tiled=True),
            lax.all_gather(gate_weight[layer_idx], "dp", axis=0, tiled=True),
            lax.all_gather(up_weight[layer_idx], "dp", axis=0, tiled=True),
            lax.all_gather(down_weight[layer_idx], "dp", axis=1, tiled=True),
        )
        gain_attn_total = jnp.zeros(weights[0].shape, jnp.float32)
        gain_ffn_total = jnp.zeros(weights[5].shape, jnp.float32)
        pair_lists = [[] for member_idx in range(7)]
        for micro_idx in range(micro_count):
            grad_now[micro_idx], gain_a, gain_f, operand_pairs = backward_step(
                weights,
                grad_now[micro_idx],
                caches[layer_idx][micro_idx],
                setups[micro_idx],
                slot,
                key_head_for_query,
                head_indicator,
                own_start,
            )
            gain_attn_total = gain_attn_total + gain_a
            gain_ffn_total = gain_ffn_total + gain_f
            for member_idx in range(7):
                pair_lists[member_idx].append(operand_pairs[member_idx])
        products = []
        for member_idx in range(7):
            left_rows = jnp.concatenate([pair[0] for pair in pair_lists[member_idx]], axis=0)
            right_rows = jnp.concatenate([pair[1] for pair in pair_lists[member_idx]], axis=0)
            products.append(dot_left_t(left_rows, right_rows))
        accums = [
            gain_attn_total,
            products[0],
            products[1],
            products[2],
            products[3],
            gain_ffn_total,
            products[4],
            products[5],
            products[6],
        ]
        grads_by_layer[layer_idx] = accums
    stacked = [
        jnp.stack([grads_by_layer[layer_idx][member_idx] for layer_idx in range(layer_count)])
        for member_idx in range(9)
    ]
    reduced = (
        lax.psum_scatter(
            stacked[0].astype(jnp.bfloat16), "dp", scatter_dimension=1, tiled=True
        ).astype(jnp.float32),
        lax.psum_scatter(
            stacked[1].astype(jnp.bfloat16), "dp", scatter_dimension=1, tiled=True
        ).astype(jnp.float32),
        lax.psum_scatter(
            stacked[2].astype(jnp.bfloat16), "dp", scatter_dimension=1, tiled=True
        ).astype(jnp.float32),
        lax.psum_scatter(
            stacked[3].astype(jnp.bfloat16), "dp", scatter_dimension=1, tiled=True
        ).astype(jnp.float32),
        lax.psum_scatter(
            stacked[4].astype(jnp.bfloat16), "dp", scatter_dimension=2, tiled=True
        ).astype(jnp.float32),
        lax.psum_scatter(
            stacked[5].astype(jnp.bfloat16), "dp", scatter_dimension=1, tiled=True
        ).astype(jnp.float32),
        lax.psum_scatter(
            stacked[6].astype(jnp.bfloat16), "dp", scatter_dimension=1, tiled=True
        ).astype(jnp.float32),
        lax.psum_scatter(
            stacked[7].astype(jnp.bfloat16), "dp", scatter_dimension=1, tiled=True
        ).astype(jnp.float32),
        lax.psum_scatter(
            stacked[8].astype(jnp.bfloat16), "dp", scatter_dimension=2, tiled=True
        ).astype(jnp.float32),
    )
    shared = (
        lax.psum(reduced[0].astype(jnp.bfloat16), "tensor").astype(jnp.float32),
        lax.psum(reduced[2].astype(jnp.bfloat16), "tensor").astype(jnp.float32),
        lax.psum(reduced[3].astype(jnp.bfloat16), "tensor").astype(jnp.float32),
        lax.psum(reduced[5].astype(jnp.bfloat16), "tensor").astype(jnp.float32),
    )
    final_grads = [
        shared[0],
        reduced[1],
        shared[1],
        shared[2],
        reduced[4],
        shared[3],
        reduced[6],
        reduced[7],
        reduced[8],
    ]
    layer_out = jnp.stack(hidden_now)
    input_grad = jnp.stack(grad_now)
    return (
        layer_out,
        input_grad,
        final_grads[0],
        final_grads[1],
        final_grads[2],
        final_grads[3],
        final_grads[4],
        final_grads[5],
        final_grads[6],
        final_grads[7],
        final_grads[8],
    )


def solution(mesh):
    return jax.shard_map(
        per_device,
        mesh=mesh,
        in_specs=(
            P(None, ("dp", "tensor"), None),
            P(None, "dp"),
            P(None, "dp", "tensor"),
            P(None, "dp", None),
            P(None, "dp", None),
            P(None, "tensor", "dp"),
            P(None, "dp"),
            P(None, "dp", "tensor"),
            P(None, "dp", "tensor"),
            P(None, "tensor", "dp"),
            P(),
            P(None, ("dp", "tensor"), None),
        ),
        out_specs=(
            P(None, ("dp", "tensor"), None),
            P(None, ("dp", "tensor"), None),
            P(None, "dp"),
            P(None, "dp", "tensor"),
            P(None, "dp", None),
            P(None, "dp", None),
            P(None, "tensor", "dp"),
            P(None, "dp"),
            P(None, "dp", "tensor"),
            P(None, "dp", "tensor"),
            P(None, "tensor", "dp"),
        ),
        check_vma=False,
    )
```

profile of v0, /device:TPU:1, one launch (start us, length us, event | category | flops | bytes accessed | tf_op | source)
XLA Modules:
  0.0 3200.1 jit_solution(8981989460224780803)
XLA Ops:
  9.3 17.8 all-gather
  48.2 46.0 %all-gather.79.cloned.1.call-done = bf16[1,2048,384]{2,1,0:T(8,128)(2,1)} async-done(((bf16[1,256,384]{2,1,0:T(8,128)(2,1)}), bf16[1,2048,384]{2,1,0:T(8,128)(2,1)}) %all-gather.79.cloned.1.call-update) | async-done | bytes 1572880 | tf_op jit(solution)/shard_map/all_gather | solution.py:456
  97.6 42.4 %all-gather.81.cloned.1.call-done = bf16[1,2048,384]{2,1,0:T(8,128)(2,1)} async-done(((bf16[1,256,384]{2,1,0:T(8,128)(2,1)}), bf16[1,2048,384]{2,1,0:T(8,128)(2,1)}) %all-gather.81.cloned.1.call-update) | async-done | bytes 1572880 | tf_op jit(solution)/shard_map/all_gather | solution.py:457
  145.0 13.5 all-gather.51.cloned.1.call-done
  168.9 46.0 %all-gather.83.cloned.1.call-done = bf16[1,2048,384]{2,1,0:T(8,128)(2,1)} async-done(((bf16[1,256,384]{2,1,0:T(8,128)(2,1)}), bf16[1,2048,384]{2,1,0:T(8,128)(2,1)}) %all-gather.83.cloned.1.call-update) | async-done | bytes 1572880 | tf_op jit(solution)/shard_map/all_gather | solution.py:455
  299.1 14.8 all-gather.5
  314.0 17.8 reduce-scatter.54.cloned.1.call-done
  352.5 81.1 %all-gather.87.cloned.1.call-done = bf16[1,2048,1152]{2,1,0:T(8,128)(2,1)} async-done(((bf16[1,256,1152]{2,1,0:T(8,128)(2,1)}), bf16[1,2048,1152]{2,1,0:T(8,128)(2,1)}) %all-gather.87.cloned.1.call-update) | async-done | bytes 4718608 | tf_op jit(solution)/shard_map/all_gather | solution.py:460
  437.8 76.6 %all-gather.89.cloned.1.call-done = bf16[1,2048,1152]{2,1,0:T(8,128)(2,1)} async-done(((bf16[1,256,1152]{2,1,0:T(8,128)(2,1)}), bf16[1,2048,1152]{2,1,0:T(8,128)(2,1)}) %all-gather.89.cloned.1.call-update) | async-done | bytes 4718608 | tf_op jit(solution)/shard_map/all_gather | solution.py:461
  519.5 77.1 %all-gather.91.cloned.1.call-done = bf16[1,1152,2048]{2,1,0:T(8,128)(2,1)} async-done(((bf16[1,1152,256]{2,1,0:T(8,128)(2,1)}), bf16[1,1152,2048]{2,1,0:T(8,128)(2,1)}) %all-gather.91.cloned.1.call-update) | async-done | bytes 4718608 | tf_op jit(solution)/shard_map/all_gather | solution.py:462
  601.7 12.8 all-gather.53.cloned.1.call-done
  628.3 16.7 all-gather.9
  645.0 25.0 reduce-scatter.56.cloned.1.call-done
  674.3 41.5 %all-gather.93.cloned.1.call-done = bf16[1,2048,384]{2,1,0:T(8,128)(2,1)} async-done(((bf16[1,256,384]{2,1,0:T(8,128)(2,1)}), bf16[1,2048,384]{2,1,0:T(8,128)(2,1)}) %all-gather.93.cloned.1.call-update) | async-done | bytes 1572880 | tf_op jit(solution)/shard_map/all_gather | solution.py:456
  715.7 18.6 all-gather.55.cloned.1.call-done
  737.1 42.4 %all-gather.95.cloned.1.call-done = bf16[1,2048,384]{2,1,0:T(8,128)(2,1)} async-done(((bf16[1,256,384]{2,1,0:T(8,128)(2,1)}), bf16[1,2048,384]{2,1,0:T(8,128)(2,1)}) %all-gather.95.cloned.1.call-update) | async-done | bytes 1572880 | tf_op jit(solution)/shard_map/all_gather | solution.py:457
  783.8 23.3 collective-permute-done.3
  821.7 14.5 all-gather.97.cloned.1.call-done
  865.9 18.0 all-gather.99.cloned.1.call-done
  889.4 15.3 all-gather.14
  915.2 15.6 all-gather.107.cloned.1.call-done
  930.8 83.0 %all-gather.105.cloned.1.call-done = bf16[1,1152,2048]{2,1,0:T(8,128)(2,1)} async-done(((bf16[1,1152,256]{2,1,0:T(8,128)(2,1)}), bf16[1,1152,2048]{2,1,0:T(8,128)(2,1)}) %all-gather.105.cloned.1.call-update) | async-done | bytes 4718608 | tf_op jit(solution)/shard_map/all_gather | solution.py:462
  1019.1 75.2 %all-gather.103.cloned.1.call-done = bf16[1,2048,1152]{2,1,0:T(8,128)(2,1)} async-done(((bf16[1,256,1152]{2,1,0:T(8,128)(2,1)}), bf16[1,2048,1152]{2,1,0:T(8,128)(2,1)}) %all-gather.103.cloned.1.call-update) | async-done | bytes 4718608 | tf_op jit(solution)/shard_map/all_gather | solution.py:461
  1094.3 18.5 all-gather.57.cloned.1.call-done
  1118.0 76.1 %all-gather.101.cloned.1.call-done = bf16[1,2048,1152]{2,1,0:T(8,128)(2,1)} async-done(((bf16[1,256,1152]{2,1,0:T(8,128)(2,1)}), bf16[1,2048,1152]{2,1,0:T(8,128)(2,1)}) %all-gather.101.cloned.1.call-update) | async-done | bytes 4718608 | tf_op jit(solution)/shard_map/all_gather | solution.py:460
  1205.7 24.1 reduce-scatter.70.cloned.1.call-done
  1233.6 17.2 all-gather.67.cloned.1.call-done
  1279.1 17.7 collective-permute-done.12
  1312.1 14.4 collective-permute-done.14
  1334.9 13.9 reduce-scatter.100.cloned.1.call-done
  1350.9 25.9 reduce-scatter.72.cloned.1.call-done
  1379.2 20.4 reduce-scatter.102.cloned.1.call-done
  1403.3 17.4 all-gather.63.cloned.1.call-done
  1429.0 17.6 collective-permute-done.9
  1463.0 11.9 collective-permute-done.11
  1508.1 27.7 reduce-scatter.66.cloned.1.call-done
  1539.5 15.6 all-gather.109.cloned.1.call-done
  1560.3 13.7 all-gather.65.cloned.1.call-done
  1594.4 18.3 reduce-scatter.78.cloned.1.call-done
  1615.1 25.7 reduce-scatter.60.cloned.1.call-done
  1643.8 17.2 all-gather.73.cloned.1.call-done
  1688.2 17.7 collective-permute-done.18
  1721.1 14.5 collective-permute-done.20
  1759.2 26.8 reduce-scatter.80.cloned.1.call-done
  1788.5 19.8 reduce-scatter.110.cloned.1.call-done
  1811.1 25.5 reduce-scatter.68.cloned.1.call-done
  1839.1 16.7 all-gather.69.cloned.1.call-done
  1889.7 12.5 reduce-scatter.74.cloned.1.call-done
  1902.2 28.0 reduce-scatter.82.cloned.1.call-done
  1935.9 16.6 all-gather.71.cloned.1.call-done
  2026.6 13.8 collective-permute-done.21
  2053.5 16.8 collective-permute-done.17
  2122.6 14.5 reduce-scatter.104.cloned.1.call-done
  2140.7 18.6 reduce-scatter.112.cloned.1.call-done
  2189.7 25.8 reduce-scatter.84.cloned.1.call-done
  2244.2 48.8 %reduce-scatter.90.cloned.1.call-done = bf16[2,256,384]{2,1,0:T(8,128)(2,1)} async-done(((bf16[2,2048,384]{2,1,0:T(8,128)(2,1)}), bf16[2,256,384]{2,1,0:T(8,128)(2,1)}) %reduce-scatter.90.cloned.1.call-update) | async-done | bytes 393232 | tf_op jit(solution)/shard_map/reduce_scatter | solution.py:534
  2293.0 77.0 %reduce-scatter.88.cloned.1.call-done = bf16[2,256,384]{2,1,0:T(8,128)(2,1)} async-done(((bf16[2,2048,384]{2,1,0:T(8,128)(2,1)}), bf16[2,256,384]{2,1,0:T(8,128)(2,1)}) %reduce-scatter.88.cloned.1.call-update) | async-done | bytes 393232 | tf_op jit(solution)/shard_map/reduce_scatter | solution.py:531
  2436.5 61.1 %reduce-scatter.116.cloned.1.call-done = bf16[256,2]{1,0:T(8,128)(2,1)} async-done(((bf16[2048,2]{1,0:T(8,128)(2,1)}), bf16[256,2]{1,0:T(8,128)(2,1)}) %reduce-scatter.116.cloned.1.call-update) | async-done | bytes 1040
  2507.3 69.0 %reduce-scatter.92.cloned.1.call-done = bf16[2,384,256]{2,1,0:T(8,128)(2,1)} async-done(((bf16[2,384,2048]{2,1,0:T(8,128)(2,1)}), bf16[2,384,256]{2,1,0:T(8,128)(2,1)}) %reduce-scatter.92.cloned.1.call-update) | async-done | bytes 393232 | tf_op jit(solution)/shard_map/reduce_scatter | solution.py:537
  2578.2 75.3 %reduce-scatter.86.cloned.1.call-done = bf16[2,256,384]{2,1,0:T(8,128)(2,1)} async-done(((bf16[2,2048,384]{2,1,0:T(8,128)(2,1)}), bf16[2,256,384]{2,1,0:T(8,128)(2,1)}) %reduce-scatter.86.cloned.1.call-update) | async-done | bytes 393232 | tf_op jit(solution)/shard_map/reduce_scatter | solution.py:528
  2655.4 33.7 %all-reduce.4.cloned.1.call-done = (bf16[2,256,384]{2,1,0:T(8,128)(2,1)}, bf16[2,256,384]{2,1,0:T(8,128)(2,1)}) async-done(((bf16[2,256,384]{2,1,0:T(8,128)(2,1)}, bf16[2,256,384]{2,1,0:T(8,128)(2,1)}), (bf16[2,256,384]{2,1,0:T(8,128)(2,1)}, bf16[2,256,384]{2,1,0:T(8,128)(2,1)})) %all-reduce.4.cloned.1.call-update) | async-done | bytes 786448 | tf_op jit(solution)/shard_map/psum | solution.py:555
  2693.0 164.9 %reduce-scatter.98.cloned.1.call-done = bf16[2,1152,256]{2,1,0:T(8,128)(2,1)} async-done(((bf16[2,1152,2048]{2,1,0:T(8,128)(2,1)}), bf16[2,1152,256]{2,1,0:T(8,128)(2,1)}) %reduce-scatter.98.cloned.1.call-update) | async-done | bytes 1179664 | tf_op jit(solution)/shard_map/reduce_scatter | solution.py:549
  2860.8 163.1 %reduce-scatter.96.cloned.1.call-done = bf16[2,256,1152]{2,1,0:T(8,128)(2,1)} async-done(((bf16[2,2048,1152]{2,1,0:T(8,128)(2,1)}), bf16[2,256,1152]{2,1,0:T(8,128)(2,1)}) %reduce-scatter.96.cloned.1.call-update) | async-done | bytes 1179664 | tf_op jit(solution)/shard_map/reduce_scatter | solution.py:546
  3026.8 163.2 %reduce-scatter.94.cloned.1.call-done = bf16[2,256,1152]{2,1,0:T(8,128)(2,1)} async-done(((bf16[2,2048,1152]{2,1,0:T(8,128)(2,1)}), bf16[2,256,1152]{2,1,0:T(8,128)(2,1)}) %reduce-scatter.94.cloned.1.call-update) | async-done | bytes 1179664 | tf_op jit(solution)/shard_map/reduce_scatter | solution.py:543
  (1062 shorter events, 828.8 us)
Async XLA Ops:
  29.9 64.3 %all-gather.79.cloned.1.call-start = ((), (), s32[]{:S(2)}) async-start(), calls=%async_computation.70 | async-start | bytes 1769472 | tf_op jit(solution)/shard_map/all_gather | solution.py:456
  30.8 109.2 %all-gather.81.cloned.1.call-start = ((), (), s32[]{:S(2)}) async-start(), calls=%async_computation.71 | async-start | bytes 1769472 | tf_op jit(solution)/shard_map/all_gather | solution.py:457
  31.6 126.9 %all-gather.51.cloned.1.call-start = ((), (), s32[]{:S(2)}) async-start(), calls=%async_computation.33 | async-start | bytes 1310720 | tf_op jit(solution)/shard_map/all_gather | solution.py:83
  32.2 182.7 %all-gather.83.cloned.1.call-start = ((), (), s32[]{:S(2)}) async-start(), calls=%async_computation.72 | async-start | bytes 1769472 | tf_op jit(solution)/shard_map/all_gather | solution.py:455
  33.1 241.1 %all-gather.85.cloned.1.call-start = ((), (), s32[]{:S(2)}) async-start(), calls=%async_computation.73 | async-start | bytes 1769472 | tf_op jit(solution)/shard_map/all_gather | solution.py:458
  33.9 280.1 %reduce-scatter.62.cloned.1.call-start = ((), (), s32[]{:S(2)}) async-start(), calls=%async_computation.42 | async-start | bytes 1310720 | tf_op jit(solution)/shard_map/reduce_scatter | solution.py:87
  164.8 61.0 %collective-permute-start = (bf16[2,256,384]{2,1,0:T(8,128)(2,1)}, bf16[2,256,384]{2,1,0:T(8,128)(2,1)}, u32[]{:S(2)}, u32[]{:S(2)}) collective-permute-start(bf16[2,256,384]{2,1,0:T(8,128)(2,1)} %pad_maximum_fusion.23), channel_id=1, source_target_pairs={{0,16},{16,0},{4,20},{20,4},{8,24},{24,8},{12,28},{28,12},{1,17},{... | collective-permute-start | bytes 1179656 | tf_op jit(solution)/shard_map/ppermute | solution.py:30
  167.7 54.8 %collective-permute-start.7 = (bf16[2,256,384]{2,1,0:T(8,128)(2,1)}, bf16[2,256,384]{2,1,0:T(8,128)(2,1)}, u32[]{:S(2)}, u32[]{:S(2)}) collective-permute-start(bf16[2,256,384]{2,1,0:T(8,128)(2,1)} %broadcast_select_fusion.25), channel_id=1, source_target_pairs={{0,4},{4,0},{8,12},{12,8},{16,20},{20,16},{24,28},{28,24},{1,5},{5... | collective-permute-start | bytes 1179656 | tf_op jit(solution)/shard_map/ppermute | solution.py:30
  277.3 54.5 %reduce-scatter.54.cloned.1.call-start = ((), (), s32[]{:S(2)}) async-start(), calls=%async_computation.34 | async-start | bytes 1310720 | tf_op jit(solution)/shard_map/reduce_scatter | solution.py:87
  298.5 54.0 %all-gather.61.cloned.1.call-start = ((), (), s32[]{:S(2)}) async-start(), calls=%async_computation.43 | async-start | bytes 1310720 | tf_op jit(solution)/shard_map/all_gather | solution.py:83
  335.2 98.4 %all-gather.87.cloned.1.call-start = ((), (), s32[]{:S(2)}) async-start(), calls=%async_computation.74 | async-start | bytes 5308416 | tf_op jit(solution)/shard_map/all_gather | solution.py:460
  336.4 178.0 %all-gather.89.cloned.1.call-start = ((), (), s32[]{:S(2)}) async-start(), calls=%async_computation.75 | async-start | bytes 5308416 | tf_op jit(solution)/shard_map/all_gather | solution.py:461
  338.9 257.7 %all-gather.91.cloned.1.call-start = ((), (), s32[]{:S(2)}) async-start(), calls=%async_computation.76 | async-start | bytes 5308416 | tf_op jit(solution)/shard_map/all_gather | solution.py:462
  340.1 274.5 %all-gather.53.cloned.1.call-start = ((), (), s32[]{:S(2)}) async-start(), calls=%async_computation.35 | async-start | bytes 1310720 | tf_op jit(solution)/shard_map/all_gather | solution.py:83
  340.8 304.2 %reduce-scatter.64.cloned.1.call-start = ((), (), s32[]{:S(2)}) async-start(), calls=%async_computation.44 | async-start | bytes 1310720 | tf_op jit(solution)/shard_map/reduce_scatter | solution.py:87
  601.6 68.4 %reduce-scatter.56.cloned.1.call-start = ((), (), s32[]{:S(2)}) async-start(), calls=%async_computation.36 | async-start | bytes 1310720 | tf_op jit(solution)/shard_map/reduce_scatter | solution.py:87
  627.6 88.1 %all-gather.93.cloned.1.call-start = ((), (), s32[]{:S(2)}) async-start(), calls=%async_computation.77 | async-start | bytes 1769472 | tf_op jit(solution)/shard_map/all_gather | solution.py:456
  628.2 106.1 %all-gather.55.cloned.1.call-start = ((), (), s32[]{:S(2)}) async-start(), calls=%async_computation.37 | async-start | bytes 1310720 | tf_op jit(solution)/shard_map/all_gather | solution.py:83
  672.9 106.6 %all-gather.95.cloned.1.call-start = ((), (), s32[]{:S(2)}) async-start(), calls=%async_computation.78 | async-start | bytes 1769472 | tf_op jit(solution)/shard_map/all_gather | solution.py:457
  673.5 162.8 %all-gather.97.cloned.1.call-start = ((), (), s32[]{:S(2)}) async-start(), calls=%async_computation.79 | async-start | bytes 1769472 | tf_op jit(solution)/shard_map/all_gather | solution.py:455
  674.2 209.6 %all-gather.99.cloned.1.call-start = ((), (), s32[]{:S(2)}) async-start(), calls=%async_computation.80 | async-start | bytes 1769472 | tf_op jit(solution)/shard_map/all_gather | solution.py:458
  821.1 90.3 %reduce-scatter.58.cloned.1.call-start = ((), (), s32[]{:S(2)}) async-start(), calls=%async_computation.38 | async-start | bytes 1310720 | tf_op jit(solution)/shard_map/reduce_scatter | solution.py:87
  887.1 43.8 %all-gather.107.cloned.1.call-start = ((), (), s32[]{:S(2)}) async-start(), calls=%async_computation.84 | async-start | bytes 1310720 | tf_op jit(solution)/shard_map/all_gather | solution.py:93
  888.0 125.9 %all-gather.105.cloned.1.call-start = ((), (), s32[]{:S(2)}) async-start(), calls=%async_computation.83 | async-start | bytes 5308416 | tf_op jit(solution)/shard_map/all_gather | solution.py:462
  888.7 205.5 %all-gather.103.cloned.1.call-start = ((), (), s32[]{:S(2)}) async-start(), calls=%async_computation.82 | async-start | bytes 5308416 | tf_op jit(solution)/shard_map/all_gather | solution.py:461
  889.3 223.5 %all-gather.57.cloned.1.call-start = ((), (), s32[]{:S(2)}) async-start(), calls=%async_computation.39 | async-start | bytes 1310720 | tf_op jit(solution)/shard_map/all_gather | solution.py:83
  914.4 279.7 %all-gather.101.cloned.1.call-start = ((), (), s32[]{:S(2)}) async-start(), calls=%async_computation.81 | async-start | bytes 5308416 | tf_op jit(solution)/shard_map/all_gather | solution.py:460
  915.0 314.8 %reduce-scatter.70.cloned.1.call-start = ((), (), s32[]{:S(2)}) async-start(), calls=%async_computation.49 | async-start | bytes 1310720 | tf_op jit(solution)/shard_map/reduce_scatter | solution.py:326
  1205.7 45.2 %all-gather.67.cloned.1.call-start = ((), (), s32[]{:S(2)}) async-start(), calls=%async_computation.50 | async-start | bytes 1310720 | tf_op jit(solution)/shard_map/all_gather | solution.py:93
  1233.6 115.2 %reduce-scatter.100.cloned.1.call-start = ((), (), s32[]{:S(2)}) async-start(), calls=%async_computation.86 | async-start | bytes 245760 | tf_op jit(solution)/shard_map/reduce_scatter | solution.py:367
  1328.3 48.5 %reduce-scatter.72.cloned.1.call-start = ((), (), s32[]{:S(2)}) async-start(), calls=%async_computation.51 | async-start | bytes 1310720 | tf_op jit(solution)/shard_map/reduce_scatter | solution.py:361
  1331.1 68.5 %reduce-scatter.102.cloned.1.call-start = ((), (), s32[]{:S(2)}) async-start(), calls=%async_computation.87 | async-start | bytes 245760
  1334.4 86.3 %all-gather.63.cloned.1.call-start = ((), (), s32[]{:S(2)}) async-start(), calls=%async_computation.45 | async-start | bytes 1310720 | tf_op jit(solution)/shard_map/all_gather | solution.py:83
  1403.3 132.5 %reduce-scatter.66.cloned.1.call-start = ((), (), s32[]{:S(2)}) async-start(), calls=%async_computation.46 | async-start | bytes 1310720 | tf_op jit(solution)/shard_map/reduce_scatter | solution.py:87
  1507.3 47.8 %all-gather.109.cloned.1.call-start = ((), (), s32[]{:S(2)}) async-start(), calls=%async_computation.85 | async-start | bytes 1310720 | tf_op jit(solution)/shard_map/all_gather | solution.py:93
  1508.1 65.9 %all-gather.65.cloned.1.call-start = ((), (), s32[]{:S(2)}) async-start(), calls=%async_computation.47 | async-start | bytes 1310720 | tf_op jit(solution)/shard_map/all_gather | solution.py:83
  1539.3 73.4 %reduce-scatter.78.cloned.1.call-start = ((), (), s32[]{:S(2)}) async-start(), calls=%async_computation.56 | async-start | bytes 1310720 | tf_op jit(solution)/shard_map/reduce_scatter | solution.py:326
  1588.1 52.7 %reduce-scatter.60.cloned.1.call-start = ((), (), s32[]{:S(2)}) async-start(), calls=%async_computation.40 | async-start | bytes 1310720 | tf_op jit(solution)/shard_map/reduce_scatter | solution.py:87
  1593.2 67.9 %all-gather.73.cloned.1.call-start = ((), (), s32[]{:S(2)}) async-start(), calls=%async_computation.57 | async-start | bytes 1310720 | tf_op jit(solution)/shard_map/all_gather | solution.py:93
  1643.8 114.1 %reduce-scatter.108.cloned.1.call-start = ((), (), s32[]{:S(2)}) async-start(), calls=%async_computation.90 | async-start | bytes 245760 | tf_op jit(solution)/shard_map/reduce_scatter | solution.py:367
  1737.4 48.7 %reduce-scatter.80.cloned.1.call-start = ((), (), s32[]{:S(2)}) async-start(), calls=%async_computation.58 | async-start | bytes 1310720 | tf_op jit(solution)/shard_map/reduce_scatter | solution.py:361
  1741.6 66.6 %reduce-scatter.110.cloned.1.call-start = ((), (), s32[]{:S(2)}) async-start(), calls=%async_computation.91 | async-start | bytes 245760
  1742.6 94.1 %reduce-scatter.68.cloned.1.call-start = ((), (), s32[]{:S(2)}) async-start(), calls=%async_computation.48 | async-start | bytes 1310720 | tf_op jit(solution)/shard_map/reduce_scatter | solution.py:87
  1748.1 107.7 %all-gather.69.cloned.1.call-start = ((), (), s32[]{:S(2)}) async-start(), calls=%async_computation.52 | async-start | bytes 1310720 | tf_op jit(solution)/shard_map/all_gather | solution.py:93
  1748.7 126.0 %all-gather.75.cloned.1.call-start = ((), (), s32[]{:S(2)}) async-start(), calls=%async_computation.59 | async-start | bytes 1310720 | tf_op jit(solution)/shard_map/all_gather | solution.py:93
  1839.1 63.1 %reduce-scatter.74.cloned.1.call-start = ((), (), s32[]{:S(2)}) async-start(), calls=%async_computation.53 | async-start | bytes 1310720 | tf_op jit(solution)/shard_map/reduce_scatter | solution.py:326
  1868.0 62.2 %reduce-scatter.82.cloned.1.call-start = ((), (), s32[]{:S(2)}) async-start(), calls=%async_computation.60 | async-start | bytes 1310720 | tf_op jit(solution)/shard_map/reduce_scatter | solution.py:326
  1889.5 63.1 %all-gather.71.cloned.1.call-start = ((), (), s32[]{:S(2)}) async-start(), calls=%async_computation.54 | async-start | bytes 1310720 | tf_op jit(solution)/shard_map/all_gather | solution.py:93
  1935.9 167.3 %reduce-scatter.106.cloned.1.call-start = ((), (), s32[]{:S(2)}) async-start(), calls=%async_computation.89 | async-start | bytes 245760
  2073.0 41.9 %reduce-scatter.114.cloned.1.call-start = ((), (), s32[]{:S(2)}) async-start(), calls=%async_computation.93 | async-start | bytes 245760
  2081.6 55.5 %reduce-scatter.104.cloned.1.call-start = ((), (), s32[]{:S(2)}) async-start(), calls=%async_computation.88 | async-start | bytes 245760 | tf_op jit(solution)/shard_map/reduce_scatter | solution.py:367
  2082.5 76.8 %reduce-scatter.112.cloned.1.call-start = ((), (), s32[]{:S(2)}) async-start(), calls=%async_computation.92 | async-start | bytes 245760 | tf_op jit(solution)/shard_map/reduce_scatter | solution.py:367
  2087.1 100.3 %reduce-scatter.76.cloned.1.call-start = ((), (), s32[]{:S(2)}) async-start(), calls=%async_computation.55 | async-start | bytes 1310720 | tf_op jit(solution)/shard_map/reduce_scatter | solution.py:361
  2089.4 126.2 %reduce-scatter.84.cloned.1.call-start = ((), (), s32[]{:S(2)}) async-start(), calls=%async_computation.62 | async-start | bytes 1310720 | tf_op jit(solution)/shard_map/reduce_scatter | solution.py:361
  2095.4 197.5 %reduce-scatter.90.cloned.1.call-start = ((), (), s32[]{:S(2)}) async-start(), calls=%async_computation.65 | async-start | bytes 3538944 | tf_op jit(solution)/shard_map/reduce_scatter | solution.py:534
  2120.2 249.7 %reduce-scatter.88.cloned.1.call-start = ((), (), s32[]{:S(2)}) async-start(), calls=%async_computation.64 | async-start | bytes 3538944 | tf_op jit(solution)/shard_map/reduce_scatter | solution.py:531
  2166.7 266.5 %reduce-scatter.118.cloned.1.call-start = ((), (), s32[]{:S(2)}) async-start(), calls=%async_computation.95 | async-start | bytes 589824
  2172.7 324.9 %reduce-scatter.116.cloned.1.call-start = ((), (), s32[]{:S(2)}) async-start(), calls=%async_computation.94 | async-start | bytes 589824
  2221.3 355.0 %reduce-scatter.92.cloned.1.call-start = ((), (), s32[]{:S(2)}) async-start(), calls=%async_computation.66 | async-start | bytes 3538944 | tf_op jit(solution)/shard_map/reduce_scatter | solution.py:537
  2225.2 428.3 %reduce-scatter.86.cloned.1.call-start = ((), (), s32[]{:S(2)}) async-start(), calls=%async_computation.63 | async-start | bytes 3538944 | tf_op jit(solution)/shard_map/reduce_scatter | solution.py:528
  2232.5 456.7 %all-reduce.4.cloned.1.call-start = ((), (), s32[]{:S(2)}) async-start(), calls=%async_computation.96 | async-start | bytes 1572864 | tf_op jit(solution)/shard_map/psum | solution.py:555
  2369.9 488.0 %reduce-scatter.98.cloned.1.call-start = ((), (), s32[]{:S(2)}) async-start(), calls=%async_computation.69 | async-start | bytes 10616832 | tf_op jit(solution)/shard_map/reduce_scatter | solution.py:549
  2378.3 645.7 %reduce-scatter.96.cloned.1.call-start = ((), (), s32[]{:S(2)}) async-start(), calls=%async_computation.68 | async-start | bytes 10616832 | tf_op jit(solution)/shard_map/reduce_scatter | solution.py:546
  2400.4 789.6 %reduce-scatter.94.cloned.1.call-start = ((), (), s32[]{:S(2)}) async-start(), calls=%async_computation.67 | async-start | bytes 10616832 | tf_op jit(solution)/shard_map/reduce_scatter | solution.py:543
  (272 other events, 8193.3 us)
Sparse Core Ops, SparseCore 0:
  30.0 18.1 all-gather.58
  51.0 43.1 all-gather.78
  96.9 42.9 all-gather.80
  141.9 16.5 all-gather.50
  161.1 53.7 all-gather.82
  217.4 56.7 all-gather.84
  277.4 26.1 reduce-scatter.61
  306.8 24.8 reduce-scatter.53
  335.3 17.1 all-gather.60
  355.1 78.4 all-gather.86
  436.4 78.0 all-gather.88
  516.9 79.6 all-gather.90
  598.7 15.7 all-gather.52
  617.5 24.4 reduce-scatter.63
  645.1 24.8 reduce-scatter.55
  672.1 43.5 all-gather.92
  717.7 16.5 all-gather.54
  736.3 43.1 all-gather.94
  781.7 54.5 all-gather.96
  838.2 45.5 all-gather.98
  887.2 24.2 reduce-scatter.57
  913.7 17.1 all-gather.106
  933.7 80.1 all-gather.104
  1016.7 77.5 all-gather.102
  1096.5 16.2 all-gather.56
  1115.6 78.4 all-gather.100
  1205.8 23.9 reduce-scatter.69
  1233.7 17.1 all-gather.66
  1328.4 20.3 reduce-scatter.99
  1351.8 24.9 reduce-scatter.71
  1380.0 19.5 reduce-scatter.101
  1403.4 17.2 all-gather.62
  1507.4 28.2 reduce-scatter.65
  1537.9 17.1 all-gather.108
  1557.2 16.7 all-gather.64
  1588.2 24.4 reduce-scatter.77
  1615.8 24.8 reduce-scatter.59
  1643.9 17.1 all-gather.72
  1737.5 20.3 reduce-scatter.107
  1761.0 25.0 reduce-scatter.79
  1788.7 19.5 reduce-scatter.109
  1811.5 25.0 reduce-scatter.67
  1838.6 17.1 all-gather.68
  1857.9 16.7 all-gather.74
  1877.6 24.4 reduce-scatter.73
  1905.3 24.8 reduce-scatter.81
  1935.4 17.1 all-gather.70
  1954.5 16.7 all-gather.76
  2073.2 19.5 reduce-scatter.105
  2095.2 19.7 reduce-scatter.113
  2117.3 19.7 reduce-scatter.103
  2139.5 19.7 reduce-scatter.111
  2162.2 25.0 reduce-scatter.75
  2190.6 24.8 reduce-scatter.83
  2219.1 73.7 reduce-scatter.89
  2296.5 73.3 reduce-scatter.87
  2373.3 59.8 reduce-scatter.117
  2436.7 60.9 reduce-scatter.115
  2501.1 75.1 reduce-scatter.91
  2579.9 73.5 reduce-scatter.85
  2655.9 33.2 all-reduce.3
  2692.8 165.1 reduce-scatter.97
  2861.4 162.5 reduce-scatter.95
  3027.4 162.5 reduce-scatter.93
where the time goes:
time: 3210 us; the launch traced here: 3200 us
  waiting for transfers between devices  2460 us (77%)
  matrix products  324 us (10%)
  other arithmetic  167 us (5%)
  local copies, waits for them, and re-layouts  119 us (4%)
  blocking collectives  72.2 us (2%)
  starting transfers between devices  40.7 us (1%)
    ppermute x24, waiting for transfers between devices, partner(): return lax.ppermute(block, axis, route)  221 us
    reduce_scatter x1, waiting for transfers between devices, per_device(): lax.psum_scatter(stacked[8].astype(jnp.bfloat16), 'dp', scatter_dimension...  165 us
    reduce_scatter x1, waiting for transfers between devices, per_device(): lax.psum_scatter(stacked[6].astype(jnp.bfloat16), 'dp', scatter_dimension...  163 us
    reduce_scatter x1, waiting for transfers between devices, per_device(): lax.psum_scatter(stacked[7].astype(jnp.bfloat16), 'dp', scatter_dimension...  163 us
    all_gather x2, waiting for transfers between devices, per_device(): lax.all_gather(down_weight[layer_idx], 'dp', axis=1, tiled=True)  160 us
    all_gather x2, waiting for transfers between devices, per_device(): lax.all_gather(gate_weight[layer_idx], 'dp', axis=0, tiled=True)  157 us
    all_gather x2, waiting for transfers between devices, per_device(): lax.all_gather(up_weight[layer_idx], 'dp', axis=0, tiled=True)  152 us
    reduce_scatter x8, waiting for transfers between devices, scatter_rows(): lax.psum_scatter(partial_rows.astype(jnp.bfloat16), 'tensor', scatter_dim...  129 us
  transfers between devices with their start and end apart: 88, of which 81 were waited for; matrix products, arithmetic and copies ran while one was open for 13% of the time, Pallas kernels for 0%

commit v1 on v0

v1 whole, which is shorter than its diff:
```python
import math

import jax
import jax.numpy as jnp
from jax import lax
from jax.sharding import PartitionSpec as P

QUERY_HEADS = 24
KEY_VALUE_HEADS = 6
HEAD_SIZE = 64
PROMPT = 1024
CONT = 128
NCONT = 8
SLOTS = 8
PROMPT_SLOTS = 4

norm_eps = 1e-06
rope_base = 10000.0
masked_score = -1000000000.0
low = jnp.bfloat16
full = jnp.float32


def after(value, *needed):
    return lax.optimization_barrier((value, *needed))[0]


def ring_order(count):
    return [*range(0, count, 2), *range(count - 1, 0, -2)]


def ring_routes(count):
    order = ring_order(count)
    forward = [(order[i], order[(i + 1) % count]) for i in range(count)]
    return forward, [(there, here) for here, there in forward]


def ring_gather(block):
    count = lax.axis_size("dp")
    forward, backward = ring_routes(count)
    ahead, behind = [block], [block]
    for _ in range(1, count // 2):
        ahead.append(lax.ppermute(ahead[-1], "dp", forward))
        behind.append(lax.ppermute(behind[-1], "dp", backward))
    half = block.shape[0] // 2
    far = jnp.concatenate(
        [
            lax.ppermute(ahead[-1][:half], "dp", forward),
            lax.ppermute(behind[-1][half:], "dp", backward),
        ],
        axis=0,
    )
    return [*ahead, far, *behind[:0:-1]]


def ring_scatter(chunk):
    count = lax.axis_size("dp")
    forward, backward = ring_routes(count)
    middle = count // 2
    far = chunk(middle).astype(low)
    half = far.shape[0] // 2

    def joined(k, arrived, lower):
        own = chunk(k)
        if arrived.shape[0] == own.shape[0]:
            return own + arrived.astype(full)
        whole = jnp.zeros_like(own[half:], low)
        parts = [arrived, whole] if lower else [whole, arrived]
        return own + jnp.concatenate(parts, axis=0).astype(full)

    back = lax.ppermute(far[:half], "dp", backward)
    ahead = lax.ppermute(far[half:], "dp", forward)
    for step in range(1, middle):
        back = lax.ppermute(joined(middle - step, back, True).astype(low), "dp", backward)
        ahead = lax.ppermute(joined(middle + step, ahead, False).astype(low), "dp", forward)
    if middle == 1:
        return chunk(0) + jnp.concatenate([back, ahead], axis=0).astype(full)
    return chunk(0) + back.astype(full) + ahead.astype(full)


def ring_sources():
    count = lax.axis_size("dp")
    order = jnp.array(ring_order(count), jnp.int32)
    place = jnp.array([ring_order(count).index(i) for i in range(count)], jnp.int32)
    own = jnp.sum(jnp.where(jnp.arange(count) == lax.axis_index("dp"), place, 0))
    steps = jnp.arange(count, dtype=jnp.int32)

    def pick(table, index):
        return jnp.sum(jnp.where(steps[None, :] == index[:, None], table[None, :], 0), axis=1)

    return pick(order, (own - steps) % count), (own - place) % count


def reorder(array, sources):
    count = sources.shape[0]
    width = array.shape[-1] // count
    return jnp.concatenate(
        [
            lax.dynamic_slice_in_dim(array, sources[k] * width, width, axis=array.ndim - 1)
            for k in range(count)
        ],
        axis=-1,
    )


def swap(block, distance):
    count = lax.axis_size("tensor")
    return lax.ppermute(block, "tensor", [(i, i ^ distance) for i in range(count)])


def tensor_gather(block):
    across = swap(block, 2)
    beside = swap(block, 1)
    return jnp.stack([block, beside, across, swap(across, 1)], axis=1)


def tensor_scatter(parts):
    arrived = swap(jnp.stack([parts[:, 1], parts[:, 3]]), 1)
    passing = parts[:, 2].astype(full) + arrived[1].astype(full)
    kept = parts[:, 0].astype(full) + arrived[0].astype(full)
    return kept + swap(passing.astype(low), 2).astype(full)


def partner(block, bit):
    count = lax.axis_size("dp")
    return lax.ppermute(block, "dp", [(i, i ^ 1 << bit) for i in range(count)])


def share_prompt(rows, slot):
    held = jnp.where(slot >= 4, partner(rows, 2), rows)
    for bit in (0, 1):
        arrived = partner(held, bit)
        lower = slot // 2**bit % 2 == 0
        held = jnp.concatenate(
            [jnp.where(lower, held, arrived), jnp.where(lower, arrived, held)], axis=1
        )
    return held


def return_prompt(grads, slot):
    held = grads
    for bit in (1, 0):
        half = held.shape[1] // 2
        lower = slot // 2**bit % 2 == 0
        kept = jnp.where(lower, held[:, :half], held[:, half:])
        sent = jnp.where(lower, held[:, half:], held[:, :half])
        held = kept + partner(sent.astype(low), bit).astype(full)
    arrived = partner(held.astype(low), 2).astype(full)
    return jnp.where(slot < 4, held + arrived, 0.0)


def dot(left, right):
    return jnp.dot(left, right, preferred_element_type=full)


def dot_left_t(left, right):
    return lax.dot_general(left, right, (((0,), (0,)), ((), ())), preferred_element_type=full)


def dot_right_t(left, right):
    return lax.dot_general(left, right, (((1,), (1,)), ((), ())), preferred_element_type=full)


def rms_forward(hidden, gain):
    inv_root = lax.rsqrt(jnp.mean(hidden * hidden, axis=-1, keepdims=True) + norm_eps)
    scaled = hidden * inv_root
    return (scaled * gain).astype(low), scaled, inv_root


def rms_backward(grad_normed, scaled, inv_root, gain):
    grad_gain = jnp.sum(grad_normed * scaled, axis=(0, 1))
    grad_scaled = grad_normed * gain
    centred = grad_scaled - scaled * jnp.mean(grad_scaled * scaled, axis=-1, keepdims=True)
    return inv_root * centred, grad_gain


def rotate(values, cosine, sine, direction):
    half = HEAD_SIZE // 2
    first, second = values[..., :half], values[..., half:]
    return jnp.concatenate(
        [
            first * cosine - direction * second * sine,
            second * cosine + direction * first * sine,
        ],
        axis=-1,
    )


def row_setup(branch_rows, slot, tensor_index, row_block):
    rows = row_block * lax.axis_size("tensor")
    at = jnp.arange(rows, dtype=jnp.int32)
    local = (tensor_index ^ (at // row_block)) * row_block + at % row_block
    is_prompt = slot < PROMPT_SLOTS
    offset = jnp.maximum((slot - PROMPT_SLOTS) * rows, 0) + local
    cont_index = offset // CONT
    matches = cont_index[:, None] == jnp.arange(NCONT, dtype=jnp.int32)[None, :]
    start = jnp.sum(jnp.where(matches[None], branch_rows[:, None, :], 0), axis=2)
    positions = jnp.where(is_prompt, slot * rows + local, start + offset % CONT)
    limits = jnp.where(is_prompt, slot * rows, start)
    seq_ids = jnp.where(is_prompt, slot, PROMPT_SLOTS + cont_index)
    prompt_at = jnp.arange(PROMPT, dtype=jnp.int32)
    prompt_at = prompt_at // rows * rows + jnp.tile(local, PROMPT // rows)
    early = prompt_at[None, None, :] < limits[:, :, None]
    same = (seq_ids[None, :] == seq_ids[:, None]) & (local[None, :] <= local[:, None])
    allowed = jnp.concatenate([early, jnp.broadcast_to(same[None], (*limits.shape, rows))], axis=2)
    half = HEAD_SIZE // 2
    inv_freq = rope_base ** (-(2.0 * jnp.arange(half, dtype=full)) / HEAD_SIZE)
    angles = positions.astype(full)[..., None] * inv_freq
    return jnp.cos(angles)[:, :, None, :], jnp.sin(angles)[:, :, None, :], allowed


def by_pair(kv, odd):
    first, last = kv[..., :HEAD_SIZE], kv[..., HEAD_SIZE:]
    return jnp.stack([first, jnp.where(odd, last, first), last], axis=2)


def from_pairs(grads, odd):
    first, mid, last = grads[:, :, 0], grads[:, :, 1], grads[:, :, 2]
    return jnp.concatenate(
        [first + jnp.where(odd, 0.0, mid), last + jnp.where(odd, mid, 0.0)], axis=-1
    )


def pair_scores(query_rot, keys, allowed):
    scores = jnp.einsum("mqghd,mkgd->mghqk", query_rot, keys, preferred_element_type=full)
    return jnp.where(allowed[:, None, None], scores / math.sqrt(HEAD_SIZE), masked_score)


def attend_forward(query_rot, keys, values, allowed):
    scores = pair_scores(query_rot, keys, allowed)
    row_max = jnp.max(scores, axis=-1, keepdims=True)
    log_total = row_max + jnp.log(jnp.sum(jnp.exp(scores - row_max), axis=-1, keepdims=True))
    probs = jnp.exp(scores - log_total).astype(low)
    attended = jnp.einsum("mghqk,mkgd->mqghd", probs, values, preferred_element_type=full)
    return attended.astype(low), log_total


def attend_backward(grad_attended, query_rot, keys, values, allowed, log_total):
    probs = jnp.exp(pair_scores(query_rot, keys, allowed) - log_total)
    grad_probs = jnp.einsum("mqghd,mkgd->mghqk", grad_attended, values, preferred_element_type=full)
    grad_values = jnp.einsum(
        "mghqk,mqghd->mkgd", probs.astype(low), grad_attended, preferred_element_type=full
    )
    grad_scores = probs * (grad_probs - jnp.sum(probs * grad_probs, axis=-1, keepdims=True))
    grad_scores = grad_scores.astype(low)
    scale = 1.0 / math.sqrt(HEAD_SIZE)
    grad_query = jnp.einsum("mghqk,mkgd->mqghd", grad_scores, keys, preferred_element_type=full)
    grad_keys = jnp.einsum("mghqk,mqghd->mkgd", grad_scores, query_rot, preferred_element_type=full)
    return grad_query * scale, grad_keys * scale, grad_values


def per_device(
    hidden_in,
    attn_gain,
    query_weight,
    key_matrix,
    value_matrix,
    out_weight,
    ffn_gain,
    gate_weight,
    up_weight,
    down_weight,
    branch_at,
    cotangent,
):
    tensor_count = lax.axis_size("tensor")
    rank = lax.axis_index("dp")
    tensor_index = lax.axis_index("tensor")
    slot = rank % SLOTS
    micro, row_block, width = hidden_in.shape
    rows = row_block * tensor_count
    layers = attn_gain.shape[0]
    q_width = query_weight.shape[2]
    heads = q_width // HEAD_SIZE
    units = gate_weight.shape[2]
    share = QUERY_HEADS // KEY_VALUE_HEADS
    kv_width = 2 * HEAD_SIZE
    kv_first = tensor_index * heads // share
    odd = tensor_index % 2 == 1
    qkv_width = q_width + 2 * kv_width
    dim_block = query_weight.shape[1]

    sources, places = ring_sources()
    branch_rows = lax.dynamic_index_in_dim(branch_at, rank // SLOTS, 1, keepdims=False)
    cosine, sine, allowed = row_setup(branch_rows, slot, tensor_index, row_block)

    kv_weight = lax.dynamic_slice_in_dim(
        jnp.stack([key_matrix, value_matrix], axis=2).reshape(
            layers, dim_block, 2, KEY_VALUE_HEADS * HEAD_SIZE
        ),
        kv_first * HEAD_SIZE,
        kv_width,
        axis=3,
    ).reshape(layers, dim_block, 2 * kv_width)
    gain_row = jnp.concatenate([attn_gain, ffn_gain], axis=0).reshape(1, -1)
    pack_width = qkv_width + q_width
    gain_rows = 16 * (-(-gain_row.shape[1] // pack_width))
    gain_row = jnp.pad(gain_row, ((0, 0), (0, -gain_row.shape[1] % pack_width)))
    gain_row = gain_row.reshape(-1, pack_width)
    gain_pad = jnp.pad(gain_row, ((0, gain_rows - gain_row.shape[0]), (0, 0)))
    packs = []
    token = None
    for layer in range(layers):
        attn_pack = jnp.concatenate(
            [query_weight[layer], kv_weight[layer], out_weight[layer].T], axis=1
        )
        if layer == 0:
            attn_pack = jnp.concatenate([attn_pack, gain_pad], axis=0)
        gate_up = jnp.concatenate([gate_weight[layer], up_weight[layer]], axis=1)
        gathered = []
        for block in (attn_pack, gate_up, down_weight[layer].T):
            if token is not None:
                block = after(block, token)
            blocks = ring_gather(block)
            token = blocks[len(blocks) // 2 - 1]
            gathered.append(blocks)
        packs.append(gathered)
    gains = jnp.stack(
        [
            block[dim_block : dim_block + gain_row.shape[0]].reshape(-1)[: 2 * layers * dim_block]
            for block in packs[0][0]
        ]
    ).reshape(-1, 2, layers, dim_block)
    gains = gains.transpose(1, 2, 0, 3).reshape(2, layers, width).astype(full)
    weights = []
    for attn_blocks, gate_up_blocks, down_blocks in packs:
        attn_all = jnp.concatenate([block[:dim_block] for block in attn_blocks], axis=0)
        weights.append(
            (
                attn_all[:, :qkv_width],
                attn_all[:, qkv_width:],
                jnp.concatenate(gate_up_blocks, axis=0),
                jnp.concatenate(down_blocks, axis=0),
            )
        )

    def gather_rows(block):
        return tensor_gather(block).reshape(-1, width)

    def scatter_rows(parts):
        return tensor_scatter(parts.astype(low).reshape(micro, tensor_count, row_block, width))

    hidden = reorder(hidden_in, sources).astype(full)
    saved = []
    for layer in range(layers):
        qkv_weight, out_t, gate_up_weight, down_t = weights[layer]
        normed, scaled, inv_root = rms_forward(hidden, gains[0, layer])
        normed_all = gather_rows(normed)
        qkv = dot(normed_all, qkv_weight).reshape(micro, rows, -1, HEAD_SIZE)
        query_rot = rotate(qkv[:, :, :heads], cosine, sine, 1.0).astype(low)
        query_rot = query_rot.reshape(micro, rows, 3, heads // 3, HEAD_SIZE)
        key_rot = rotate(qkv[:, :, heads : heads + 2], cosine, sine, 1.0).astype(low)
        local_kv = jnp.concatenate([key_rot, qkv[:, :, heads + 2 :].astype(low)], axis=2)
        local_kv = local_kv.reshape(micro, rows, 2 * kv_width)
        all_kv = jnp.concatenate([share_prompt(local_kv, slot), local_kv], axis=1)
        keys = by_pair(all_kv[..., :kv_width], odd)
        values = by_pair(all_kv[..., kv_width:], odd)
        attended, log_total = attend_forward(query_rot, keys, values, allowed)
        attended = attended.reshape(-1, q_width)
        middle = hidden + scatter_rows(dot_right_t(attended, out_t))
        normed_ffn, scaled_ffn, inv_root_ffn = rms_forward(middle, gains[1, layer])
        normed_ffn_all = gather_rows(normed_ffn)
        gate_up = dot(normed_ffn_all, gate_up_weight)
        gate, up = gate_up[:, :units], gate_up[:, units:]
        active = (jax.nn.silu(gate) * up).astype(low)
        hidden = middle + scatter_rows(dot_right_t(active, down_t))
        saved.append(
            (
                (normed_all, scaled, inv_root, query_rot, keys, values, log_total, attended),
                (normed_ffn_all, scaled_ffn, inv_root_ffn, gate, up, active),
            )
        )
    layer_out = reorder(hidden, places)

    grad_out = reorder(cotangent, sources).astype(full)
    gain_grads = [[None] * layers, [None] * layers]
    reduced = [None] * layers

    def column_chunks(left, right):
        def chunk(k):
            return dot_left_t(left[:, k * dim_block : (k + 1) * dim_block], right)

        return chunk

    for layer in reversed(range(layers)):
        qkv_weight, out_t, gate_up_weight, down_t = weights[layer]
        attn_saved, ffn_saved = saved[layer]
        normed_all, scaled, inv_root, query_rot, keys, values, log_total, attended = attn_saved
        normed_ffn_all, scaled_ffn, inv_root_ffn, gate, up, active = ffn_saved
        grad_branch = gather_rows(grad_out.astype(low))
        grad_active = dot(grad_branch, down_t)
        sig = jax.nn.sigmoid(gate)
        grad_gate = (grad_active * up * sig * (1.0 + gate * (1.0 - sig))).astype(low)
        grad_up = (grad_active * gate * sig).astype(low)
        grad_gate_up = jnp.concatenate([grad_gate, grad_up], axis=1)
        grad_normed_ffn = scatter_rows(dot_right_t(grad_gate_up, gate_up_weight))
        grad_mid_norm, gain_grads[1][layer] = rms_backward(
            grad_normed_ffn, scaled_ffn, inv_root_ffn, gains[1, layer]
        )
        down_grad = ring_scatter(column_chunks(grad_branch, active))
        gate_up_grad = ring_scatter(column_chunks(normed_ffn_all, grad_gate_up))
        grad_middle = grad_out + grad_mid_norm
        grad_branch1 = gather_rows(grad_middle.astype(low))
        grad_attended = dot(grad_branch1, out_t).astype(low).reshape(query_rot.shape)
        grad_query_rot, grad_key_pairs, grad_value_pairs = attend_backward(
            grad_attended, query_rot, keys, values, allowed, log_total
        )
        grad_kv = jnp.concatenate(
            [from_pairs(grad_key_pairs, odd), from_pairs(grad_value_pairs, odd)], axis=-1
        )
        grad_kv = grad_kv[:, PROMPT:] + return_prompt(grad_kv[:, :PROMPT], slot)
        grad_heads = jnp.concatenate(
            [
                grad_query_rot.reshape(micro, rows, heads, HEAD_SIZE),
                grad_kv[..., :kv_width].reshape(micro, rows, 2, HEAD_SIZE),
            ],
            axis=2,
        )
        grad_heads = rotate(grad_heads, cosine, sine, -1.0).astype(low)
        grad_qkv = jnp.concatenate(
            [
                grad_heads.reshape(micro * rows, -1),
                grad_kv[..., kv_width:].astype(low).reshape(micro * rows, -1),
            ],
            axis=1,
        )
        grad_normed = scatter_rows(dot_right_t(grad_qkv, qkv_weight))
        grad_hidden_norm, gain_grads[0][layer] = rms_backward(
            grad_normed, scaled, inv_root, gains[0, layer]
        )
        grad_out = grad_middle + grad_hidden_norm
        of_qkv = column_chunks(normed_all, grad_qkv)
        of_out = column_chunks(grad_branch1, attended)
        if layer == 0:
            gain_all = jnp.stack([jnp.stack(gain_grads[0]), jnp.stack(gain_grads[1])])
            gain_all = gain_all.reshape(2 * layers, -1, dim_block).transpose(1, 0, 2)
            gain_all = gain_all.reshape(gain_all.shape[0], -1)
            spare = gain_row.size - gain_all.shape[1]
            gain_all = jnp.pad(gain_all, ((0, 0), (0, spare))).reshape(-1, *gain_row.shape)
            gain_all = jnp.pad(gain_all, ((0, 0), (0, gain_rows - gain_row.shape[0]), (0, 0)))

        def attn_chunk(k, of_qkv=of_qkv, of_out=of_out, layer=layer):
            part = jnp.concatenate([of_qkv(k), of_out(k)], axis=1)
            return part if layer else jnp.concatenate([part, gain_all[k]], axis=0)

        reduced[layer] = (ring_scatter(attn_chunk), gate_up_grad, down_grad)
    input_grad = reorder(grad_out, places)

    kv_grads = jnp.stack([reduced[layer][0][:dim_block, q_width:qkv_width] for layer in range(layers)])
    gain_part = reduced[0][0][dim_block : dim_block + gain_row.shape[0]].reshape(-1)
    gain_part = gain_part[: 2 * layers * dim_block].reshape(2 * layers * dim_block // 128, 128)
    shared = jnp.concatenate([kv_grads.reshape(-1, 128), gain_part], axis=0).astype(low)
    every = tensor_gather(shared[None])[0].astype(full)
    kv_every = every[:, : kv_grads.size // 128].reshape(tensor_count, layers, dim_block, 2, kv_width)
    gain_sum = jnp.sum(every[:, kv_grads.size // 128 :], axis=0).reshape(2, layers, dim_block)
    by_head = [0.0] * KEY_VALUE_HEADS
    for index in range(tensor_count):
        part = kv_every[0]
        for distance in range(1, tensor_count):
            part = jnp.where(tensor_index == index ^ distance, kv_every[distance], part)
        first = index * heads // share
        by_head[first] = by_head[first] + part[..., :HEAD_SIZE]
        by_head[first + 1] = by_head[first + 1] + part[..., HEAD_SIZE:]
    kv_full = jnp.concatenate(by_head, axis=-1)

    def stacked(pick):
        return jnp.stack([pick(reduced[layer]) for layer in range(layers)])

    return (
        layer_out,
        input_grad,
        gain_sum[0],
        stacked(lambda grads: grads[0][:dim_block, :q_width]),
        kv_full[:, :, 0],
        kv_full[:, :, 1],
        stacked(lambda grads: grads[0][:dim_block, qkv_width:].T),
        gain_sum[1],
        stacked(lambda grads: grads[1][:, :units]),
        stacked(lambda grads: grads[1][:, units:]),
        stacked(lambda grads: grads[2].T),
    )


def solution(mesh):
    rows = P(None, ("dp", "tensor"), None)
    split = P(None, "dp", "tensor")
    across = P(None, "tensor", "dp")
    whole = P(None, "dp", None)
    gain = P(None, "dp")
    return jax.shard_map(
        per_device,
        mesh=mesh,
        in_specs=(rows, gain, split, whole, whole, across, gain, split, split, across, P(), rows),
        out_specs=(rows, rows, gain, split, whole, whole, across, gain, split, split, across),
        check_vma=False,
    )
```

time: 3210 us -> 1150 us (0.36)
  waiting for transfers between devices: 2460 us -> 499 us
  starting transfers between devices: 40.7 us -> 204 us
  matrix products: 324 us -> 224 us
  other arithmetic: 167 us -> 91.2 us
  blocking collectives: 72.2 us -> 0 us
    reduce_scatter x27 -> x0, waiting for transfers between devices: 1120 us -> none  [the longest x1 165 us: per_device(): lax.psum_scatter(stacked[8].astype(jnp.bfloat16), 'dp', scatter_dimension...]
    all_gather x30 -> x0, waiting for transfers between devices: 957 us -> none  [the longest x2 160 us: per_device(): lax.all_gather(down_weight[layer_idx], 'dp', axis=1, tiled=True)]
    ppermute x24 -> x151, waiting for transfers between devices: 221 us -> 499 us  [the longest x12 133 us: partner(): return lax.ppermute(block, 'dp', [(i, i ^ 1 << bit) for i in range(count)])]
    ppermute x24 -> x151, starting transfers between devices: 35.4 us -> 204 us  [the longest x43 99.5 us: swap(): lax.ppermute(block, 'tensor', [(i, i ^ distance) for i in range(count)])]
    unnamed x70 -> x0, waiting for transfers between devices: 129 us -> none
    dot_general x60 -> x20, matrix products: 193 us -> 115 us  [the longest x8 32.3 us: dot(): return jnp.dot(left, right, preferred_element_type=full)]
    all_gather x4 -> x0, blocking collectives: 64.7 us -> none  [the longest x2 34.6 us: per_device(): lax.all_gather(attn_gain[layer_idx], 'dp', axis=0, tiled=True)]
    dot_general x28 -> x8, matrix products: 81.8 us -> 35.7 us  [dot_right_t(): lax.dot_general(left, right, (((1,), (1,)), ((), ())), preferred_element_...]
  transfers between devices with their start and end apart: 88 -> 151, of which waited for: 81 -> 55; matrix products, arithmetic and copies ran while one was open for 13% -> 29% of each run, Pallas kernels for 0% -> 0%
where the time goes in v1:
time: 1150 us; the launch traced here: 1140 us
  waiting for transfers between devices  499 us (43%)
  matrix products  224 us (19%)
  starting transfers between devices  204 us (18%)
  local copies, waits for them, and re-layouts  105 us (9%)
  other arithmetic  91.2 us (8%)
  between operations  15.8 us (1%)
    ppermute x12, waiting for transfers between devices, partner(): return lax.ppermute(block, 'dp', [(i, i ^ 1 << bit) for i in range(count)])  133 us
    ppermute x43, starting transfers between devices, swap(): lax.ppermute(block, 'tensor', [(i, i ^ distance) for i in range(count)])  99.5 us
    ppermute x18, waiting for transfers between devices, ring_scatter(): lax.ppermute(joined(middle + step, ahead, False).astype(low), 'dp', forward)  95.2 us
    dot_general x64, matrix products, dot_left_t(): lax.dot_general(left, right, (((0,), (0,)), ((), ())), preferred_element_...  73.9 us
    ppermute x18, waiting for transfers between devices, ring_gather(): ahead.append(lax.ppermute(ahead[-1], 'dp', forward))  60.1 us
    unnamed x462, local copies, waits for them, and re-layouts  51.5 us
    ppermute x43, waiting for transfers between devices, swap(): lax.ppermute(block, 'tensor', [(i, i ^ distance) for i in range(count)])  48.9 us
    ppermute x6, waiting for transfers between devices, ring_gather(): lax.ppermute(ahead[-1][:half], 'dp', forward)  45.5 us
  transfers between devices with their start and end apart: 151, of which 55 were waited for; matrix products, arithmetic and copies ran while one was open for 29% of the time, Pallas kernels for 0%

profile of v1, /device:TPU:1, one launch (start us, length us, event | category | flops | bytes accessed | tf_op | source)
XLA Modules:
  0.0 1139.2 jit_solution(2291217527061836263)
XLA Ops:
  31.4 8.5 collective-permute-done.4
  44.6 7.7 collective-permute-done.5
  91.2 10.3 collective-permute-done.11
  106.0 17.6 %collective-permute-done.12 = bf16[2,256,256]{1,2,0:T(8,128)(2,1)} collective-permute-done((bf16[2,256,256]{1,2,0:T(8,128)(2,1)S(1)}, bf16[2,256,256]{1,2,0:T(8,128)(2,1)}, u32[]{:S(2)}, u32[]{:S(2)}) %collective-permute-start.12) | collective-permute-done | bytes 262176 | tf_op jit(solution)/shard_map/ppermute | solution.py:126
  131.4 6.3 collective-permute-done.13
  139.3 6.8 fusion.349
  146.1 7.5 exponential_reduce_fusion.1
  154.3 8.0 fusion.57
  174.5 23.2 %collective-permute-done.21 = bf16[256,2304]{1,0:T(8,128)(2,1)S(1)} collective-permute-done((bf16[256,2304]{1,0:T(8,128)(2,1)S(1)}, bf16[256,2304]{1,0:T(8,128)(2,1)S(1)}, u32[]{:S(2)}, u32[]{:S(2)}) %collective-permute-start.21) | collective-permute-done | bytes 1179680 | tf_op jit(solution)/shard_map/ppermute | solution.py:43
  204.0 20.3 %collective-permute-done.22 = bf16[128,2304]{1,0:T(8,128)(2,1)S(1)} collective-permute-done((bf16[128,2304]{1,0:T(8,128)(2,1)S(1)}, bf16[128,2304]{1,0:T(8,128)(2,1)S(1)}, u32[]{:S(2)}, u32[]{:S(2)}) %collective-permute-start.22) | collective-permute-done | bytes 589856 | tf_op jit(solution)/shard_map/ppermute | solution.py:48
  227.1 8.6 collective-permute-done.17
  242.4 5.0 fusion.352
  247.5 7.0 collective-permute-done.29
  261.0 12.7 %collective-permute-done.34 = bf16[128,1152]{0,1:T(8,128)(2,1)S(1)} collective-permute-done((bf16[128,1152]{0,1:T(8,128)(2,1)S(1)}, bf16[128,1152]{0,1:T(8,128)(2,1)S(1)}, u32[]{:S(2)}, u32[]{:S(2)}) %collective-permute-start.34) | collective-permute-done | bytes 294944 | tf_op jit(solution)/shard_map/ppermute | solution.py:49
  282.5 11.9 %collective-permute-done.45 = bf16[256,1024]{0,1:T(8,128)(2,1)S(1)} collective-permute-done((bf16[256,1024]{0,1:T(8,128)(2,1)S(1)}, bf16[256,1024]{0,1:T(8,128)(2,1)S(1)}, u32[]{:S(2)}, u32[]{:S(2)}) %collective-permute-start.45) | collective-permute-done | bytes 524320 | tf_op jit(solution)/shard_map/ppermute | solution.py:44
  300.0 7.0 collective-permute-done.46
  316.6 14.5 %collective-permute-done.38 = bf16[2,64,2048]{2,1,0:T(8,128)(2,1)S(1)} collective-permute-done((bf16[2,64,2048]{2,1,0:T(8,128)(2,1)S(1)}, bf16[2,64,2048]{2,1,0:T(8,128)(2,1)S(1)}, u32[]{:S(2)}, u32[]{:S(2)}) %collective-permute-start.38) | collective-permute-done | bytes 524320 | tf_op jit(solution)/shard_map/ppermute | solution.py:108
  343.6 9.6 collective-permute-done.48
  361.5 13.7 %collective-permute-done.49 = bf16[2,256,256]{1,2,0:T(8,128)(2,1)S(1)} collective-permute-done((bf16[2,256,256]{1,2,0:T(8,128)(2,1)S(1)}, bf16[2,256,256]{1,2,0:T(8,128)(2,1)S(1)}, u32[]{:S(2)}, u32[]{:S(2)}) %collective-permute-start.49) | collective-permute-done | bytes 262176 | tf_op jit(solution)/shard_map/ppermute | solution.py:126
  379.0 8.7 collective-permute-done.50
  389.2 6.9 fusion.350
  396.1 7.5 exponential_reduce_fusion
  403.7 8.1 fusion.58
  424.8 22.0 %collective-permute-done.58 = bf16[256,2304]{1,0:T(8,128)(2,1)S(1)} collective-permute-done((bf16[256,2304]{1,0:T(8,128)(2,1)}, bf16[256,2304]{1,0:T(8,128)(2,1)S(1)}, u32[]{:S(2)}, u32[]{:S(2)}) %collective-permute-start.58) | collective-permute-done | bytes 1179680 | tf_op jit(solution)/shard_map/ppermute | solution.py:43
  453.1 20.6 %collective-permute-done.59 = bf16[128,2304]{1,0:T(8,128)(2,1)S(1)} collective-permute-done((bf16[128,2304]{1,0:T(8,128)(2,1)S(1)}, bf16[128,2304]{1,0:T(8,128)(2,1)S(1)}, u32[]{:S(2)}, u32[]{:S(2)}) %collective-permute-start.59) | collective-permute-done | bytes 589856 | tf_op jit(solution)/shard_map/ppermute | solution.py:48
  477.2 8.1 collective-permute-done.54
  494.2 7.1 collective-permute-done.66
  503.0 6.6 fusion.354
  518.7 6.9 multiply_convert_fusion.3
  525.7 6.3 convolution_convert_fusion.2
  532.5 9.1 convolution_convert_fusion.9
  544.3 5.3 collective-permute-start.77
  553.8 11.2 collective-permute-done.131
  568.2 9.5 collective-permute-done.148
  583.9 31.8 %collective-permute-done.149 = bf16[256,1152]{1,0:T(8,128)(2,1)S(1)} collective-permute-done((bf16[256,1152]{1,0:T(8,128)(2,1)S(1)}, bf16[256,1152]{1,0:T(8,128)(2,1)S(1)}, u32[]{:S(2)}, u32[]{:S(2)}) %collective-permute-start.149) | collective-permute-done | bytes 589856 | tf_op jit(solution)/shard_map/ppermute | solution.py:75
  651.8 7.1 fusion.25
  659.0 12.2 %fusion.3 = (f32[2,3,2,256]{3,2,1,0:T(2,128)S(1)}, f32[2,3,1280,256,2]{3,2,4,1,0:T(8,128)}) fusion(f32[2,3,2,256,1280]{3,4,2,1,0:T(8,128)} %get-tuple-element.227, f32[2,3,2,256]{3,2,1,0:T(2,128)S(1)} %log_add_fusion, bf16[2,256,3,2,64]{1,0,4,3,2:T(2,128)(2,1)S(1)} %copy-done.21, bf16[2,1280,1,64]{1,3,0,2:T(8,128)(2,1)S(1)} %copy-done.32, ...), kind=kOutput, calls=%fused_computation.7 | convolution fusion | flops 516092928 | bytes 32858112 | tf_op jit(solution)/shard_map/mqghd,mkgd->mghqk/dot_general | solution.py:240
  671.4 7.4 fusion.5
  683.3 5.7 fusion.22
  694.6 7.9 collective-permute-done.82
  714.8 22.7 %collective-permute-done.84 = bf16[2,256,256]{1,2,0:T(8,128)(2,1)S(1)} collective-permute-done((bf16[2,256,256]{1,2,0:T(8,128)(2,1)S(1)}, bf16[2,256,256]{1,2,0:T(8,128)(2,1)S(1)}, u32[]{:S(2)}, u32[]{:S(2)}) %collective-permute-start.84) | collective-permute-done | bytes 262176 | tf_op jit(solution)/shard_map/ppermute | solution.py:126
  748.0 7.7 collective-permute-start.108
  789.9 6.7 collective-permute-start.87
  797.9 7.8 collective-permute-start.89
  809.4 5.9 multiply_convert_fusion.1
  815.9 5.3 convolution_convert_fusion.8
  826.4 5.8 collective-permute-done.139
  834.8 10.0 collective-permute-done.123
  848.2 9.3 collective-permute-done.140
  860.4 35.0 %collective-permute-done.141 = bf16[256,1152]{1,0:T(8,128)(2,1)S(1)} collective-permute-done((bf16[256,1152]{1,0:T(8,128)(2,1)S(1)}, bf16[256,1152]{1,0:T(8,128)(2,1)S(1)}, u32[]{:S(2)}, u32[]{:S(2)}) %collective-permute-start.141) | collective-permute-done | bytes 589856 | tf_op jit(solution)/shard_map/ppermute | solution.py:75
  929.1 7.0 fusion.37
  936.2 12.0 %fusion = (f32[2,3,2,256]{3,2,1,0:T(2,128)S(1)}, f32[2,3,1280,256,2]{3,2,4,1,0:T(8,128)}) fusion(f32[2,3,2,256,1280]{3,4,2,1,0:T(8,128)} %get-tuple-element.225, f32[2,3,2,256]{3,2,1,0:T(2,128)S(1)} %copy-done.123, bf16[2,256,3,2,64]{1,0,4,3,2:T(2,128)(2,1)S(1)} %reshape.850, bf16[2,1280,1,64]{1,3,0,2:T(8,128)(2,1)S(1)} %copy-done.26, ...), kind=kOutput, calls=%fused_computation.2 | convolution fusion | flops 516092928 | bytes 32858112 | tf_op jit(solution)/shard_map/mqghd,mkgd->mghqk/dot_general | solution.py:240
  948.3 7.4 fusion.2
  960.3 5.7 fusion.34
  969.9 10.0 collective-permute-done.95
  993.0 21.8 %collective-permute-done.97 = bf16[2,256,256]{1,2,0:T(8,128)(2,1)S(1)} collective-permute-done((bf16[2,256,256]{1,2,0:T(8,128)(2,1)S(1)}, bf16[2,256,256]{1,2,0:T(8,128)(2,1)S(1)}, u32[]{:S(2)}, u32[]{:S(2)}) %collective-permute-start.97) | collective-permute-done | bytes 262176 | tf_op jit(solution)/shard_map/ppermute | solution.py:126
  1041.5 12.4 %collective-permute-done.99 = bf16[2,64,2048]{2,1,0:T(8,128)(2,1)S(1)} collective-permute-done((bf16[2,64,2048]{2,1,0:T(8,128)(2,1)S(1)}, bf16[2,64,2048]{2,1,0:T(8,128)(2,1)S(1)}, u32[]{:S(2)}, u32[]{:S(2)}) %collective-permute-start.99) | collective-permute-done | bytes 524320 | tf_op jit(solution)/shard_map/ppermute | solution.py:108
  1055.7 8.8 collective-permute-start.100
  1073.9 8.4 collective-permute-done.101
  1086.7 8.3 collective-permute-done.102
  1097.5 9.1 collective-permute-done.103
  1110.2 4.9 collective-permute-start.116
  1115.1 4.8 collective-permute-start.118
  1128.2 7.4 concatenate.384
  (1060 shorter events, 456.7 us)
Async XLA Ops:
  89.7 38.6 %collective-permute-start.23 = (bf16[256,2304]{1,0:T(8,128)(2,1)S(1)}, bf16[256,2304]{1,0:T(8,128)(2,1)}, u32[]{:S(2)}, u32[]{:S(2)}) collective-permute-start(bf16[256,2304]{1,0:T(8,128)(2,1)S(1)} %copy-done.14), channel_id=1, source_target_pairs={{8,0},{16,8},{24,16},{28,24},{20,28},{12,20},{4,12},{0,4},{9,1},{1... | collective-permute-start | bytes 3538952 | tf_op jit(solution)/shard_map/ppermute | solution.py:44
  90.9 37.8 %collective-permute-start.19 = (bf16[256,2304]{1,0:T(8,128)(2,1)S(1)}, bf16[256,2304]{1,0:T(8,128)(2,1)}, u32[]{:S(2)}, u32[]{:S(2)}) collective-permute-start(bf16[256,2304]{1,0:T(8,128)(2,1)S(1)} %copy-done.14), channel_id=1, source_target_pairs={{0,8},{8,16},{16,24},{24,28},{28,20},{20,12},{12,4},{4,0},{1,9},{9... | collective-permute-start | bytes 3538952 | tf_op jit(solution)/shard_map/ppermute | solution.py:43
  101.5 22.0 %collective-permute-start.12 = (bf16[2,256,256]{1,2,0:T(8,128)(2,1)S(1)}, bf16[2,256,256]{1,2,0:T(8,128)(2,1)}, u32[]{:S(2)}, u32[]{:S(2)}) collective-permute-start(bf16[2,256,256]{1,2,0:T(8,128)(2,1)S(1)} %broadcast_select_fusion.5), channel_id=1, source_target_pairs={{0,4},{4,0},{8,12},{12,8},{16,20},{20,16},{24,28},{28,24},{1,5},{5... | collective-permute-start | bytes 786440 | tf_op jit(solution)/shard_map/ppermute | solution.py:126
  128.3 41.9 %collective-permute-start.24 = (bf16[256,2304]{1,0:T(8,128)(2,1)}, bf16[256,2304]{1,0:T(8,128)(2,1)S(1)}, u32[]{:S(2)}, u32[]{:S(2)}) collective-permute-start(bf16[256,2304]{1,0:T(8,128)(2,1)} %collective-permute-done.23), channel_id=1, source_target_pairs={{8,0},{16,8},{24,16},{28,24},{20,28},{12,20},{4,12},{0,4},{9,1},{1... | collective-permute-start | bytes 3538952 | tf_op jit(solution)/shard_map/ppermute | solution.py:44
  128.7 41.6 %collective-permute-start.20 = (bf16[256,2304]{1,0:T(8,128)(2,1)}, bf16[256,2304]{1,0:T(8,128)(2,1)S(1)}, u32[]{:S(2)}, u32[]{:S(2)}) collective-permute-start(bf16[256,2304]{1,0:T(8,128)(2,1)} %collective-permute-done.19), channel_id=1, source_target_pairs={{0,8},{8,16},{16,24},{24,28},{28,20},{20,12},{12,4},{4,0},{1,9},{9... | collective-permute-start | bytes 3538952 | tf_op jit(solution)/shard_map/ppermute | solution.py:43
  170.2 28.9 %collective-permute-start.25 = (bf16[256,2304]{1,0:T(8,128)(2,1)S(1)}, bf16[256,2304]{1,0:T(8,128)(2,1)S(1)}, u32[]{:S(2)}, u32[]{:S(2)}) collective-permute-start(bf16[256,2304]{1,0:T(8,128)(2,1)S(1)} %collective-permute-done.24), channel_id=1, source_target_pairs={{8,0},{16,8},{24,16},{28,24},{20,28},{12,20},{4,12},{0,4},{9,1},{1... | collective-permute-start | bytes 3538952 | tf_op jit(solution)/shard_map/ppermute | solution.py:44
  170.3 27.4 %collective-permute-start.21 = (bf16[256,2304]{1,0:T(8,128)(2,1)S(1)}, bf16[256,2304]{1,0:T(8,128)(2,1)S(1)}, u32[]{:S(2)}, u32[]{:S(2)}) collective-permute-start(bf16[256,2304]{1,0:T(8,128)(2,1)S(1)} %collective-permute-done.20), channel_id=1, source_target_pairs={{0,8},{8,16},{16,24},{24,28},{28,20},{20,12},{12,4},{4,0},{1,9},{9... | collective-permute-start | bytes 3538952 | tf_op jit(solution)/shard_map/ppermute | solution.py:43
  173.4 27.7 %collective-permute-start.15 = (bf16[2,64,2048]{2,1,0:T(8,128)(2,1)S(1)}, bf16[2,64,2048]{2,1,0:T(8,128)(2,1)S(1)}, u32[]{:S(2)}, u32[]{:S(2)}) collective-permute-start(bf16[2,64,2048]{2,1,0:T(8,128)(2,1)S(1)} %fusion.99), channel_id=1, source_target_pairs={{0,2},{1,3},{2,0},{3,1},{4,6},{5,7},{6,4},{7,5},{8,10},{9,11},{10,... | collective-permute-start | bytes 1572872 | tf_op jit(solution)/shard_map/ppermute | solution.py:108
  197.7 27.7 %collective-permute-start.31 = (bf16[256,1152]{0,1:T(8,128)(2,1)S(1)}, bf16[256,1152]{0,1:T(8,128)(2,1)S(1)}, u32[]{:S(2)}, u32[]{:S(2)}) collective-permute-start(bf16[256,1152]{0,1:T(8,128)(2,1)S(1)} %copy-done.45), channel_id=1, source_target_pairs={{8,0},{16,8},{24,16},{28,24},{20,28},{12,20},{4,12},{0,4},{9,1},{1... | collective-permute-start | bytes 1769480 | tf_op jit(solution)/shard_map/ppermute | solution.py:44
  198.0 27.8 %collective-permute-start.27 = (bf16[256,1152]{0,1:T(8,128)(2,1)S(1)}, bf16[256,1152]{0,1:T(8,128)(2,1)S(1)}, u32[]{:S(2)}, u32[]{:S(2)}) collective-permute-start(bf16[256,1152]{0,1:T(8,128)(2,1)S(1)} %copy-done.45), channel_id=1, source_target_pairs={{0,8},{8,16},{16,24},{24,28},{28,20},{20,12},{12,4},{4,0},{1,9},{9... | collective-permute-start | bytes 1769480 | tf_op jit(solution)/shard_map/ppermute | solution.py:43
  199.2 27.7 %collective-permute-start.26 = (bf16[128,2304]{1,0:T(8,128)(2,1)S(1)}, bf16[128,2304]{1,0:T(8,128)(2,1)S(1)}, u32[]{:S(2)}, u32[]{:S(2)}) collective-permute-start(bf16[128,2304]{1,0:T(8,128)(2,1)S(1)} %slice.1222), channel_id=1, source_target_pairs={{8,0},{16,8},{24,16},{28,24},{20,28},{12,20},{4,12},{0,4},{9,1},{1... | collective-permute-start | bytes 1769480 | tf_op jit(solution)/shard_map/ppermute | solution.py:49
  199.6 24.8 %collective-permute-start.22 = (bf16[128,2304]{1,0:T(8,128)(2,1)S(1)}, bf16[128,2304]{1,0:T(8,128)(2,1)S(1)}, u32[]{:S(2)}, u32[]{:S(2)}) collective-permute-start(bf16[128,2304]{1,0:T(8,128)(2,1)S(1)} %slice.1221), channel_id=1, source_target_pairs={{0,8},{8,16},{16,24},{24,28},{28,20},{20,12},{12,4},{4,0},{1,9},{9... | collective-permute-start | bytes 1769480 | tf_op jit(solution)/shard_map/ppermute | solution.py:48
  201.8 40.3 %collective-permute-start.16 = (bf16[2,64,2048]{2,1,0:T(8,128)(2,1)S(1)}, bf16[2,64,2048]{2,1,0:T(8,128)(2,1)S(1)}, u32[]{:S(2)}, u32[]{:S(2)}) collective-permute-start(bf16[2,64,2048]{2,1,0:T(8,128)(2,1)S(1)} %multiply_convert_fusion.8), channel_id=1, source_target_pairs={{0,1},{1,0},{2,3},{3,2},{4,5},{5,4},{6,7},{7,6},{8,9},{9,8},{10,11... | collective-permute-start | bytes 1572872 | tf_op jit(solution)/shard_map/ppermute | solution.py:108
  256.4 24.5 %collective-permute-start.44 = (bf16[256,1024]{0,1:T(8,128)(2,1)S(1)}, bf16[256,1024]{0,1:T(8,128)(2,1)S(1)}, u32[]{:S(2)}, u32[]{:S(2)}) collective-permute-start(bf16[256,1024]{0,1:T(8,128)(2,1)S(1)} %copy-done.52), channel_id=1, source_target_pairs={{8,0},{16,8},{24,16},{28,24},{20,28},{12,20},{4,12},{0,4},{9,1},{1... | collective-permute-start | bytes 1572872 | tf_op jit(solution)/shard_map/ppermute | solution.py:44
  256.8 24.5 %collective-permute-start.40 = (bf16[256,1024]{0,1:T(8,128)(2,1)S(1)}, bf16[256,1024]{0,1:T(8,128)(2,1)S(1)}, u32[]{:S(2)}, u32[]{:S(2)}) collective-permute-start(bf16[256,1024]{0,1:T(8,128)(2,1)S(1)} %copy-done.52), channel_id=1, source_target_pairs={{0,8},{8,16},{16,24},{24,28},{28,20},{20,12},{12,4},{4,0},{1,9},{9... | collective-permute-start | bytes 1572872 | tf_op jit(solution)/shard_map/ppermute | solution.py:43
  297.9 43.8 %collective-permute-start.75 = (bf16[2,64,2048]{2,1,0:T(8,128)(2,1)S(1)}, bf16[2,64,2048]{2,1,0:T(8,128)(2,1)S(1)}, u32[]{:S(2)}, u32[]{:S(2)}) collective-permute-start(bf16[2,64,2048]{2,1,0:T(8,128)(2,1)S(1)} %constant_dynamic-update-slice_fusion.77), channel_id=1, source_target_pairs={{0,2},{1,3},{2,0},{3,1},{4,6},{5,7},{6,4},{7,5},{8,10},{9,11},{10,... | collective-permute-start | bytes 1572872 | tf_op jit(solution)/shard_map/ppermute | solution.py:108
  298.0 77.4 %collective-permute-start.74 = (bf16[2,64,2048]{2,1,0:T(8,128)(2,1)S(1)}, bf16[2,64,2048]{2,1,0:T(8,128)(2,1)}, u32[]{:S(2)}, u32[]{:S(2)}) collective-permute-start(bf16[2,64,2048]{2,1,0:T(8,128)(2,1)S(1)} %constant_dynamic-update-slice_fusion.77), channel_id=1, source_target_pairs={{0,1},{1,0},{2,3},{3,2},{4,5},{5,4},{6,7},{7,6},{8,9},{9,8},{10,11... | collective-permute-start | bytes 1572872 | tf_op jit(solution)/shard_map/ppermute | solution.py:108
  309.3 21.9 %collective-permute-start.38 = (bf16[2,64,2048]{2,1,0:T(8,128)(2,1)S(1)}, bf16[2,64,2048]{2,1,0:T(8,128)(2,1)S(1)}, u32[]{:S(2)}, u32[]{:S(2)}) collective-permute-start(bf16[2,64,2048]{2,1,0:T(8,128)(2,1)S(1)} %multiply_convert_fusion.7), channel_id=1, source_target_pairs={{0,2},{1,3},{2,0},{3,1},{4,6},{5,7},{6,4},{7,5},{8,10},{9,11},{10,... | collective-permute-start | bytes 1572872 | tf_op jit(solution)/shard_map/ppermute | solution.py:108
  313.6 21.9 %collective-permute-start.37 = (bf16[2,64,2048]{2,1,0:T(8,128)(2,1)S(1)}, bf16[2,64,2048]{2,1,0:T(8,128)(2,1)S(1)}, u32[]{:S(2)}, u32[]{:S(2)}) collective-permute-start(bf16[2,64,2048]{2,1,0:T(8,128)(2,1)S(1)} %multiply_convert_fusion.7), channel_id=1, source_target_pairs={{0,1},{1,0},{2,3},{3,2},{4,5},{5,4},{6,7},{7,6},{8,9},{9,8},{10,11... | collective-permute-start | bytes 1572872 | tf_op jit(solution)/shard_map/ppermute | solution.py:108
  341.7 33.7 %collective-permute-start.76 = (bf16[2,64,2048]{2,1,0:T(8,128)(2,1)S(1)}, bf16[2,64,2048]{2,1,0:T(8,128)(2,1)}, u32[]{:S(2)}, u32[]{:S(2)}) collective-permute-start(bf16[2,64,2048]{2,1,0:T(8,128)(2,1)S(1)} %collective-permute-done.75), channel_id=1, source_target_pairs={{0,1},{1,0},{2,3},{3,2},{4,5},{5,4},{6,7},{7,6},{8,9},{9,8},{10,11... | collective-permute-start | bytes 1572872 | tf_op jit(solution)/shard_map/ppermute | solution.py:108
  342.0 35.0 %collective-permute-start.60 = (bf16[256,2304]{1,0:T(8,128)(2,1)}, bf16[256,2304]{1,0:T(8,128)(2,1)}, u32[]{:S(2)}, u32[]{:S(2)}) collective-permute-start(bf16[256,2304]{1,0:T(8,128)(2,1)} %pad_maximum_fusion.16), channel_id=1, source_target_pairs={{8,0},{16,8},{24,16},{28,24},{20,28},{12,20},{4,12},{0,4},{9,1},{1... | collective-permute-start | bytes 3538952 | tf_op jit(solution)/shard_map/ppermute | solution.py:44
  342.0 35.4 %collective-permute-start.56 = (bf16[256,2304]{1,0:T(8,128)(2,1)}, bf16[256,2304]{1,0:T(8,128)(2,1)}, u32[]{:S(2)}, u32[]{:S(2)}) collective-permute-start(bf16[256,2304]{1,0:T(8,128)(2,1)} %pad_maximum_fusion.16), channel_id=1, source_target_pairs={{0,8},{8,16},{16,24},{24,28},{28,20},{20,12},{12,4},{4,0},{1,9},{9... | collective-permute-start | bytes 3538952 | tf_op jit(solution)/shard_map/ppermute | solution.py:43
  353.2 22.0 %collective-permute-start.49 = (bf16[2,256,256]{1,2,0:T(8,128)(2,1)S(1)}, bf16[2,256,256]{1,2,0:T(8,128)(2,1)S(1)}, u32[]{:S(2)}, u32[]{:S(2)}) collective-permute-start(bf16[2,256,256]{1,2,0:T(8,128)(2,1)S(1)} %broadcast_select_fusion.4), channel_id=1, source_target_pairs={{0,4},{4,0},{8,12},{12,8},{16,20},{20,16},{24,28},{28,24},{1,5},{5... | collective-permute-start | bytes 786440 | tf_op jit(solution)/shard_map/ppermute | solution.py:126
  377.0 41.8 %collective-permute-start.61 = (bf16[256,2304]{1,0:T(8,128)(2,1)}, bf16[256,2304]{1,0:T(8,128)(2,1)S(1)}, u32[]{:S(2)}, u32[]{:S(2)}) collective-permute-start(bf16[256,2304]{1,0:T(8,128)(2,1)} %collective-permute-done.60), channel_id=1, source_target_pairs={{8,0},{16,8},{24,16},{28,24},{20,28},{12,20},{4,12},{0,4},{9,1},{1... | collective-permute-start | bytes 3538952 | tf_op jit(solution)/shard_map/ppermute | solution.py:44
  377.3 41.6 %collective-permute-start.57 = (bf16[256,2304]{1,0:T(8,128)(2,1)}, bf16[256,2304]{1,0:T(8,128)(2,1)}, u32[]{:S(2)}, u32[]{:S(2)}) collective-permute-start(bf16[256,2304]{1,0:T(8,128)(2,1)} %collective-permute-done.56), channel_id=1, source_target_pairs={{0,8},{8,16},{16,24},{24,28},{28,20},{20,12},{12,4},{4,0},{1,9},{9... | collective-permute-start | bytes 3538952 | tf_op jit(solution)/shard_map/ppermute | solution.py:43
  418.9 29.4 %collective-permute-start.62 = (bf16[256,2304]{1,0:T(8,128)(2,1)S(1)}, bf16[256,2304]{1,0:T(8,128)(2,1)S(1)}, u32[]{:S(2)}, u32[]{:S(2)}) collective-permute-start(bf16[256,2304]{1,0:T(8,128)(2,1)S(1)} %collective-permute-done.61), channel_id=1, source_target_pairs={{8,0},{16,8},{24,16},{28,24},{20,28},{12,20},{4,12},{0,4},{9,1},{1... | collective-permute-start | bytes 3538952 | tf_op jit(solution)/shard_map/ppermute | solution.py:44
  418.9 27.8 %collective-permute-start.58 = (bf16[256,2304]{1,0:T(8,128)(2,1)}, bf16[256,2304]{1,0:T(8,128)(2,1)S(1)}, u32[]{:S(2)}, u32[]{:S(2)}) collective-permute-start(bf16[256,2304]{1,0:T(8,128)(2,1)} %collective-permute-done.57), channel_id=1, source_target_pairs={{0,8},{8,16},{16,24},{24,28},{28,20},{20,12},{12,4},{4,0},{1,9},{9... | collective-permute-start | bytes 3538952 | tf_op jit(solution)/shard_map/ppermute | solution.py:43
  423.3 26.8 %collective-permute-start.52 = (bf16[2,64,2048]{2,1,0:T(8,128)(2,1)S(1)}, bf16[2,64,2048]{2,1,0:T(8,128)(2,1)S(1)}, u32[]{:S(2)}, u32[]{:S(2)}) collective-permute-start(bf16[2,64,2048]{2,1,0:T(8,128)(2,1)S(1)} %fusion.93), channel_id=1, source_target_pairs={{0,2},{1,3},{2,0},{3,1},{4,6},{5,7},{6,4},{7,5},{8,10},{9,11},{10,... | collective-permute-start | bytes 1572872 | tf_op jit(solution)/shard_map/ppermute | solution.py:108
  446.8 28.3 %collective-permute-start.68 = (bf16[256,1152]{0,1:T(8,128)(2,1)S(1)}, bf16[256,1152]{0,1:T(8,128)(2,1)S(1)}, u32[]{:S(2)}, u32[]{:S(2)}) collective-permute-start(bf16[256,1152]{0,1:T(8,128)(2,1)S(1)} %copy-done.44), channel_id=1, source_target_pairs={{8,0},{16,8},{24,16},{28,24},{20,28},{12,20},{4,12},{0,4},{9,1},{1... | collective-permute-start | bytes 1769480 | tf_op jit(solution)/shard_map/ppermute | solution.py:44
  446.8 29.5 %collective-permute-start.64 = (bf16[256,1152]{0,1:T(8,128)(2,1)S(1)}, bf16[256,1152]{0,1:T(8,128)(2,1)S(1)}, u32[]{:S(2)}, u32[]{:S(2)}) collective-permute-start(bf16[256,1152]{0,1:T(8,128)(2,1)S(1)} %copy-done.44), channel_id=1, source_target_pairs={{0,8},{8,16},{16,24},{24,28},{28,20},{20,12},{12,4},{4,0},{1,9},{9... | collective-permute-start | bytes 1769480 | tf_op jit(solution)/shard_map/ppermute | solution.py:43
  448.3 28.7 %collective-permute-start.63 = (bf16[128,2304]{1,0:T(8,128)(2,1)S(1)}, bf16[128,2304]{1,0:T(8,128)(2,1)S(1)}, u32[]{:S(2)}, u32[]{:S(2)}) collective-permute-start(bf16[128,2304]{1,0:T(8,128)(2,1)S(1)} %slice.1256), channel_id=1, source_target_pairs={{8,0},{16,8},{24,16},{28,24},{20,28},{12,20},{4,12},{0,4},{9,1},{1... | collective-permute-start | bytes 1769480 | tf_op jit(solution)/shard_map/ppermute | solution.py:49
  448.6 25.1 %collective-permute-start.59 = (bf16[128,2304]{1,0:T(8,128)(2,1)S(1)}, bf16[128,2304]{1,0:T(8,128)(2,1)S(1)}, u32[]{:S(2)}, u32[]{:S(2)}) collective-permute-start(bf16[128,2304]{1,0:T(8,128)(2,1)S(1)} %slice.1255), channel_id=1, source_target_pairs={{0,8},{8,16},{16,24},{24,28},{28,20},{20,12},{12,4},{4,0},{1,9},{9... | collective-permute-start | bytes 1769480 | tf_op jit(solution)/shard_map/ppermute | solution.py:48
  451.1 40.0 %collective-permute-start.53 = (bf16[2,64,2048]{2,1,0:T(8,128)(2,1)S(1)}, bf16[2,64,2048]{2,1,0:T(8,128)(2,1)S(1)}, u32[]{:S(2)}, u32[]{:S(2)}) collective-permute-start(bf16[2,64,2048]{2,1,0:T(8,128)(2,1)S(1)} %multiply_convert_fusion.6), channel_id=1, source_target_pairs={{0,1},{1,0},{2,3},{3,2},{4,5},{5,4},{6,7},{7,6},{8,9},{9,8},{10,11... | collective-permute-start | bytes 1572872 | tf_op jit(solution)/shard_map/ppermute | solution.py:108
  544.3 36.0 %collective-permute-start.77 = (bf16[2,2,64,2048]{3,2,1,0:T(8,128)(2,1)S(1)}, bf16[2,2,64,2048]{3,2,1,0:T(8,128)(2,1)S(1)}, u32[]{:S(2)}, u32[]{:S(2)}) collective-permute-start(bf16[2,2,64,2048]{3,2,1,0:T(8,128)(2,1)S(1)} %pad_maximum_fusion.29), channel_id=1, source_target_pairs={{0,1},{1,0},{2,3},{3,2},{4,5},{5,4},{6,7},{7,6},{8,9},{9,8},{10,11... | collective-permute-start | bytes 3145736 | tf_op jit(solution)/shard_map/ppermute | solution.py:108
  550.8 30.9 %collective-permute-start.72 = (bf16[2,2,64,2048]{3,2,1,0:T(8,128)(2,1)S(1)}, bf16[2,2,64,2048]{3,2,1,0:T(8,128)(2,1)S(1)}, u32[]{:S(2)}, u32[]{:S(2)}) collective-permute-start(bf16[2,2,64,2048]{3,2,1,0:T(8,128)(2,1)S(1)} %pad_maximum_fusion.28), channel_id=1, source_target_pairs={{0,1},{1,0},{2,3},{3,2},{4,5},{5,4},{6,7},{7,6},{8,9},{9,8},{10,11... | collective-permute-start | bytes 3145736 | tf_op jit(solution)/shard_map/ppermute | solution.py:108
  552.3 25.4 %collective-permute-start.148 = (bf16[256,1152]{1,0:T(8,128)(2,1)S(1)}, bf16[256,1152]{1,0:T(8,128)(2,1)S(1)}, u32[]{:S(2)}, u32[]{:S(2)}) collective-permute-start(bf16[256,1152]{1,0:T(8,128)(2,1)S(1)} %add_convert_fusion.14), channel_id=1, source_target_pairs={{0,8},{8,16},{16,24},{24,28},{28,20},{20,12},{12,4},{4,0},{1,9},{9... | collective-permute-start | bytes 1769480 | tf_op jit(solution)/shard_map/ppermute | solution.py:75
  567.0 55.7 %collective-permute-start.132 = (bf16[256,2304]{1,0:T(8,128)(2,1)S(1)}, bf16[256,2304]{1,0:T(8,128)(2,1)S(1)}, u32[]{:S(2)}, u32[]{:S(2)}) collective-permute-start(bf16[256,2304]{1,0:T(8,128)(2,1)S(1)} %add_convert_fusion.2), channel_id=1, source_target_pairs={{0,8},{8,16},{16,24},{24,28},{28,20},{20,12},{12,4},{4,0},{1,9},{9... | collective-permute-start | bytes 3538952 | tf_op jit(solution)/shard_map/ppermute | solution.py:75
  577.7 49.4 %collective-permute-start.128 = (bf16[256,2304]{1,0:T(8,128)(2,1)S(1)}, bf16[256,2304]{1,0:T(8,128)(2,1)S(1)}, u32[]{:S(2)}, u32[]{:S(2)}) collective-permute-start(bf16[256,2304]{1,0:T(8,128)(2,1)S(1)} %add_convert_fusion.5), channel_id=1, source_target_pairs={{8,0},{16,8},{24,16},{28,24},{20,28},{12,20},{4,12},{0,4},{9,1},{1... | collective-permute-start | bytes 3538952 | tf_op jit(solution)/shard_map/ppermute | solution.py:74
  579.4 36.2 %collective-permute-start.149 = (bf16[256,1152]{1,0:T(8,128)(2,1)S(1)}, bf16[256,1152]{1,0:T(8,128)(2,1)S(1)}, u32[]{:S(2)}, u32[]{:S(2)}) collective-permute-start(bf16[256,1152]{1,0:T(8,128)(2,1)S(1)} %add_convert_fusion.13), channel_id=1, source_target_pairs={{0,8},{8,16},{16,24},{24,28},{28,20},{20,12},{12,4},{4,0},{1,9},{9... | collective-permute-start | bytes 1769480 | tf_op jit(solution)/shard_map/ppermute | solution.py:75
  580.4 40.7 %collective-permute-start.145 = (bf16[256,1152]{1,0:T(8,128)(2,1)S(1)}, bf16[256,1152]{1,0:T(8,128)(2,1)S(1)}, u32[]{:S(2)}, u32[]{:S(2)}) collective-permute-start(bf16[256,1152]{1,0:T(8,128)(2,1)S(1)} %add_convert_fusion.16), channel_id=1, source_target_pairs={{8,0},{16,8},{24,16},{28,24},{20,28},{12,20},{4,12},{0,4},{9,1},{1... | collective-permute-start | bytes 1769480 | tf_op jit(solution)/shard_map/ppermute | solution.py:74
  581.8 35.5 %collective-permute-start.78 = (bf16[2,64,2048]{2,1,0:T(8,128)(2,1)S(1)}, bf16[2,64,2048]{2,1,0:T(8,128)(2,1)S(1)}, u32[]{:S(2)}, u32[]{:S(2)}) collective-permute-start(bf16[2,64,2048]{2,1,0:T(8,128)(2,1)S(1)} %fusion.88), channel_id=1, source_target_pairs={{0,2},{1,3},{2,0},{3,1},{4,6},{5,7},{6,4},{7,5},{8,10},{9,11},{10,... | collective-permute-start | bytes 1572872 | tf_op jit(solution)/shard_map/ppermute | solution.py:108
  627.1 75.7 %collective-permute-start.133 = (bf16[256,2304]{1,0:T(8,128)(2,1)}, bf16[256,2304]{1,0:T(8,128)(2,1)}, u32[]{:S(2)}, u32[]{:S(2)}) collective-permute-start(bf16[256,2304]{1,0:T(8,128)(2,1)} %add_convert_fusion.1), channel_id=1, source_target_pairs={{0,8},{8,16},{16,24},{24,28},{28,20},{20,12},{12,4},{4,0},{1,9},{9... | collective-permute-start | bytes 3538952 | tf_op jit(solution)/shard_map/ppermute | solution.py:75
  635.8 73.9 %collective-permute-start.129 = (bf16[256,2304]{1,0:T(8,128)(2,1)}, bf16[256,2304]{1,0:T(8,128)(2,1)}, u32[]{:S(2)}, u32[]{:S(2)}) collective-permute-start(bf16[256,2304]{1,0:T(8,128)(2,1)} %add_convert_fusion.4), channel_id=1, source_target_pairs={{8,0},{16,8},{24,16},{28,24},{20,28},{12,20},{4,12},{0,4},{9,1},{1... | collective-permute-start | bytes 3538952 | tf_op jit(solution)/shard_map/ppermute | solution.py:74
  706.1 58.8 %collective-permute-start.134 = (bf16[256,2304]{1,0:T(8,128)(2,1)}, bf16[256,2304]{1,0:T(8,128)(2,1)}, u32[]{:S(2)}, u32[]{:S(2)}) collective-permute-start(bf16[256,2304]{1,0:T(8,128)(2,1)} %add_convert_fusion), channel_id=1, source_target_pairs={{0,8},{8,16},{16,24},{24,28},{28,20},{20,12},{12,4},{4,0},{1,9},{9... | collective-permute-start | bytes 3538952 | tf_op jit(solution)/shard_map/ppermute | solution.py:75
  709.4 28.0 %collective-permute-start.84 = (bf16[2,256,256]{1,2,0:T(8,128)(2,1)S(1)}, bf16[2,256,256]{1,2,0:T(8,128)(2,1)S(1)}, u32[]{:S(2)}, u32[]{:S(2)}) collective-permute-start(bf16[2,256,256]{1,2,0:T(8,128)(2,1)S(1)} %fusion.312), channel_id=1, source_target_pairs={{0,16},{4,20},{8,24},{12,28},{16,0},{20,4},{24,8},{28,12},{1,17},{... | collective-permute-start | bytes 786440 | tf_op jit(solution)/shard_map/ppermute | solution.py:126
  713.0 52.0 %collective-permute-start.130 = (bf16[256,2304]{1,0:T(8,128)(2,1)}, bf16[256,2304]{1,0:T(8,128)(2,1)}, u32[]{:S(2)}, u32[]{:S(2)}) collective-permute-start(bf16[256,2304]{1,0:T(8,128)(2,1)} %add_convert_fusion.3), channel_id=1, source_target_pairs={{8,0},{16,8},{24,16},{28,24},{20,28},{12,20},{4,12},{0,4},{9,1},{1... | collective-permute-start | bytes 3538952 | tf_op jit(solution)/shard_map/ppermute | solution.py:74
  763.0 24.0 %collective-permute-start.73 = (bf16[2,64,2048]{2,1,0:T(8,128)(2,1)S(1)}, bf16[2,64,2048]{2,1,0:T(8,128)(2,1)S(1)}, u32[]{:S(2)}, u32[]{:S(2)}) collective-permute-start(bf16[2,64,2048]{2,1,0:T(8,128)(2,1)S(1)} %copy-done.113), channel_id=1, source_target_pairs={{0,2},{1,3},{2,0},{3,1},{4,6},{5,7},{6,4},{7,5},{8,10},{9,11},{10,... | collective-permute-start | bytes 1572872 | tf_op jit(solution)/shard_map/ppermute | solution.py:108
  781.2 24.5 %collective-permute-start.111 = (bf16[256,1024]{1,0:T(8,128)(2,1)S(1)}, bf16[256,1024]{1,0:T(8,128)(2,1)S(1)}, u32[]{:S(2)}, u32[]{:S(2)}) collective-permute-start(bf16[256,1024]{1,0:T(8,128)(2,1)S(1)} %fusion.76), channel_id=1, source_target_pairs={{8,0},{16,8},{24,16},{28,24},{20,28},{12,20},{4,12},{0,4},{9,1},{1... | collective-permute-start | bytes 1572872 | tf_op jit(solution)/shard_map/ppermute | solution.py:74
  785.1 20.6 %collective-permute-start.115 = (bf16[256,1024]{1,0:T(8,128)(2,1)S(1)}, bf16[256,1024]{1,0:T(8,128)(2,1)S(1)}, u32[]{:S(2)}, u32[]{:S(2)}) collective-permute-start(bf16[256,1024]{1,0:T(8,128)(2,1)S(1)} %fusion.79), channel_id=1, source_target_pairs={{0,8},{8,16},{16,24},{24,28},{28,20},{20,12},{12,4},{4,0},{1,9},{9... | collective-permute-start | bytes 1572872 | tf_op jit(solution)/shard_map/ppermute | solution.py:75
  824.1 20.8 %collective-permute-start.123 = (bf16[128,2304]{1,0:T(8,128)(2,1)S(1)}, bf16[128,2304]{1,0:T(8,128)(2,1)S(1)}, u32[]{:S(2)}, u32[]{:S(2)}) collective-permute-start(bf16[128,2304]{1,0:T(8,128)(2,1)S(1)} %get-tuple-element.142), channel_id=1, source_target_pairs={{0,8},{8,16},{16,24},{24,28},{28,20},{20,12},{12,4},{4,0},{1,9},{9... | collective-permute-start | bytes 1769480 | tf_op jit(solution)/shard_map/ppermute | solution.py:72
  824.8 35.3 %collective-permute-start.90 = (bf16[2,2,64,2048]{3,2,1,0:T(8,128)(2,1)S(1)}, bf16[2,2,64,2048]{3,2,1,0:T(8,128)(2,1)S(1)}, u32[]{:S(2)}, u32[]{:S(2)}) collective-permute-start(bf16[2,2,64,2048]{3,2,1,0:T(8,128)(2,1)S(1)} %pad_maximum_fusion.31), channel_id=1, source_target_pairs={{0,1},{1,0},{2,3},{3,2},{4,5},{5,4},{6,7},{7,6},{8,9},{9,8},{10,11... | collective-permute-start | bytes 3145736 | tf_op jit(solution)/shard_map/ppermute | solution.py:108
  825.4 20.6 %collective-permute-start.119 = (bf16[128,2304]{1,0:T(8,128)(2,1)S(1)}, bf16[128,2304]{1,0:T(8,128)(2,1)S(1)}, u32[]{:S(2)}, u32[]{:S(2)}) collective-permute-start(bf16[128,2304]{1,0:T(8,128)(2,1)S(1)} %get-tuple-element.141), channel_id=1, source_target_pairs={{8,0},{16,8},{24,16},{28,24},{20,28},{12,20},{4,12},{0,4},{9,1},{1... | collective-permute-start | bytes 1769480 | tf_op jit(solution)/shard_map/ppermute | solution.py:71
  832.7 24.7 %collective-permute-start.140 = (bf16[256,1152]{1,0:T(8,128)(2,1)S(1)}, bf16[256,1152]{1,0:T(8,128)(2,1)S(1)}, u32[]{:S(2)}, u32[]{:S(2)}) collective-permute-start(bf16[256,1152]{1,0:T(8,128)(2,1)S(1)} %add_convert_fusion.20), channel_id=1, source_target_pairs={{0,8},{8,16},{16,24},{24,28},{28,20},{20,12},{12,4},{4,0},{1,9},{9... | collective-permute-start | bytes 1769480 | tf_op jit(solution)/shard_map/ppermute | solution.py:75
  833.6 24.7 %collective-permute-start.136 = (bf16[256,1152]{1,0:T(8,128)(2,1)S(1)}, bf16[256,1152]{1,0:T(8,128)(2,1)S(1)}, u32[]{:S(2)}, u32[]{:S(2)}) collective-permute-start(bf16[256,1152]{1,0:T(8,128)(2,1)S(1)} %add_convert_fusion.23), channel_id=1, source_target_pairs={{8,0},{16,8},{24,16},{28,24},{20,28},{12,20},{4,12},{0,4},{9,1},{1... | collective-permute-start | bytes 1769480 | tf_op jit(solution)/shard_map/ppermute | solution.py:74
  845.6 54.4 %collective-permute-start.124 = (bf16[256,2304]{1,0:T(8,128)(2,1)S(1)}, bf16[256,2304]{1,0:T(8,128)(2,1)S(1)}, u32[]{:S(2)}, u32[]{:S(2)}) collective-permute-start(bf16[256,2304]{1,0:T(8,128)(2,1)S(1)} %add_convert_fusion.8), channel_id=1, source_target_pairs={{0,8},{8,16},{16,24},{24,28},{28,20},{20,12},{12,4},{4,0},{1,9},{9... | collective-permute-start | bytes 3538952 | tf_op jit(solution)/shard_map/ppermute | solution.py:75
  846.8 56.9 %collective-permute-start.120 = (bf16[256,2304]{1,0:T(8,128)(2,1)S(1)}, bf16[256,2304]{1,0:T(8,128)(2,1)S(1)}, u32[]{:S(2)}, u32[]{:S(2)}) collective-permute-start(bf16[256,2304]{1,0:T(8,128)(2,1)S(1)} %add_convert_fusion.11), channel_id=1, source_target_pairs={{8,0},{16,8},{24,16},{28,24},{20,28},{12,20},{4,12},{0,4},{9,1},{1... | collective-permute-start | bytes 3538952 | tf_op jit(solution)/shard_map/ppermute | solution.py:74
  858.0 37.4 %collective-permute-start.141 = (bf16[256,1152]{1,0:T(8,128)(2,1)S(1)}, bf16[256,1152]{1,0:T(8,128)(2,1)S(1)}, u32[]{:S(2)}, u32[]{:S(2)}) collective-permute-start(bf16[256,1152]{1,0:T(8,128)(2,1)S(1)} %add_convert_fusion.19), channel_id=1, source_target_pairs={{0,8},{8,16},{16,24},{24,28},{28,20},{20,12},{12,4},{4,0},{1,9},{9... | collective-permute-start | bytes 1769480 | tf_op jit(solution)/shard_map/ppermute | solution.py:75
  858.9 37.4 %collective-permute-start.137 = (bf16[256,1152]{1,0:T(8,128)(2,1)S(1)}, bf16[256,1152]{1,0:T(8,128)(2,1)S(1)}, u32[]{:S(2)}, u32[]{:S(2)}) collective-permute-start(bf16[256,1152]{1,0:T(8,128)(2,1)S(1)} %add_convert_fusion.22), channel_id=1, source_target_pairs={{8,0},{16,8},{24,16},{28,24},{20,28},{12,20},{4,12},{0,4},{9,1},{1... | collective-permute-start | bytes 1769480 | tf_op jit(solution)/shard_map/ppermute | solution.py:74
  860.3 37.8 %collective-permute-start.91 = (bf16[2,64,2048]{2,1,0:T(8,128)(2,1)S(1)}, bf16[2,64,2048]{2,1,0:T(8,128)(2,1)S(1)}, u32[]{:S(2)}, u32[]{:S(2)}) collective-permute-start(bf16[2,64,2048]{2,1,0:T(8,128)(2,1)S(1)} %fusion.84), channel_id=1, source_target_pairs={{0,2},{1,3},{2,0},{3,1},{4,6},{5,7},{6,4},{7,5},{8,10},{9,11},{10,... | collective-permute-start | bytes 1572872 | tf_op jit(solution)/shard_map/ppermute | solution.py:108
  903.7 76.8 %collective-permute-start.125 = (bf16[256,2304]{1,0:T(8,128)(2,1)}, bf16[256,2304]{1,0:T(8,128)(2,1)}, u32[]{:S(2)}, u32[]{:S(2)}) collective-permute-start(bf16[256,2304]{1,0:T(8,128)(2,1)} %add_convert_fusion.7), channel_id=1, source_target_pairs={{0,8},{8,16},{16,24},{24,28},{28,20},{20,12},{12,4},{4,0},{1,9},{9... | collective-permute-start | bytes 3538952 | tf_op jit(solution)/shard_map/ppermute | solution.py:75
  909.7 78.8 %collective-permute-start.121 = (bf16[256,2304]{1,0:T(8,128)(2,1)}, bf16[256,2304]{1,0:T(8,128)(2,1)}, u32[]{:S(2)}, u32[]{:S(2)}) collective-permute-start(bf16[256,2304]{1,0:T(8,128)(2,1)} %add_convert_fusion.10), channel_id=1, source_target_pairs={{8,0},{16,8},{24,16},{28,24},{20,28},{12,20},{4,12},{0,4},{9,1},{1... | collective-permute-start | bytes 3538952 | tf_op jit(solution)/shard_map/ppermute | solution.py:74
  983.7 54.1 %collective-permute-start.126 = (bf16[256,2304]{1,0:T(8,128)(2,1)}, bf16[256,2304]{1,0:T(8,128)(2,1)S(1)}, u32[]{:S(2)}, u32[]{:S(2)}) collective-permute-start(bf16[256,2304]{1,0:T(8,128)(2,1)} %add_convert_fusion.6), channel_id=1, source_target_pairs={{0,8},{8,16},{16,24},{24,28},{28,20},{20,12},{12,4},{4,0},{1,9},{9... | collective-permute-start | bytes 3538952 | tf_op jit(solution)/shard_map/ppermute | solution.py:75
  987.4 27.3 %collective-permute-start.97 = (bf16[2,256,256]{1,2,0:T(8,128)(2,1)S(1)}, bf16[2,256,256]{1,2,0:T(8,128)(2,1)S(1)}, u32[]{:S(2)}, u32[]{:S(2)}) collective-permute-start(bf16[2,256,256]{1,2,0:T(8,128)(2,1)S(1)} %fusion.313), channel_id=1, source_target_pairs={{0,16},{4,20},{8,24},{12,28},{16,0},{20,4},{24,8},{28,12},{1,17},{... | collective-permute-start | bytes 786440 | tf_op jit(solution)/shard_map/ppermute | solution.py:126
  991.7 46.1 %collective-permute-start.122 = (bf16[256,2304]{1,0:T(8,128)(2,1)}, bf16[256,2304]{1,0:T(8,128)(2,1)}, u32[]{:S(2)}, u32[]{:S(2)}) collective-permute-start(bf16[256,2304]{1,0:T(8,128)(2,1)} %add_convert_fusion.9), channel_id=1, source_target_pairs={{8,0},{16,8},{24,16},{28,24},{20,28},{12,20},{4,12},{0,4},{9,1},{1... | collective-permute-start | bytes 3538952 | tf_op jit(solution)/shard_map/ppermute | solution.py:74
  (267 other events, 4116.1 us)

commit v2 on v1

v2 whole, which is shorter than its diff:
```python
import math

import jax
import jax.numpy as jnp
from jax import lax
from jax.experimental import pallas as pl
from jax.experimental.pallas import tpu as pltpu
from jax.sharding import PartitionSpec as P

QUERY_HEADS = 24
KEY_VALUE_HEADS = 6
HEAD_SIZE = 64
PROMPT = 1024
CONT = 128
NCONT = 8
SLOTS = 8
PROMPT_SLOTS = 4

norm_eps = 1e-06
rope_base = 10000.0
masked_score = -1000000000.0
low = jnp.bfloat16
full = jnp.float32
lanes = 2 * HEAD_SIZE
score_scale = 1.0 / math.sqrt(HEAD_SIZE)
in_hbm = pl.BlockSpec(memory_space=pltpu.HBM)
in_smem = pl.BlockSpec(memory_space=pltpu.SMEM)


def after(value, *needed):
    return lax.optimization_barrier((value, *needed))[0]


def shape_of(shape, dtype=low):
    return jax.ShapeDtypeStruct(shape, dtype)


def hint(microseconds):
    return pl.CostEstimate(
        flops=int(microseconds * FLOPS_PER_US), transcendentals=0, bytes_accessed=1024
    )


FLOPS_PER_US = 2e9


def ring_order(count):
    return [*range(0, count, 2), *range(count - 1, 0, -2)]


def ring_routes(count):
    order = ring_order(count)
    forward = [(order[i], order[(i + 1) % count]) for i in range(count)]
    return forward, [(there, here) for here, there in forward]


class Pieces:
    def __init__(self, arrays, places):
        self.arrays, self.places = arrays, places

    def copies(self, refs, source_ref, columns):
        for i, first, count, k in self.places:
            start = 0 if k is None else pl.multiple_of(source_ref[k] * count, count)
            yield refs[i].at[pl.ds(start, count), columns], first, count


def ring_gather(block, rows):
    count = lax.axis_size("dp")
    forward, backward = ring_routes(count)
    ahead, behind = [block], [block]
    for _ in range(1, count // 2):
        ahead.append(lax.ppermute(ahead[-1], "dp", forward))
        behind.append(lax.ppermute(behind[-1], "dp", backward))
    half = rows // 2
    far = (
        lax.ppermute(ahead[-1][:half], "dp", forward),
        lax.ppermute(behind[-1][half:], "dp", backward),
    )
    steps = [*zip(ahead[1:], behind[1:], strict=True), far]
    pieces = [(part, k * rows, rows) for k, part in enumerate(ahead)]
    middle = count // 2 * rows
    pieces += [(far[0], middle, half), (far[1], middle + half, rows - half)]
    pieces += [(part, (count - k) * rows, rows) for k, part in enumerate(behind) if k > 0]
    pieces = sorted(pieces, key=lambda piece: piece[1])
    arrays = [part for part, _, _ in pieces]
    return Pieces(arrays, [(i, first, size, None) for i, (_, first, size) in enumerate(pieces)]), steps


class RingSum:
    def __init__(self, chunk):
        self.count = lax.axis_size("dp")
        self.forward, self.backward = ring_routes(self.count)
        self.middle, self.step, self.chunk = self.count // 2, 0, chunk
        self.send(chunk((self.middle,), (), False))

    def send(self, parts):
        self.sent = parts
        self.arrived = (
            lax.ppermute(parts[0], "dp", self.backward),
            lax.ppermute(parts[1], "dp", self.forward),
        )

    def hold(self, value):
        return after(value, *self.arrived)

    def advance(self, *needed):
        if self.step + 1 == self.middle:
            return
        self.step += 1
        arrived = [after(part, *needed) for part in self.arrived] if needed else self.arrived
        self.send(self.chunk((self.middle - self.step, self.middle + self.step), arrived, False))

    def finish(self, *needed):
        while self.step + 1 < self.middle:
            self.advance(*needed)
        arrived = [after(part, *needed) for part in self.arrived] if needed else self.arrived
        return self.chunk((0,), arrived, True)[0]


def ring_sources():
    count = lax.axis_size("dp")
    order = jnp.array(ring_order(count), jnp.int32)
    place = jnp.array([ring_order(count).index(i) for i in range(count)], jnp.int32)
    own = jnp.sum(jnp.where(jnp.arange(count) == lax.axis_index("dp"), place, 0))
    steps = jnp.arange(count, dtype=jnp.int32)

    def pick(table, index):
        return jnp.sum(jnp.where(steps[None, :] == index[:, None], table[None, :], 0), axis=1)

    return pick(order, (own - steps) % count), (own - place) % count


def reorder(array, sources):
    count = sources.shape[0]
    width = array.shape[-1] // count
    return jnp.concatenate(
        [
            lax.dynamic_slice_in_dim(array, sources[k] * width, width, axis=array.ndim - 1)
            for k in range(count)
        ],
        axis=-1,
    )


def swap(block, distance):
    count = lax.axis_size("tensor")
    return lax.ppermute(block, "tensor", [(i, i ^ distance) for i in range(count)])


def tensor_gather(block):
    across = swap(block, 2)
    return block, swap(block, 1), across, swap(across, 1)


def tensor_scatter(kept, sent):
    arrived = swap(sent, 1)
    passing = kept[1].astype(full) + arrived[1].astype(full)
    across = swap(passing.astype(low), 2)
    return kept[0].astype(full) + arrived[0].astype(full) + across.astype(full)


def partner(block, bit):
    count = lax.axis_size("dp")
    return lax.ppermute(block, "dp", [(i, i ^ 1 << bit) for i in range(count)])


def share_prompt(rows, slot):
    held = jnp.where(slot >= 4, partner(rows, 2), rows)
    for bit in (0, 1):
        arrived = partner(held, bit)
        lower = slot // 2**bit % 2 == 0
        held = jnp.concatenate(
            [jnp.where(lower, held, arrived), jnp.where(lower, arrived, held)], axis=0
        )
    return held


def return_prompt(grads, slot, between):
    held = grads
    for bit in (1, 0):
        half = held.shape[0] // 2
        lower = slot // 2**bit % 2 == 0
        kept = jnp.where(lower, held[:half], held[half:])
        sent = jnp.where(lower, held[half:], held[:half])
        held = kept + partner(sent.astype(low), bit).astype(full)
        between(held)
    arrived = partner(held.astype(low), 2).astype(full)
    return jnp.where(slot < 4, held + arrived, 0.0)


def rms_forward(hidden, gain):
    inv_root = lax.rsqrt(jnp.mean(hidden * hidden, axis=-1, keepdims=True) + norm_eps)
    scaled = hidden * inv_root
    return (scaled * gain).astype(low), scaled, inv_root


def rms_backward(grad_normed, scaled, inv_root, gain):
    grad_gain = jnp.sum(grad_normed * scaled, axis=0)
    grad_scaled = grad_normed * gain
    centred = grad_scaled - scaled * jnp.mean(grad_scaled * scaled, axis=-1, keepdims=True)
    return inv_root * centred, grad_gain


def row_setup(branch_rows, slot, tensor_index, row_block):
    blocks = lax.axis_size("tensor")
    rows = row_block * blocks
    at = jnp.arange(rows, dtype=jnp.int32)
    local = (tensor_index ^ (at // row_block)) * row_block + at % row_block
    is_prompt = slot < PROMPT_SLOTS
    offset = jnp.maximum((slot - PROMPT_SLOTS) * rows, 0) + local
    cont_index = offset // CONT
    matches = cont_index[:, None] == jnp.arange(NCONT, dtype=jnp.int32)[None, :]
    start = jnp.sum(jnp.where(matches[None], branch_rows[:, None, :], 0), axis=2)
    positions = jnp.where(is_prompt, slot * rows + local, start + offset % CONT)
    limits = jnp.where(is_prompt, slot * rows, start)
    seq_ids = jnp.where(is_prompt, slot, PROMPT_SLOTS + cont_index)
    prompt_at = jnp.arange(PROMPT, dtype=jnp.int32)
    prompt_at = prompt_at // rows * rows + jnp.tile(local, PROMPT // rows)
    same = (seq_ids[:, None] == seq_ids[None, :]) & (local[:, None] <= local[None, :])
    bias = jnp.where(same, 0.0, masked_score)
    half = HEAD_SIZE // 2
    inv_freq = rope_base ** (-(2.0 * jnp.arange(half, dtype=full)) / HEAD_SIZE)
    positions = positions.reshape(-1, blocks, row_block).transpose(1, 0, 2).reshape(-1)
    angles = positions.astype(full)[:, None] * inv_freq
    cosine, sine = jnp.cos(angles), jnp.sin(angles)
    tables = (
        jnp.concatenate([cosine] * 4, axis=1),
        jnp.concatenate([-sine, sine, -sine, sine], axis=1),
    )
    return tables, (prompt_at[:, None], limits[:, None, :], bias)


def rotated(values, cosine, sine):
    half = HEAD_SIZE // 2
    first = lax.broadcasted_iota(jnp.int32, values.shape, 1) % HEAD_SIZE < half
    other = jnp.where(first, pltpu.roll(values, lanes - half, 1), pltpu.roll(values, half, 1))
    return values * cosine + other * sine


group_rows = 256


def dot(left, right):
    return jnp.dot(left, right, preferred_element_type=full)


def by_lanes(left, right):
    return lax.dot_general(left, right, (((1,), (1,)), ((), ())), preferred_element_type=full)


def by_rows(left, right):
    return lax.dot_general(left, right, (((0,), (0,)), ((), ())), preferred_element_type=full)


def gathered_call(sources, rows, pieces, parts, tile, epilogue, extras, outs, name, length):
    steps = parts[0][1] // tile
    block, width = rows[0].shape

    def kernel(source_ref, *refs):
        refs = list(refs)
        row_refs = [refs.pop(0) for _ in rows]
        piece_refs = [refs.pop(0) for _ in pieces.arrays]
        extra_refs = [refs.pop(0) for _ in extras]
        out_refs = [refs.pop(0) for _ in outs]
        row_buf, weight_buf, row_sem, weight_sem = refs
        step = pl.program_id(0)

        @pl.when(step == 0)
        def _():
            for j, ref in enumerate(row_refs):
                pltpu.make_async_copy(ref, row_buf.at[pl.ds(j * block, block)], row_sem).start()
            for at in range(steps):
                for p, (first, _) in enumerate(parts):
                    columns = pl.ds(first + at * tile, tile)
                    for ref, start, count in pieces.copies(piece_refs, source_ref, columns):
                        pltpu.make_async_copy(
                            ref,
                            weight_buf.at[at, p, pl.ds(start, count)],
                            weight_sem.at[at],
                        ).start()
            pltpu.make_async_copy(row_buf, row_buf, row_sem).wait()

        pltpu.make_async_copy(weight_buf.at[step], weight_buf.at[step], weight_sem.at[step]).wait()
        products = [dot(row_buf[...], weight_buf[step, p]) for p in range(len(parts))]
        epilogue(products, extra_refs, out_refs)

    total = block * len(rows)
    return pl.pallas_call(
        kernel,
        grid=(steps,),
        in_specs=[in_smem] + [in_hbm] * (len(rows) + len(pieces.arrays)) + [spec for _, spec in extras],
        out_shape=[shape for shape, _ in outs],
        out_specs=[spec for _, spec in outs],
        scratch_shapes=[
            pltpu.VMEM((total, width), low),
            pltpu.VMEM((steps, len(parts), width, tile), low),
            pltpu.SemaphoreType.DMA,
            pltpu.SemaphoreType.DMA((steps,)),
        ],
        compiler_params=pltpu.CompilerParams(vmem_limit_bytes=48 << 20),
        cost_estimate=hint(length),
        name=name,
    )(sources, *rows, *pieces.arrays, *[value for value, _ in extras])


def spread_call(sources, values, pieces, first, columns, width, block, prologue, outs, name, length):
    groups = width // group_rows

    def kernel(source_ref, *refs):
        refs = list(refs)
        piece_refs = [refs.pop(0) for _ in pieces.arrays]
        value_refs = [refs.pop(0) for _ in values]
        kept_ref, sent_ref = refs.pop(0), refs.pop(0)
        out_refs = [refs.pop(0) for _ in outs]
        row_buf, weight_buf, weight_sem = refs
        step = pl.program_id(0)

        @pl.when(step == 0)
        def _():
            for ref, start, count in pieces.copies(piece_refs, source_ref, pl.ds(first, columns)):
                pltpu.make_async_copy(
                    ref,
                    weight_buf.at[start // group_rows, pl.ds(start % group_rows, count)],
                    weight_sem.at[start // group_rows],
                ).start()
            prologue(value_refs, row_buf, out_refs)

        pltpu.make_async_copy(weight_buf.at[step], weight_buf.at[step], weight_sem.at[step]).wait()
        product = by_lanes(row_buf[...], weight_buf[step]).astype(low)
        kept_ref[0] = product[:block]
        sent_ref[0] = product[block : 2 * block]
        kept_ref[1] = product[2 * block : 3 * block]
        sent_ref[1] = product[3 * block :]

    part = pl.BlockSpec((2, block, group_rows), lambda g: (0, 0, g))
    return pl.pallas_call(
        kernel,
        grid=(groups,),
        in_specs=[in_smem] + [in_hbm] * len(pieces.arrays) + [whole_spec(value) for value in values],
        out_shape=[shape_of((2, block, width))] * 2 + list(outs),
        out_specs=[part, part] + [whole_spec(out) for out in outs],
        scratch_shapes=[
            pltpu.VMEM((4 * block, columns), low),
            pltpu.VMEM((groups, group_rows, columns), low),
            pltpu.SemaphoreType.DMA((groups,)),
        ],
        compiler_params=pltpu.CompilerParams(vmem_limit_bytes=40 << 20),
        cost_estimate=hint(length),
        name=name,
    )(sources, *pieces.arrays, *values)


def whole_spec(value):
    return pl.BlockSpec(value.shape, lambda *_: (0,) * len(value.shape))


def copy_rows(value_refs, row_buf, _):
    row_buf[...] = value_refs[0][...]


def ring_chunks(lefts, right, plan, dim_block, name, length, extra=None):
    total = right.shape[1]
    tile = total // len(plan)
    block = lefts[0][0].shape[0]
    half = dim_block // 2
    more = 0 if extra is None else extra.shape[1]

    def plain(ks, arrived, last):
        parts = []
        for k in ks:
            columns = []
            for step, segments in enumerate(plan):
                for left, first, end in segments:
                    rows = [part[:, k * dim_block : (k + 1) * dim_block] for part in lefts[left]]
                    cut = right[:, step * tile + first : step * tile + end]
                    columns.append(by_rows(jnp.concatenate(rows), cut))
            part = jnp.concatenate(columns, axis=1)
            parts.append(part if extra is None else jnp.concatenate([part, extra[k]], axis=0))
        if last:
            return [parts[0] + sum(piece.astype(full) for piece in arrived)]
        if len(ks) == 1:
            return [parts[0][:half].astype(low), parts[0][half:].astype(low)]
        if arrived[0].shape == parts[0].shape:
            return [(a + b.astype(full)).astype(low) for a, b in zip(parts, arrived, strict=True)]
        lower = jnp.concatenate([parts[0][:half] + arrived[0].astype(full), parts[0][half:]])
        upper = jnp.concatenate([parts[1][:half], parts[1][half:] + arrived[1].astype(full)])
        return [lower.astype(low), upper.astype(low)]

    if dim_block % 128:
        return plain

    def chunk(ks, arrived, last):
        split = len(ks) == 1 and not last
        halves = len(ks) == 2 and arrived[0].shape[0] < dim_block + more
        out_rows = (half, dim_block + more - half) if split else (dim_block + more,) * len(ks)

        def kernel(*refs):
            refs = list(refs)
            left_refs = [[[refs.pop(0) for _ in range(4)] for _ in lefts] for _ in ks]
            right_ref = refs.pop(0)
            extra_refs = [refs.pop(0) for _ in ks] if more else None
            arrived_refs = [refs.pop(0) for _ in arrived]
            out_refs = [refs.pop(0) for _ in out_rows]
            (turned,) = refs
            step = pl.program_id(0)

            def finished(first, value, which, a, b):
                end = first + value.shape[0]
                cols = slice(a, b)

                def plus(ref, start, stop, offset):
                    came = ref[start - offset : stop - offset, cols].astype(full)
                    return value[start - first : stop - first] + came

                if split:
                    if first == 0:
                        out_refs[0][:, cols] = value[:half].astype(low)
                        out_refs[1][: end - half, cols] = value[half:].astype(low)
                    else:
                        out_refs[1][first - half : end - half, cols] = value.astype(low)
                    return
                out = out_refs[which]
                if last:
                    for ref in arrived_refs:
                        value = value + ref[first:end, cols].astype(full)
                    out[first:end, cols] = value
                elif not halves:
                    out[first:end, cols] = plus(arrived_refs[which], first, end, 0).astype(low)
                elif which == 0 and first == 0:
                    out[:half, cols] = plus(arrived_refs[0], 0, half, 0).astype(low)
                    out[half:end, cols] = value[half:].astype(low)
                elif which == 0:
                    out[first:end, cols] = value.astype(low)
                else:
                    start = max(first, half)
                    if first < half:
                        out[first:half, cols] = value[: half - first].astype(low)
                    out[start:end, cols] = plus(arrived_refs[1], start, end, half).astype(low)

            ready = set()
            for at, segments in enumerate(plan):
                fresh = {left for left, _, _ in segments} - ready
                ready |= fresh

                @pl.when(step == at)
                def _(segments=segments, fresh=fresh):
                    for which in range(len(ks)):
                        for left in fresh:
                            for j, ref in enumerate(left_refs[which][left]):
                                turned[which, left, :, j * block : (j + 1) * block] = ref[...].T
                        for left, first, end in segments:
                            product = dot(turned[which, left], right_ref[:, first:end])
                            finished(0, product, which, first, end)
                        if more:
                            finished(dim_block, extra_refs[which][0], which, 0, tile)

        def left_spec(k):
            return pl.BlockSpec((block, dim_block), lambda t: (0, k))

        def tile_spec(rows):
            return pl.BlockSpec((rows, tile), lambda t: (0, t))

        def extra_spec(k):
            return pl.BlockSpec((1, more, tile), lambda t: (k, 0, t))

        in_specs = [left_spec(k) for k in ks for _ in lefts for _ in range(4)]
        in_specs.append(tile_spec(4 * block))
        if more:
            in_specs += [extra_spec(k) for k in ks]
        in_specs += [tile_spec(part.shape[0]) for part in arrived]
        return pl.pallas_call(
            kernel,
            grid=(len(plan),),
            in_specs=in_specs,
            out_shape=[shape_of((rows, total), full if last else low) for rows in out_rows],
            out_specs=[tile_spec(rows) for rows in out_rows],
            scratch_shapes=[pltpu.VMEM((len(ks), len(lefts), dim_block, 4 * block), low)],
            compiler_params=pltpu.CompilerParams(vmem_limit_bytes=32 << 20),
            cost_estimate=hint(length * len(ks)),
            name=name,
        )(
            *[rows for _ in ks for left in lefts for rows in left],
            right,
            *([extra] * len(ks) if more else []),
            *arrived,
        )

    return chunk


def uses_last(odd_ref):
    pair = pl.program_id(1)
    return (pair == 2) | ((pair == 1) & (odd_ref[0] == 1))


def lower_lanes(shape):
    return lax.broadcasted_iota(jnp.int32, shape, 1) < HEAD_SIZE


def flat(ref):
    value = ref[:, 0]
    return value.reshape(-1, value.shape[-1])


def both_halves(kv_ref, last):
    both = flat(kv_ref).astype(full)
    turned = pltpu.roll(both, HEAD_SIZE, 1)
    lower = lower_lanes(both.shape).astype(jnp.int32)
    return jnp.where(lower == last.astype(jnp.int32), turned, both).astype(low)


def of_head(pair_rows, head):
    lower = lower_lanes(pair_rows.shape)
    return jnp.where(lower if head == 0 else ~lower, pair_rows, jnp.zeros_like(pair_rows))


def attend_kernel(
    odd_ref, q_ref, pk_ref, pv_ref, lk_ref, lv_ref, at_ref, limit_ref, bias_ref,
    out_ref, pp_ref, lp_ref,
):
    last = uses_last(odd_ref)
    prompt_keys, own_keys = both_halves(pk_ref, last), both_halves(lk_ref, last)
    prompt_values, own_values = both_halves(pv_ref, last), both_halves(lv_ref, last)
    early = at_ref[...] < limit_ref[0]
    bias = bias_ref[...]
    parts = []
    for head in range(2):
        query = of_head(flat(q_ref), head)
        far = jnp.where(early, by_lanes(prompt_keys, query), masked_score)
        near = by_lanes(own_keys, query) + bias
        top = jnp.maximum(
            jnp.max(far, axis=0, keepdims=True), jnp.max(near, axis=0, keepdims=True)
        )
        far, near = jnp.exp(far - top), jnp.exp(near - top)
        total = jnp.sum(far, axis=0, keepdims=True) + jnp.sum(near, axis=0, keepdims=True)
        inverse = 1.0 / total
        far, near = (far * inverse).astype(low), (near * inverse).astype(low)
        pp_ref[0, head] = far
        lp_ref[0, head] = near
        parts.append(by_rows(prompt_values, far) + by_rows(own_values, near))
    upper = lax.broadcasted_iota(jnp.int32, parts[0].shape, 0) < HEAD_SIZE
    out = jnp.where(upper, parts[0], parts[1]).T.astype(low)
    out_ref[:, 0] = out.reshape(out_ref.shape[0], *out_ref.shape[2:])


def attend_backward_kernel(
    odd_ref, grad_ref, q_ref, pk_ref, pv_ref, lk_ref, lv_ref, pp_ref, lp_ref,
    gq_ref, gp_ref, gl_ref,
):
    last = uses_last(odd_ref)
    prompt_keys, own_keys = both_halves(pk_ref, last), both_halves(lk_ref, last)
    prompt_values, own_values = both_halves(pv_ref, last), both_halves(lv_ref, last)
    parts, prompt_k, prompt_v, own_k, own_v = [], 0.0, 0.0, 0.0, 0.0
    for head in range(2):
        query, grad = of_head(flat(q_ref), head), of_head(flat(grad_ref), head)
        far, near = pp_ref[0, head], lp_ref[0, head]
        far_full, near_full = far.astype(full), near.astype(full)
        far_grad = far_full * by_lanes(prompt_values, grad)
        near_grad = near_full * by_lanes(own_values, grad)
        mean = jnp.sum(far_grad, axis=0, keepdims=True) + jnp.sum(near_grad, axis=0, keepdims=True)
        far_grad = (far_grad - far_full * mean).astype(low)
        near_grad = (near_grad - near_full * mean).astype(low)
        prompt_v += dot(far, grad)
        own_v += dot(near, grad)
        prompt_k += dot(far_grad, query)
        own_k += dot(near_grad, query)
        parts.append(by_rows(prompt_keys, far_grad) + by_rows(own_keys, near_grad))
    upper = lax.broadcasted_iota(jnp.int32, parts[0].shape, 0) < HEAD_SIZE
    grad_query = jnp.where(upper, parts[0], parts[1]).T * score_scale
    gq_ref[:, 0] = grad_query.reshape(gq_ref.shape[0], *gq_ref.shape[2:])

    def add(ref, first, rows):
        both = rows + pltpu.roll(rows, HEAD_SIZE, 1)
        lower = lower_lanes(rows.shape).astype(jnp.int32)
        part = jnp.where(lower == last.astype(jnp.int32), 0.0, both)
        ref[:, 0, :, first : first + lanes] += part.reshape(ref.shape[0], ref.shape[2], lanes)

    @pl.when(pl.program_id(1) == 0)
    def _():
        gp_ref[...] = jnp.zeros_like(gp_ref)
        gl_ref[...] = jnp.zeros_like(gl_ref)

    add(gp_ref, 0, prompt_k)
    add(gp_ref, lanes, prompt_v)
    add(gl_ref, 0, own_k)
    add(gl_ref, lanes, own_v)


def attend_specs(query, prompt_kv):
    blocks, _, rows, _ = query.shape
    many = prompt_kv.shape[0]
    keys, own = many * rows, blocks * rows
    inputs = [
        pl.BlockSpec((blocks, 1, rows, lanes), lambda m, g, odd: (0, m, 0, g)),
        pl.BlockSpec((many, 1, rows, lanes), lambda m, g, odd: (0, m, 0, 0)),
        pl.BlockSpec((many, 1, rows, lanes), lambda m, g, odd: (0, m, 0, 1)),
        pl.BlockSpec((blocks, 1, rows, lanes), lambda m, g, odd: (0, m, 0, 0)),
        pl.BlockSpec((blocks, 1, rows, lanes), lambda m, g, odd: (0, m, 0, 1)),
    ]
    kept = [
        pl.BlockSpec((1, 2, keys, own), lambda m, g, odd: (m, g, 0, 0)),
        pl.BlockSpec((1, 2, own, own), lambda m, g, odd: (m, g, 0, 0)),
    ]
    return inputs, kept, keys, own


def attend_forward(odd, query, prompt_kv, own_kv, at, limits, bias):
    _, micro, _, width = query.shape
    heads = width // HEAD_SIZE
    inputs, kept, keys, own = attend_specs(query, prompt_kv)
    return pl.pallas_call(
        attend_kernel,
        out_shape=(
            shape_of(query.shape),
            pltpu.HBM((micro, heads, keys, own), low),
            pltpu.HBM((micro, heads, own, own), low),
        ),
        grid_spec=pltpu.PrefetchScalarGridSpec(
            num_scalar_prefetch=1,
            grid=(micro, heads // 2),
            in_specs=[
                *inputs,
                pl.BlockSpec((keys, 1), lambda m, g, odd: (0, 0)),
                pl.BlockSpec((1, 1, own), lambda m, g, odd: (m, 0, 0)),
                pl.BlockSpec((own, own), lambda m, g, odd: (0, 0)),
            ],
            out_specs=[inputs[0], *kept],
        ),
        compiler_params=pltpu.CompilerParams(vmem_limit_bytes=40 << 20),
        cost_estimate=hint(14),
        name="attend",
    )(odd, query, prompt_kv, prompt_kv, own_kv, own_kv, at, limits, bias)


def attend_backward(odd, grad, query, prompt_kv, own_kv, prompt_probs, own_probs):
    _, micro, _, width = query.shape
    heads = width // HEAD_SIZE
    inputs, kept, _, _ = attend_specs(query, prompt_kv)
    prompt_probs = pltpu.with_memory_space_constraint(prompt_probs, pltpu.HBM)
    own_probs = pltpu.with_memory_space_constraint(own_probs, pltpu.HBM)

    def summed(value):
        shape = (value.shape[0], 1, *value.shape[2:])
        return pl.BlockSpec(shape, lambda m, g, odd: (0, m, 0, 0))

    return pl.pallas_call(
        attend_backward_kernel,
        out_shape=(
            shape_of(query.shape, full),
            shape_of(prompt_kv.shape, full),
            shape_of(own_kv.shape, full),
        ),
        grid_spec=pltpu.PrefetchScalarGridSpec(
            num_scalar_prefetch=1,
            grid=(micro, heads // 2),
            in_specs=[inputs[0], *inputs, *kept],
            out_specs=[inputs[0], summed(prompt_kv), summed(own_kv)],
        ),
        compiler_params=pltpu.CompilerParams(vmem_limit_bytes=40 << 20),
        cost_estimate=hint(16),
        name="attend_back",
    )(odd, grad, query, prompt_kv, prompt_kv, own_kv, own_kv, prompt_probs, own_probs)


def key_value_grads(own, parts, heads, share):
    layers, (rows, _) = len(parts), parts[0][0].shape
    count = len(parts[0])
    width = KEY_VALUE_HEADS * HEAD_SIZE

    def kernel(own_ref, *refs):
        ins, outs = refs[:-2], refs[-2:]
        lower = lower_lanes((rows, lanes))
        for layer in range(layers):
            for out, first in zip(outs, (0, lanes), strict=True):
                totals = [jnp.zeros((rows, lanes), full) for _ in range(width // lanes)]
                for index in range(count):
                    head = index * heads // share
                    for distance in range(count):
                        keep = (own_ref[0] == index ^ distance).astype(full)
                        both = ins[layer * count + distance][:, first : first + lanes].astype(full) * keep
                        if head % 2 == 0:
                            totals[head // 2] += both
                            continue
                        turned = pltpu.roll(both, HEAD_SIZE, 1)
                        totals[head // 2] += jnp.where(lower, 0.0, turned)
                        totals[head // 2 + 1] += jnp.where(lower, turned, 0.0)
                for at, total in enumerate(totals):
                    out[layer, :, at * lanes : (at + 1) * lanes] = total

    flat_parts = [part for layer in parts for part in layer]
    return pl.pallas_call(
        kernel,
        out_shape=[shape_of((layers, rows, width), full)] * 2,
        in_specs=[in_smem] + [pl.BlockSpec(memory_space=pltpu.VMEM)] * len(flat_parts),
        out_specs=[pl.BlockSpec(memory_space=pltpu.VMEM)] * 2,
        compiler_params=pltpu.CompilerParams(vmem_limit_bytes=16 << 20),
        cost_estimate=hint(3),
        name="key_value_grads",
    )(own, *flat_parts)


def per_device(
    hidden_in,
    attn_gain,
    query_weight,
    key_matrix,
    value_matrix,
    out_weight,
    ffn_gain,
    gate_weight,
    up_weight,
    down_weight,
    branch_at,
    cotangent,
):
    tensor_count = lax.axis_size("tensor")
    rank = lax.axis_index("dp")
    tensor_index = lax.axis_index("tensor")
    slot = rank % SLOTS
    micro, row_block, width = hidden_in.shape
    block = micro * row_block
    rows = block * tensor_count
    layers = attn_gain.shape[0]
    q_width = query_weight.shape[2]
    heads = q_width // HEAD_SIZE
    units = gate_weight.shape[2]
    share = QUERY_HEADS // KEY_VALUE_HEADS
    kv_first = tensor_index * heads // share
    qkv_width = q_width + 2 * lanes
    dim_block = query_weight.shape[1]
    four = (tensor_count, micro, row_block)

    sources, places = ring_sources()
    branch_rows = lax.dynamic_index_in_dim(branch_at, rank // SLOTS, 1, keepdims=False)
    (cosine, sine), masks = row_setup(branch_rows, slot, tensor_index, row_block)
    odd_flag = (tensor_index % 2).astype(jnp.int32).reshape(1)

    kv_weight = lax.dynamic_slice_in_dim(
        jnp.stack([key_matrix, value_matrix], axis=2).reshape(
            layers, dim_block, 2, KEY_VALUE_HEADS * HEAD_SIZE
        ),
        kv_first * HEAD_SIZE,
        lanes,
        axis=3,
    ).reshape(layers, dim_block, 2 * lanes)
    gain_row = jnp.concatenate([attn_gain, ffn_gain], axis=0).reshape(1, -1)
    pack_width = qkv_width + q_width
    gain_rows = 16 * (-(-gain_row.shape[1] // (16 * pack_width)))
    gain_row = jnp.pad(gain_row, ((0, 0), (0, -gain_row.shape[1] % pack_width)))
    gain_row = gain_row.reshape(-1, pack_width)
    gain_pad = jnp.pad(gain_row, ((0, gain_rows - gain_row.shape[0]), (0, 0)))
    packs = []
    arrivals = []
    for layer in range(layers):
        attn_pack = jnp.concatenate(
            [query_weight[layer], kv_weight[layer], out_weight[layer].T], axis=1
        )
        if layer == 0:
            attn_pack = jnp.concatenate([attn_pack, gain_pad], axis=0)
        ffn_pack = jnp.concatenate(
            [gate_weight[layer], up_weight[layer], down_weight[layer].T], axis=1
        )
        gathered = []
        for piece in (attn_pack, ffn_pack):
            if arrivals:
                piece = after(piece, *arrivals[-1][-2])
            pieces, steps = ring_gather(piece, dim_block)
            arrivals.append(steps)
            gathered.append(pieces)
        packs.append(gathered)
    gains = jnp.stack(
        [
            piece[size : size + gain_row.shape[0]].reshape(-1)[: 2 * layers * dim_block]
            for piece, (_, first, size, _) in zip(packs[0][0].arrays, packs[0][0].places, strict=True)
            if (first + size) % dim_block == 0
        ]
    ).reshape(-1, 2, layers, dim_block)
    gains = gains.transpose(1, 2, 0, 3).reshape(2, layers, width).astype(full)

    unit_tile = units // 3

    def tiled(total, tile):
        return pl.BlockSpec((total, tile), lambda t: (0, t))

    def qkv_epilogue(products, extra_refs, out_refs):
        cos, sin = extra_refs[0][...], extra_refs[1][...]
        for at in range(0, q_width, lanes):
            head = rotated(products[0][:, at : at + lanes], cos, sin) * score_scale
            out_refs[0][:, at : at + lanes] = head.astype(low)
        key = rotated(products[0][:, q_width : q_width + lanes], cos, sin)
        out_refs[1][:, :lanes] = key.astype(low)
        out_refs[1][:, lanes:] = products[0][:, q_width + lanes :].astype(low)

    def active_epilogue(products, _, out_refs):
        gate, up = products
        out_refs[0][...] = (gate * jax.nn.sigmoid(gate) * up).astype(low)
        out_refs[1][...] = gate.astype(low)
        out_refs[2][...] = up.astype(low)

    def active_backward(products, extra_refs, out_refs):
        grad = products[0]
        gate, up = extra_refs[0][...].astype(full), extra_refs[1][...].astype(full)
        sig = jax.nn.sigmoid(gate)
        at = pl.multiple_of(pl.program_id(0) * unit_tile, 128)
        out = out_refs[0]
        out[:, pl.ds(at, unit_tile)] = (
            grad * up * sig * (1.0 + gate * (1.0 - sig))
        ).astype(low)
        out[:, pl.ds(units + at, unit_tile)] = (grad * gate * sig).astype(low)

    def plain_epilogue(products, _, out_refs):
        out_refs[0][...] = products[0].astype(low)

    def rotate_back(value_refs, row_buf, out_refs):
        query_ref, kv_ref, cos_ref, sin_ref = value_refs
        cos, sin = cos_ref[...], -sin_ref[...]
        for at in range(0, q_width, lanes):
            row_buf[:, at : at + lanes] = rotated(query_ref[:, at : at + lanes], cos, sin).astype(low)
        row_buf[:, q_width : q_width + lanes] = rotated(kv_ref[:, :lanes], cos, sin).astype(low)
        row_buf[:, q_width + lanes :] = kv_ref[:, lanes:].astype(low)
        out_refs[0][...] = row_buf[...]

    def arrived(value, *wanted):
        needed = [
            part
            for chain, step in wanted
            if chain < len(arrivals)
            for part in (arrivals[chain][step])
        ]
        return after(value, *needed) if needed else value

    hidden = reorder(hidden_in.reshape(block, width), sources).astype(full)
    saved = []
    for layer in range(layers):
        attn_pieces, ffn_pieces = packs[layer]
        normed, scaled, inv_root = rms_forward(hidden, gains[0, layer])
        normed_all = tensor_gather(normed)
        normed_all = (arrived(normed_all[0], (2 * layer + 1, 0)), *normed_all[1:])
        query_rot, own_kv = gathered_call(
                sources,
            normed_all,
            attn_pieces,
            [(0, qkv_width)],
            qkv_width,
            qkv_epilogue,
            [(cosine, whole_spec(cosine)), (sine, whole_spec(sine))],
            [
                (shape_of((rows, q_width)), pl.BlockSpec((rows, q_width), lambda t: (0, 0))),
                (shape_of((rows, 2 * lanes)), pl.BlockSpec((rows, 2 * lanes), lambda t: (0, 0))),
            ],
            "queries_keys_values",
            6,
        )
        query_rot, own_kv = query_rot.reshape(*four, -1), own_kv.reshape(*four, -1)
        prompt_kv = share_prompt(own_kv, slot)
        prompt_kv = arrived(prompt_kv, (2 * layer + 1, 1))
        attended, prompt_probs, own_probs = attend_forward(
            odd_flag, query_rot, prompt_kv, own_kv, *masks
        )
        attended = attended.reshape(rows, q_width)
        parts = spread_call(
                sources,
            [attended], attn_pieces, qkv_width, q_width, width, block, copy_rows, [], "out", 4
        )
        if layer == 0:
            parts = (arrived(parts[0], (1, 2)), *parts[1:])
        middle = hidden + tensor_scatter(*parts)
        middle = arrived(middle, *([(1, 3), (2, 0)] if layer == 0 else [(3, 2)]))
        normed_ffn, scaled_ffn, inv_root_ffn = rms_forward(middle, gains[1, layer])
        normed_ffn_all = tensor_gather(normed_ffn)
        normed_ffn_all = (arrived(normed_ffn_all[0], (2 * layer + 2, 1)), *normed_ffn_all[1:])
        active, gate, up = gathered_call(
                sources,
            normed_ffn_all,
            ffn_pieces,
            [(0, units), (units, units)],
            unit_tile,
            active_epilogue,
            [],
            [(shape_of((rows, units)), tiled(rows, unit_tile))] * 3,
            "active",
            9,
        )
        active = arrived(active, (2 * layer + 2, 3))
        parts = spread_call(
                sources,
            [active], ffn_pieces, 2 * units, units, width, block, copy_rows, [], "down", 5
        )
        hidden = middle + tensor_scatter(*parts)
        saved.append(
            (
                (normed_all, scaled, inv_root, attended),
                (query_rot, prompt_kv, own_kv, prompt_probs, own_probs),
                (normed_ffn_all, scaled_ffn, inv_root_ffn, gate, up, active),
            )
        )
    layer_out = reorder(hidden, places)

    grad_out = reorder(cotangent.reshape(block, width), sources).astype(full)
    gain_grads = [[None] * layers, [None] * layers]
    attn_grad, gate_up_grad, down_grad = [None] * layers, [None] * layers, [None] * layers
    for layer in reversed(range(layers)):
        attn_pieces, ffn_pieces = packs[layer]
        attn_saved, attend_saved, ffn_saved = saved[layer]
        normed_all, scaled, inv_root, attended = attn_saved
        normed_ffn_all, scaled_ffn, inv_root_ffn, gate, up, active = ffn_saved
        grad_branch = tensor_gather(grad_out.astype(low))
        grad_units = gathered_call(
                sources,
            grad_branch,
            ffn_pieces,
            [(2 * units, units)],
            unit_tile,
            active_backward,
            [(value, tiled(rows, unit_tile)) for value in (gate, up)],
            [(shape_of((rows, 2 * units)), pl.BlockSpec((rows, 2 * units), lambda t: (0, 0)))],
            "active_back",
            7,
        )[0]
        parts = spread_call(
                sources,
            [grad_units], ffn_pieces, 0, 2 * units, width, block, copy_rows, [], "ffn_back", 8
        )
        down_grad[layer] = RingSum(
            ring_chunks([grad_branch], active, [[(0, 0, units)]], dim_block, "down_chunk", 1.5)
        )
        gate_up_grad[layer] = RingSum(
            ring_chunks(
                [normed_ffn_all],
                grad_units,
                [[(0, 0, units)], [(0, 0, units)]],
                dim_block,
                "gate_up_chunk",
                2.5,
            )
        )
        grad_mid_norm, gain_grads[1][layer] = rms_backward(
            tensor_scatter(*parts), scaled_ffn, inv_root_ffn, gains[1, layer]
        )
        grad_middle = grad_out + grad_mid_norm
        grad_branch1 = tensor_gather(grad_middle.astype(low))
        grad_attended = gathered_call(
                sources,
            grad_branch1,
            attn_pieces,
            [(qkv_width, q_width)],
            q_width,
            plain_epilogue,
            [],
            [(shape_of((rows, q_width)), pl.BlockSpec((rows, q_width), lambda t: (0, 0)))],
            "attended_back",
            4,
        )[0].reshape(*four, -1)
        grad_query, grad_prompt, grad_own = attend_backward(odd_flag, grad_attended, *attend_saved)
        stages = []
        grad_kv = grad_own + return_prompt(grad_prompt, slot, stages.append)
        kept, sent, grad_attn = spread_call(
                sources,
            [grad_query.reshape(rows, -1), grad_kv.reshape(rows, -1), cosine, sine],
            attn_pieces,
            0,
            qkv_width,
            width,
            block,
            rotate_back,
            [shape_of((rows, qkv_width))],
            "normed_back",
            6,
        )
        grad_normed = tensor_scatter(kept, sent)
        grad_hidden_norm, gain_grads[0][layer] = rms_backward(
            grad_normed, scaled, inv_root, gains[0, layer]
        )
        grad_out = grad_middle + grad_hidden_norm
        gain_all = None
        if layer == 0:
            gain_all = jnp.stack([jnp.stack(gain_grads[0]), jnp.stack(gain_grads[1])])
            gain_all = gain_all.reshape(2 * layers, -1, dim_block).transpose(1, 0, 2)
            gain_all = gain_all.reshape(gain_all.shape[0], -1)
            used = -(-gain_all.shape[1] // pack_width)
            spare = used * pack_width - gain_all.shape[1]
            gain_all = jnp.pad(gain_all, ((0, 0), (0, spare))).reshape(-1, used, pack_width)
            gain_all = jnp.pad(gain_all, ((0, 0), (0, 16 - used), (0, 0)))
        attn_grad[layer] = RingSum(
            ring_chunks(
                [normed_all, grad_branch1],
                jnp.concatenate([grad_attn, attended], axis=1),
                [[(0, 0, qkv_width), (1, qkv_width, pack_width)]],
                dim_block,
                "attn_chunk",
                2,
                gain_all,
            )
        )
    first = attn_grad[0].sent
    for rings in (attn_grad, gate_up_grad, down_grad):
        rings[:] = [
            ring.finish(*(first if layer == 0 and ring is not attn_grad[0] else ()))
            for layer, ring in enumerate(rings)
        ]
    input_grad = reorder(grad_out, places)

    parts = []
    for layer in range(layers):
        shared = attn_grad[layer].astype(low)
        shared = shared[:, q_width:qkv_width] if layer else shared
        parts.append(tensor_gather(shared))
    kv_parts = [[part[:dim_block, q_width:qkv_width] if i == 0 else part for part in layer] for i, layer in enumerate(parts)]
    key_grad, value_grad = key_value_grads(tensor_index.reshape(1), kv_parts, heads, share)
    gain_sum = sum(part[dim_block:].astype(full) for part in parts[0]).reshape(-1)
    gain_sum = gain_sum[: 2 * layers * dim_block].reshape(2, layers, dim_block)

    return (
        layer_out.reshape(hidden_in.shape),
        input_grad.reshape(hidden_in.shape),
        gain_sum[0],
        jnp.stack([grad[:dim_block, :q_width] for grad in attn_grad]),
        key_grad,
        value_grad,
        jnp.stack([grad[:dim_block, qkv_width:].T for grad in attn_grad]),
        gain_sum[1],
        jnp.stack([grad[:, :units] for grad in gate_up_grad]),
        jnp.stack([grad[:, units:] for grad in gate_up_grad]),
        jnp.stack([grad[:, :units].T for grad in down_grad]),
    )


def solution(mesh):
    rows = P(None, ("dp", "tensor"), None)
    split = P(None, "dp", "tensor")
    across = P(None, "tensor", "dp")
    whole = P(None, "dp", None)
    gain = P(None, "dp")
    return jax.shard_map(
        per_device,
        mesh=mesh,
        in_specs=(rows, gain, split, whole, whole, across, gain, split, split, across, P(), rows),
        out_specs=(rows, rows, gain, split, whole, whole, across, gain, split, split, across),
        check_vma=False,
    )
```

time: 1150 us -> 1070 us (0.930)
  Pallas kernels: 0 us -> 234 us
  matrix products: 224 us -> 0 us
  other arithmetic: 91.2 us -> 46.2 us
  starting transfers between devices: 204 us -> 176 us
  local copies, waits for them, and re-layouts: 105 us -> 80.7 us
    pallas_call x0 -> x51, Pallas kernels: none -> 234 us  [the longest x8 63.3 us: gathered_call(): pl.pallas_call(kernel, grid=(steps,), in_specs=[in_smem] + [in_hbm] * (le...]
    dot_general x92 -> x0, matrix products: 224 us -> none  [the longest x64 73.9 us: dot_left_t(): lax.dot_general(left, right, (((0,), (0,)), ((), ())), preferred_element_...]
    ppermute x18 -> x12, waiting for transfers between devices: 35.2 us -> 96.9 us  [ring_gather(): behind.append(lax.ppermute(behind[-1], 'dp', backward))]
    ppermute x18 -> x12, waiting for transfers between devices: 60.1 us -> 3.27 us  [ring_gather(): ahead.append(lax.ppermute(ahead[-1], 'dp', forward))]
    ppermute x43 -> x46, waiting for transfers between devices: 48.9 us -> 95.9 us  [swap(): lax.ppermute(block, 'tensor', [(i, i ^ distance) for i in range(count)])]
    ppermute x6 -> x4, waiting for transfers between devices: 45.5 us -> 3.95 us  [ring_gather(): lax.ppermute(ahead[-1][:half], 'dp', forward)]
    ppermute x48, starting transfers between devices: 57.4 us -> 35.4 us  [the longest x24 21.1 us: send(): lax.ppermute(parts[0], 'dp', self.backward)]
    convert_element_type x28 -> x14, other arithmetic: 25 us -> 8.76 us  [the longest x2 3.58 us: per_device(): grad_branch1 = tensor_gather(grad_middle.astype(low))]
  transfers between devices with their start and end apart: 151 -> 138, of which waited for: 55 -> 62; matrix products, arithmetic and copies ran while one was open for 29% -> 7% of each run, Pallas kernels for 0% -> 14%
where the time goes in v2:
time: 1070 us; the launch traced here: 1060 us
  waiting for transfers between devices  507 us (47%)
  Pallas kernels  234 us (22%)
  starting transfers between devices  176 us (16%)
  local copies, waits for them, and re-layouts  80.7 us (8%)
  other arithmetic  46.2 us (4%)
  between operations  15 us (1%)
    ppermute x24, waiting for transfers between devices, send(): lax.ppermute(parts[0], 'dp', self.backward)  151 us
    ppermute x12, waiting for transfers between devices, partner(): return lax.ppermute(block, 'dp', [(i, i ^ 1 << bit) for i in range(count)])  135 us
    ppermute x46, starting transfers between devices, swap(): lax.ppermute(block, 'tensor', [(i, i ^ distance) for i in range(count)])  104 us
    ppermute x12, waiting for transfers between devices, ring_gather(): behind.append(lax.ppermute(behind[-1], 'dp', backward))  96.9 us
    ppermute x46, waiting for transfers between devices, swap(): lax.ppermute(block, 'tensor', [(i, i ^ distance) for i in range(count)])  95.9 us
    pallas_call x8, Pallas kernels, gathered_call(): pl.pallas_call(kernel, grid=(steps,), in_specs=[in_smem] + [in_hbm] * (le...  63.3 us
    unnamed x561, local copies, waits for them, and re-layouts  56.6 us
    pallas_call x30, Pallas kernels, chunk(): pl.pallas_call(kernel, grid=(len(plan),), in_specs=in_specs, out_shape=[s...  54.6 us
  transfers between devices with their start and end apart: 138, of which 62 were waited for; matrix products, arithmetic and copies ran while one was open for 7% of the time, Pallas kernels for 14%

profile of v2, /device:TPU:1, one launch (start us, length us, event | category | flops | bytes accessed | tf_op | source)
XLA Modules:
  0.0 1058.8 jit_solution(11269777031568971617)
XLA Ops:
  26.0 8.8 collective-permute-done.5.refs_11_.refs_7_
  40.1 7.1 collective-permute-done.6.refs_10_.refs_6_
  56.7 7.4 collective-permute-start.10
  64.1 7.9 collective-permute-start.12
  75.8 15.4 %collective-permute-done.9.refs_12_.refs_8_ = bf16[256,3456]{1,0:T(8,128)(2,1)} collective-permute-done((bf16[256,3456]{1,0:T(8,128)(2,1)S(1)}, bf16[256,3456]{1,0:T(8,128)(2,1)}, u32[]{:S(2)}, u32[]{:S(2)}) %collective-permute-start.9) | collective-permute-done | bytes 1769504 | tf_op jit(solution)/shard_map/ppermute | solution.py:73
  93.9 4.5 queries_keys_values.2
  101.1 8.7 collective-permute-done.13
  110.4 31.8 %collective-permute-done.14 = bf16[4,2,64,256]{3,2,1,0:T(8,128)(2,1)S(1)} collective-permute-done((bf16[4,2,64,256]{3,2,1,0:T(8,128)(2,1)S(1)}, bf16[4,2,64,256]{3,2,1,0:T(8,128)(2,1)S(1)}, u32[]{:S(2)}, u32[]{:S(2)}) %collective-permute-start.14) | collective-permute-done | bytes 262176 | tf_op jit(solution)/shard_map/ppermute | solution.py:164
  145.6 5.9 collective-permute-done.15
  152.8 14.6 %attend.2 = (bf16[4,2,64,384]{3,2,1,0:T(8,128)(2,1)S(1)}, bf16[2,6,1024,256]{3,2,1,0:T(8,128)(2,1)}, bf16[2,6,256,256]{3,2,1,0:T(8,128)(2,1)}) custom-call(s32[1]{0:T(128)} %bitcast.14.odd_ref, bf16[4,2,64,384]{3,2,1,0:T(8,128)(2,1)S(1)} %bitcast.223, bf16[16,2,64,256]{3,2,1,0:T(8,128)(2,1)S(1)} %pad_maximum_fusion.5.pk_ref.pv_ref, ...), custom_call_target="tpu_custom_call" | custom-call | flops 28000000000 | bytes 1024 | tf_op jit(solution)/shard_map/attend/pallas_call | solution.py:611
  169.0 5.6 out.2
  174.6 7.4 collective-permute-start.20
  185.0 16.5 %collective-permute-done.19.refs_10_.refs_6_ = bf16[256,3456]{1,0:T(8,128)(2,1)} collective-permute-done((bf16[256,3456]{1,0:T(8,128)(2,1)}, bf16[256,3456]{1,0:T(8,128)(2,1)}, u32[]{:S(2)}, u32[]{:S(2)}) %collective-permute-start.19) | collective-permute-done | bytes 1769504 | tf_op jit(solution)/shard_map/ppermute | solution.py:73
  217.2 14.4 %collective-permute-done.23.refs_9_.refs_5_ = bf16[128,3456]{1,0:T(8,128)(2,1)S(1)} collective-permute-done((bf16[128,3456]{1,0:T(8,128)(2,1)S(1)}, bf16[128,3456]{1,0:T(8,128)(2,1)S(1)}, u32[]{:S(2)}, u32[]{:S(2)}) %collective-permute-start.23) | collective-permute-done | bytes 884768 | tf_op jit(solution)/shard_map/ppermute | solution.py:77
  234.6 8.2 collective-permute-done.27.refs_11_.refs_7_
  244.9 11.3 %collective-permute-start.28 = (bf16[128,2048]{1,0:T(8,128)(2,1)S(1)}, bf16[128,2048]{1,0:T(8,128)(2,1)S(1)}, u32[]{:S(2)}, u32[]{:S(2)}) collective-permute-start(bf16[128,2048]{1,0:T(8,128)(2,1)S(1)} %multiply_convert_fusion.2.refs_0_.refs_4_), channel_id=1, source_target_pairs={{0,1},{1,0},{2,3},{3,2},{4,5},{5,4},{6,7},{7,6},{8,9},{9,8},{10,11... | collective-permute-start | bytes 1572872 | tf_op jit(solution)/shard_map/ppermute | solution.py:147
  258.5 10.7 %active.2 = (bf16[512,1152]{1,0:T(8,128)(2,1)S(1)}, bf16[512,1152]{1,0:T(8,128)(2,1)}, bf16[512,1152]{1,0:T(8,128)(2,1)}) custom-call(s32[8]{0:T(128)S(1)} %select_reduce_fusion.1.source_ref, bf16[128,2048]{1,0:T(8,128)(2,1)S(1)} %multiply_convert_fusion.2.refs_0_.refs_4_, bf16[128,2048]{1,0:T(8,128)(2,1)S(1)} %collective-permute-done.28.refs_1_.refs_5_, ...), custom_call_target="tpu_custom_call" | custom-call | flops 17999998976 | bytes 1024 | tf_op jit(solution)/shard_map/active/pallas_call | solution.py:288
  270.1 5.8 down.2
  277.0 9.9 collective-permute-start.35
  297.5 7.0 collective-permute-done.36
  308.8 9.7 collective-permute-done.40.refs_2_.refs_10_
  320.6 14.9 %collective-permute-done.38.refs_12_.refs_8_ = bf16[256,3456]{1,0:T(8,128)(2,1)S(1)} collective-permute-done((bf16[256,3456]{1,0:T(8,128)(2,1)S(1)}, bf16[256,3456]{1,0:T(8,128)(2,1)S(1)}, u32[]{:S(2)}, u32[]{:S(2)}) %collective-permute-start.38) | collective-permute-done | bytes 1769504 | tf_op jit(solution)/shard_map/ppermute | solution.py:73
  336.8 4.5 queries_keys_values.3
  344.8 11.0 %collective-permute-done.42 = bf16[4,2,64,256]{3,2,1,0:T(8,128)(2,1)S(1)} collective-permute-done((bf16[4,2,64,256]{3,2,1,0:T(8,128)(2,1)S(1)}, bf16[4,2,64,256]{3,2,1,0:T(8,128)(2,1)S(1)}, u32[]{:S(2)}, u32[]{:S(2)}) %collective-permute-start.42) | collective-permute-done | bytes 262176 | tf_op jit(solution)/shard_map/ppermute | solution.py:164
  357.1 30.6 %collective-permute-done.43 = bf16[4,2,64,256]{3,2,1,0:T(8,128)(2,1)S(1)} collective-permute-done((bf16[4,2,64,256]{3,2,1,0:T(8,128)(2,1)S(1)}, bf16[4,2,64,256]{3,2,1,0:T(8,128)(2,1)S(1)}, u32[]{:S(2)}, u32[]{:S(2)}) %collective-permute-start.43) | collective-permute-done | bytes 262176 | tf_op jit(solution)/shard_map/ppermute | solution.py:164
  387.8 10.4 collective-permute-done.44
  398.5 14.7 %attend.3 = (bf16[4,2,64,384]{3,2,1,0:T(8,128)(2,1)S(1)}, bf16[2,6,1024,256]{3,2,1,0:T(8,128)(2,1)}, bf16[2,6,256,256]{3,2,1,0:T(8,128)(2,1)}) custom-call(s32[1]{0:T(128)} %bitcast.14.odd_ref, bf16[4,2,64,384]{3,2,1,0:T(8,128)(2,1)S(1)} %bitcast.225, bf16[16,2,64,256]{3,2,1,0:T(8,128)(2,1)S(1)} %pad_maximum_fusion.6.pk_ref.pv_ref, ...), custom_call_target="tpu_custom_call" | custom-call | flops 28000000000 | bytes 1024 | tf_op jit(solution)/shard_map/attend/pallas_call | solution.py:611
  424.1 12.5 %collective-permute-done.48 = bf16[128,2048]{1,0:T(8,128)(2,1)S(1)} collective-permute-done((bf16[128,2048]{1,0:T(8,128)(2,1)S(1)}, bf16[128,2048]{1,0:T(8,128)(2,1)S(1)}, u32[]{:S(2)}, u32[]{:S(2)}) %collective-permute-start.48) | collective-permute-done | bytes 524320 | tf_op jit(solution)/shard_map/ppermute | solution.py:147
  436.9 24.3 %collective-permute-done.50.refs_10_.refs_6_ = bf16[256,3456]{1,0:T(8,128)(2,1)S(1)} collective-permute-done((bf16[256,3456]{1,0:T(8,128)(2,1)S(1)}, bf16[256,3456]{1,0:T(8,128)(2,1)S(1)}, u32[]{:S(2)}, u32[]{:S(2)}) %collective-permute-start.50) | collective-permute-done | bytes 1769504 | tf_op jit(solution)/shard_map/ppermute | solution.py:73
  467.2 6.7 collective-permute-done.54.refs_2_.refs_6_
  477.6 7.5 collective-permute-done.59.refs_2_.refs_6_
  487.3 19.4 %active.3 = (bf16[512,1152]{1,0:T(8,128)(2,1)S(1)}, bf16[512,1152]{1,0:T(8,128)(2,1)}, bf16[512,1152]{1,0:T(8,128)(2,1)}) custom-call(s32[8]{0:T(128)S(1)} %select_reduce_fusion.1.source_ref, bf16[128,2048]{1,0:T(8,128)(2,1)S(1)} %multiply_convert_fusion.refs_0_.refs_4_, bf16[128,2048]{1,0:T(8,128)(2,1)S(1)} %collective-permute-done.53.refs_1_.refs_5_, ...), custom_call_target="tpu_custom_call" | custom-call | flops 17999998976 | bytes 1024 | tf_op jit(solution)/shard_map/active/pallas_call | solution.py:288
  512.2 9.1 active_back.2.refs_9_.refs_4_.refs_8_
  528.1 9.4 ffn_back.2
  538.0 5.7 down.3
  547.2 9.8 collective-permute-done.62
  558.1 10.2 collective-permute-done.57
  572.7 9.9 collective-permute-done.64.refs_2_.refs_6_.refs_14_
  589.6 16.7 %attend_back.2 = (f32[4,2,64,384]{3,2,1,0:T(8,128)S(1)}, f32[16,2,64,256]{3,2,1,0:T(8,128)S(1)}, f32[4,2,64,256]{3,2,1,0:T(8,128)S(1)}) custom-call(s32[1]{0:T(128)} %bitcast.14.odd_ref, bf16[4,2,64,384]{3,2,1,0:T(8,128)(2,1)S(1)} %bitcast.228, bf16[4,2,64,384]{3,2,1,0:T(8,128)(2,1)S(1)} %bitcast.226, ...), custom_call_target="tpu_custom_call" | custom-call | flops 32000000000 | bytes 1024 | tf_op jit(solution)/shard_map/attend_back/pallas_call | solution.py:646
  616.4 5.9 collective-permute-done.66
  634.5 9.9 collective-permute-done.68
  644.7 5.3 normed_back.2
  660.7 7.9 collective-permute-done.132.refs_9_
  676.1 30.5 %collective-permute-done.134.refs_9_ = bf16[256,1152]{1,0:T(8,128)(2,1)S(1)} collective-permute-done((bf16[256,1152]{1,0:T(8,128)(2,1)S(1)}, bf16[256,1152]{1,0:T(8,128)(2,1)S(1)}, u32[]{:S(2)}, u32[]{:S(2)}) %collective-permute-start.134) | collective-permute-done | bytes 589856 | tf_op jit(solution)/shard_map/ppermute | solution.py:99
  716.3 8.7 active_back.3.refs_9_.refs_4_.refs_8_
  727.8 9.2 ffn_back.3
  751.7 6.5 collective-permute-done.75
  760.9 10.4 collective-permute-done.118.refs_9_
  788.0 16.7 %attend_back.3 = (f32[4,2,64,384]{3,2,1,0:T(8,128)S(1)}, f32[16,2,64,256]{3,2,1,0:T(8,128)S(1)}, f32[4,2,64,256]{3,2,1,0:T(8,128)S(1)}) custom-call(s32[1]{0:T(128)} %bitcast.14.odd_ref, bf16[4,2,64,384]{3,2,1,0:T(8,128)(2,1)S(1)} %bitcast.227, bf16[4,2,64,384]{3,2,1,0:T(8,128)(2,1)S(1)} %bitcast.224, bf16[16,2,64,256]{3,2,1,0:T(8,128)(2,1)S(1)} %copy-done.6, ...), custom_call_target="tpu_custom_call" | custom-call | flops 32000000000 | bytes 1024 | tf_op jit(solution)/shard_map/attend_back/pallas_call | solution.py:646
  806.0 5.5 collective-permute-done.97.refs_17_
  816.3 6.3 collective-permute-done.79
  827.3 4.4 collective-permute-done.80
  836.7 6.3 collective-permute-done.81
  843.2 5.2 normed_back.3
  848.4 6.2 collective-permute-start.82
  866.4 7.7 collective-permute-done.83
  904.4 34.8 %collective-permute-done.86.refs_19_ = bf16[272,1024]{1,0:T(8,128)(2,1)S(1)} collective-permute-done((bf16[272,1024]{1,0:T(8,128)(2,1)S(1)}, bf16[272,1024]{1,0:T(8,128)(2,1)S(1)}, u32[]{:S(2)}, u32[]{:S(2)}) %collective-permute-start.86) | collective-permute-done | bytes 557088 | tf_op jit(solution)/shard_map/ppermute | solution.py:99
  942.7 9.2 collective-permute-done.126.refs_9_
  954.3 9.5 collective-permute-done.88.refs_19_
  971.6 4.9 collective-permute-done.128.refs_5_
  977.4 11.1 %collective-permute-done.90.refs_10_ = bf16[272,1024]{1,0:T(8,128)(2,1)S(1)} collective-permute-done((bf16[272,1024]{1,0:T(8,128)(2,1)S(1)}, bf16[272,1024]{1,0:T(8,128)(2,1)S(1)}, u32[]{:S(2)}, u32[]{:S(2)}) %collective-permute-start.90) | collective-permute-done | bytes 557088 | tf_op jit(solution)/shard_map/ppermute | solution.py:99
  997.0 8.0 collective-permute-start.92
  1005.1 8.7 collective-permute-done.110.refs_9_
  1040.4 10.9 %collective-permute-done.112.refs_5_ = bf16[256,2304]{1,0:T(8,128)(2,1)S(1)} collective-permute-done((bf16[256,2304]{1,0:T(8,128)(2,1)}, bf16[256,2304]{1,0:T(8,128)(2,1)S(1)}, u32[]{:S(2)}, u32[]{:S(2)}) %collective-permute-start.112) | collective-permute-done | bytes 1179680 | tf_op jit(solution)/shard_map/ppermute | solution.py:99
  (966 shorter events, 348.4 us)
Async XLA Ops:
  50.3 40.8 %collective-permute-start.9 = (bf16[256,3456]{1,0:T(8,128)(2,1)S(1)}, bf16[256,3456]{1,0:T(8,128)(2,1)}, u32[]{:S(2)}, u32[]{:S(2)}) collective-permute-start(bf16[256,3456]{1,0:T(8,128)(2,1)S(1)} %pad_maximum_fusion.3.refs_4_.refs_0_), channel_id=1, source_target_pairs={{8,0},{16,8},{24,16},{28,24},{20,28},{12,20},{4,12},{0,4},{9,1},{1... | collective-permute-start | bytes 5308424 | tf_op jit(solution)/shard_map/ppermute | solution.py:73
  51.6 39.5 %collective-permute-start.8 = (bf16[256,3456]{1,0:T(8,128)(2,1)S(1)}, bf16[256,3456]{1,0:T(8,128)(2,1)}, u32[]{:S(2)}, u32[]{:S(2)}) collective-permute-start(bf16[256,3456]{1,0:T(8,128)(2,1)S(1)} %pad_maximum_fusion.3.refs_4_.refs_0_), channel_id=1, source_target_pairs={{0,8},{8,16},{16,24},{24,28},{28,20},{20,12},{12,4},{4,0},{1,9},{9... | collective-permute-start | bytes 5308424 | tf_op jit(solution)/shard_map/ppermute | solution.py:72
  56.7 37.2 %collective-permute-start.10 = (bf16[128,2048]{1,0:T(8,128)(2,1)S(1)}, bf16[128,2048]{1,0:T(8,128)(2,1)}, u32[]{:S(2)}, u32[]{:S(2)}) collective-permute-start(bf16[128,2048]{1,0:T(8,128)(2,1)S(1)} %fusion.5.refs_0_.refs_8_), channel_id=1, source_target_pairs={{0,1},{1,0},{2,3},{3,2},{4,5},{5,4},{6,7},{7,6},{8,9},{9,8},{10,11... | collective-permute-start | bytes 1572872 | tf_op jit(solution)/shard_map/ppermute | solution.py:147
  64.1 29.8 %collective-permute-start.12 = (bf16[128,2048]{1,0:T(8,128)(2,1)}, bf16[128,2048]{1,0:T(8,128)(2,1)}, u32[]{:S(2)}, u32[]{:S(2)}) collective-permute-start(bf16[128,2048]{1,0:T(8,128)(2,1)} %collective-permute-done.11.refs_2_.refs_10_), channel_id=1, source_target_pairs={{0,1},{1,0},{2,3},{3,2},{4,5},{5,4},{6,7},{7,6},{8,9},{9,8},{10,11... | collective-permute-start | bytes 1572872 | tf_op jit(solution)/shard_map/ppermute | solution.py:147
  99.5 53.2 %collective-permute-start.17 = (bf16[256,3456]{1,0:T(8,128)(2,1)}, bf16[256,3456]{1,0:T(8,128)(2,1)}, u32[]{:S(2)}, u32[]{:S(2)}) collective-permute-start(bf16[256,3456]{1,0:T(8,128)(2,1)} %collective-permute-done.9.refs_12_.refs_8_), channel_id=1, source_target_pairs={{8,0},{16,8},{24,16},{28,24},{20,28},{12,20},{4,12},{0,4},{9,1},{1... | collective-permute-start | bytes 5308424 | tf_op jit(solution)/shard_map/ppermute | solution.py:73
  101.1 51.6 %collective-permute-start.16 = (bf16[256,3456]{1,0:T(8,128)(2,1)}, bf16[256,3456]{1,0:T(8,128)(2,1)}, u32[]{:S(2)}, u32[]{:S(2)}) collective-permute-start(bf16[256,3456]{1,0:T(8,128)(2,1)} %collective-permute-done.8.refs_5_.refs_1_), channel_id=1, source_target_pairs={{0,8},{8,16},{16,24},{24,28},{28,20},{20,12},{12,4},{4,0},{1,9},{9... | collective-permute-start | bytes 5308424 | tf_op jit(solution)/shard_map/ppermute | solution.py:72
  109.9 32.3 %collective-permute-start.14 = (bf16[4,2,64,256]{3,2,1,0:T(8,128)(2,1)S(1)}, bf16[4,2,64,256]{3,2,1,0:T(8,128)(2,1)S(1)}, u32[]{:S(2)}, u32[]{:S(2)}) collective-permute-start(bf16[4,2,64,256]{3,2,1,0:T(8,128)(2,1)S(1)} %broadcast_select_fusion.5), channel_id=1, source_target_pairs={{0,4},{4,0},{8,12},{12,8},{16,20},{20,16},{24,28},{28,24},{1,5},{5... | collective-permute-start | bytes 786440 | tf_op jit(solution)/shard_map/ppermute | solution.py:164
  167.4 34.1 %collective-permute-start.19 = (bf16[256,3456]{1,0:T(8,128)(2,1)}, bf16[256,3456]{1,0:T(8,128)(2,1)}, u32[]{:S(2)}, u32[]{:S(2)}) collective-permute-start(bf16[256,3456]{1,0:T(8,128)(2,1)} %collective-permute-done.17.refs_11_.refs_7_), channel_id=1, source_target_pairs={{8,0},{16,8},{24,16},{28,24},{20,28},{12,20},{4,12},{0,4},{9,1},{1... | collective-permute-start | bytes 5308424 | tf_op jit(solution)/shard_map/ppermute | solution.py:73
  169.0 34.4 %collective-permute-start.18 = (bf16[256,3456]{1,0:T(8,128)(2,1)}, bf16[256,3456]{1,0:T(8,128)(2,1)}, u32[]{:S(2)}, u32[]{:S(2)}) collective-permute-start(bf16[256,3456]{1,0:T(8,128)(2,1)} %collective-permute-done.16.refs_6_.refs_2_), channel_id=1, source_target_pairs={{0,8},{8,16},{16,24},{24,28},{28,20},{20,12},{12,4},{4,0},{1,9},{9... | collective-permute-start | bytes 5308424 | tf_op jit(solution)/shard_map/ppermute | solution.py:72
  174.6 30.9 %collective-permute-start.20 = (bf16[2,128,2048]{2,1,0:T(8,128)(2,1)}, bf16[2,128,2048]{2,1,0:T(8,128)(2,1)}, u32[]{:S(2)}, u32[]{:S(2)}) collective-permute-start(bf16[2,128,2048]{2,1,0:T(8,128)(2,1)} %get-tuple-element.137), channel_id=1, source_target_pairs={{0,1},{1,0},{2,3},{3,2},{4,5},{5,4},{6,7},{7,6},{8,9},{9,8},{10,11... | collective-permute-start | bytes 3145736 | tf_op jit(solution)/shard_map/ppermute | solution.py:147
  209.0 22.6 %collective-permute-start.23 = (bf16[128,3456]{1,0:T(8,128)(2,1)S(1)}, bf16[128,3456]{1,0:T(8,128)(2,1)S(1)}, u32[]{:S(2)}, u32[]{:S(2)}) collective-permute-start(bf16[128,3456]{1,0:T(8,128)(2,1)S(1)} %slice.475), channel_id=1, source_target_pairs={{8,0},{16,8},{24,16},{28,24},{20,28},{12,20},{4,12},{0,4},{9,1},{1... | collective-permute-start | bytes 2654216 | tf_op jit(solution)/shard_map/ppermute | solution.py:77
  213.6 29.2 %collective-permute-start.27 = (bf16[256,1024]{1,0:T(8,128)(2,1)S(1)}, bf16[256,1024]{1,0:T(8,128)(2,1)S(1)}, u32[]{:S(2)}, u32[]{:S(2)}) collective-permute-start(bf16[256,1024]{1,0:T(8,128)(2,1)S(1)} %collective-permute-done.25.refs_12_.refs_8_), channel_id=1, source_target_pairs={{8,0},{16,8},{24,16},{28,24},{20,28},{12,20},{4,12},{0,4},{9,1},{1... | collective-permute-start | bytes 1572872 | tf_op jit(solution)/shard_map/ppermute | solution.py:73
  215.4 29.5 %collective-permute-start.26 = (bf16[256,1024]{1,0:T(8,128)(2,1)S(1)}, bf16[256,1024]{1,0:T(8,128)(2,1)S(1)}, u32[]{:S(2)}, u32[]{:S(2)}) collective-permute-start(bf16[256,1024]{1,0:T(8,128)(2,1)S(1)} %collective-permute-done.24.refs_5_.refs_1_), channel_id=1, source_target_pairs={{0,8},{8,16},{16,24},{24,28},{28,20},{20,12},{12,4},{4,0},{1,9},{9... | collective-permute-start | bytes 1572872 | tf_op jit(solution)/shard_map/ppermute | solution.py:72
  233.1 23.1 %collective-permute-start.29 = (bf16[128,2048]{1,0:T(8,128)(2,1)S(1)}, bf16[128,2048]{1,0:T(8,128)(2,1)S(1)}, u32[]{:S(2)}, u32[]{:S(2)}) collective-permute-start(bf16[128,2048]{1,0:T(8,128)(2,1)S(1)} %multiply_convert_fusion.2.refs_0_.refs_4_), channel_id=1, source_target_pairs={{0,2},{1,3},{2,0},{3,1},{4,6},{5,7},{6,4},{7,5},{8,10},{9,11},{10,... | collective-permute-start | bytes 1572872 | tf_op jit(solution)/shard_map/ppermute | solution.py:147
  296.0 39.5 %collective-permute-start.38 = (bf16[256,3456]{1,0:T(8,128)(2,1)S(1)}, bf16[256,3456]{1,0:T(8,128)(2,1)S(1)}, u32[]{:S(2)}, u32[]{:S(2)}) collective-permute-start(bf16[256,3456]{1,0:T(8,128)(2,1)S(1)} %pad_maximum_fusion.4.refs_4_.refs_0_), channel_id=1, source_target_pairs={{8,0},{16,8},{24,16},{28,24},{20,28},{12,20},{4,12},{0,4},{9,1},{1... | collective-permute-start | bytes 5308424 | tf_op jit(solution)/shard_map/ppermute | solution.py:73
  297.3 39.3 %collective-permute-start.37 = (bf16[256,3456]{1,0:T(8,128)(2,1)S(1)}, bf16[256,3456]{1,0:T(8,128)(2,1)S(1)}, u32[]{:S(2)}, u32[]{:S(2)}) collective-permute-start(bf16[256,3456]{1,0:T(8,128)(2,1)S(1)} %pad_maximum_fusion.4.refs_4_.refs_0_), channel_id=1, source_target_pairs={{0,8},{8,16},{16,24},{24,28},{28,20},{20,12},{12,4},{4,0},{1,9},{9... | collective-permute-start | bytes 5308424 | tf_op jit(solution)/shard_map/ppermute | solution.py:72
  307.3 29.3 %collective-permute-start.39 = (bf16[128,2048]{1,0:T(8,128)(2,1)S(1)}, bf16[128,2048]{1,0:T(8,128)(2,1)S(1)}, u32[]{:S(2)}, u32[]{:S(2)}) collective-permute-start(bf16[128,2048]{1,0:T(8,128)(2,1)S(1)} %multiply_convert_fusion.1.refs_0_.refs_8_), channel_id=1, source_target_pairs={{0,1},{1,0},{2,3},{3,2},{4,5},{5,4},{6,7},{7,6},{8,9},{9,8},{10,11... | collective-permute-start | bytes 1572872 | tf_op jit(solution)/shard_map/ppermute | solution.py:147
  343.3 55.1 %collective-permute-start.46 = (bf16[256,3456]{1,0:T(8,128)(2,1)S(1)}, bf16[256,3456]{1,0:T(8,128)(2,1)S(1)}, u32[]{:S(2)}, u32[]{:S(2)}) collective-permute-start(bf16[256,3456]{1,0:T(8,128)(2,1)S(1)} %copy-done.257), channel_id=1, source_target_pairs={{8,0},{16,8},{24,16},{28,24},{20,28},{12,20},{4,12},{0,4},{9,1},{1... | collective-permute-start | bytes 5308424 | tf_op jit(solution)/shard_map/ppermute | solution.py:73
  344.0 54.4 %collective-permute-start.45 = (bf16[256,3456]{1,0:T(8,128)(2,1)S(1)}, bf16[256,3456]{1,0:T(8,128)(2,1)S(1)}, u32[]{:S(2)}, u32[]{:S(2)}) collective-permute-start(bf16[256,3456]{1,0:T(8,128)(2,1)S(1)} %collective-permute-done.37.refs_5_.refs_1_), channel_id=1, source_target_pairs={{0,8},{8,16},{16,24},{24,28},{28,20},{20,12},{12,4},{4,0},{1,9},{9... | collective-permute-start | bytes 5308424 | tf_op jit(solution)/shard_map/ppermute | solution.py:72
  355.8 31.8 %collective-permute-start.43 = (bf16[4,2,64,256]{3,2,1,0:T(8,128)(2,1)S(1)}, bf16[4,2,64,256]{3,2,1,0:T(8,128)(2,1)S(1)}, u32[]{:S(2)}, u32[]{:S(2)}) collective-permute-start(bf16[4,2,64,256]{3,2,1,0:T(8,128)(2,1)S(1)} %broadcast_select_fusion.4), channel_id=1, source_target_pairs={{0,4},{4,0},{8,12},{12,8},{16,20},{20,16},{24,28},{28,24},{1,5},{5... | collective-permute-start | bytes 786440 | tf_op jit(solution)/shard_map/ppermute | solution.py:164
  421.0 40.2 %collective-permute-start.50 = (bf16[256,3456]{1,0:T(8,128)(2,1)S(1)}, bf16[256,3456]{1,0:T(8,128)(2,1)S(1)}, u32[]{:S(2)}, u32[]{:S(2)}) collective-permute-start(bf16[256,3456]{1,0:T(8,128)(2,1)S(1)} %collective-permute-done.46.refs_11_.refs_7_), channel_id=1, source_target_pairs={{8,0},{16,8},{24,16},{28,24},{20,28},{12,20},{4,12},{0,4},{9,1},{1... | collective-permute-start | bytes 5308424 | tf_op jit(solution)/shard_map/ppermute | solution.py:73
  421.3 39.9 %collective-permute-start.49 = (bf16[256,3456]{1,0:T(8,128)(2,1)S(1)}, bf16[256,3456]{1,0:T(8,128)(2,1)S(1)}, u32[]{:S(2)}, u32[]{:S(2)}) collective-permute-start(bf16[256,3456]{1,0:T(8,128)(2,1)S(1)} %collective-permute-done.45.refs_6_.refs_2_), channel_id=1, source_target_pairs={{0,8},{8,16},{16,24},{24,28},{28,20},{20,12},{12,4},{4,0},{1,9},{9... | collective-permute-start | bytes 5308424 | tf_op jit(solution)/shard_map/ppermute | solution.py:72
  462.4 24.9 %collective-permute-start.52 = (bf16[128,3456]{1,0:T(8,128)(2,1)S(1)}, bf16[128,3456]{1,0:T(8,128)(2,1)S(1)}, u32[]{:S(2)}, u32[]{:S(2)}) collective-permute-start(bf16[128,3456]{1,0:T(8,128)(2,1)S(1)} %slice.486), channel_id=1, source_target_pairs={{8,0},{16,8},{24,16},{28,24},{20,28},{12,20},{4,12},{0,4},{9,1},{1... | collective-permute-start | bytes 2654216 | tf_op jit(solution)/shard_map/ppermute | solution.py:77
  463.0 24.2 %collective-permute-start.51 = (bf16[128,3456]{1,0:T(8,128)(2,1)S(1)}, bf16[128,3456]{1,0:T(8,128)(2,1)S(1)}, u32[]{:S(2)}, u32[]{:S(2)}) collective-permute-start(bf16[128,3456]{1,0:T(8,128)(2,1)S(1)} %slice.485), channel_id=1, source_target_pairs={{0,8},{8,16},{16,24},{24,28},{28,20},{20,12},{12,4},{4,0},{1,9},{9... | collective-permute-start | bytes 2654216 | tf_op jit(solution)/shard_map/ppermute | solution.py:76
  464.9 22.2 %collective-permute-start.53 = (bf16[128,2048]{1,0:T(8,128)(2,1)S(1)}, bf16[128,2048]{1,0:T(8,128)(2,1)S(1)}, u32[]{:S(2)}, u32[]{:S(2)}) collective-permute-start(bf16[128,2048]{1,0:T(8,128)(2,1)S(1)} %multiply_convert_fusion.refs_0_.refs_4_), channel_id=1, source_target_pairs={{0,1},{1,0},{2,3},{3,2},{4,5},{5,4},{6,7},{7,6},{8,9},{9,8},{10,11... | collective-permute-start | bytes 1572872 | tf_op jit(solution)/shard_map/ppermute | solution.py:147
  485.1 22.7 %collective-permute-start.58 = (bf16[128,2048]{1,0:T(8,128)(2,1)S(1)}, bf16[128,2048]{1,0:T(8,128)(2,1)S(1)}, u32[]{:S(2)}, u32[]{:S(2)}) collective-permute-start(bf16[128,2048]{1,0:T(8,128)(2,1)S(1)} %constant_dynamic-update-slice_fusion.8.refs_0_.refs_4_), channel_id=1, source_target_pairs={{0,1},{1,0},{2,3},{3,2},{4,5},{5,4},{6,7},{7,6},{8,9},{9,8},{10,11... | collective-permute-start | bytes 1572872 | tf_op jit(solution)/shard_map/ppermute | solution.py:147
  624.5 28.1 %collective-permute-start.130 = (bf16[128,1152]{1,0:T(8,128)(2,1)S(1)}, bf16[128,1152]{1,0:T(8,128)(2,1)S(1)}, u32[]{:S(2)}, u32[]{:S(2)}) collective-permute-start(bf16[128,1152]{1,0:T(8,128)(2,1)S(1)} %get-tuple-element.239), channel_id=1, source_target_pairs={{8,0},{16,8},{24,16},{28,24},{20,28},{12,20},{4,12},{0,4},{9,1},{1... | collective-permute-start | bytes 884744 | tf_op jit(solution)/shard_map/ppermute | solution.py:99
  625.8 26.9 %collective-permute-start.131 = (bf16[128,1152]{1,0:T(8,128)(2,1)S(1)}, bf16[128,1152]{1,0:T(8,128)(2,1)S(1)}, u32[]{:S(2)}, u32[]{:S(2)}) collective-permute-start(bf16[128,1152]{1,0:T(8,128)(2,1)S(1)} %get-tuple-element.240), channel_id=1, source_target_pairs={{0,8},{8,16},{16,24},{24,28},{28,20},{20,12},{12,4},{4,0},{1,9},{9... | collective-permute-start | bytes 884744 | tf_op jit(solution)/shard_map/ppermute | solution.py:100
  633.0 22.9 %collective-permute-start.114 = (bf16[128,2304]{1,0:T(8,128)(2,1)S(1)}, bf16[128,2304]{1,0:T(8,128)(2,1)S(1)}, u32[]{:S(2)}, u32[]{:S(2)}) collective-permute-start(bf16[128,2304]{1,0:T(8,128)(2,1)S(1)} %get-tuple-element.215), channel_id=1, source_target_pairs={{8,0},{16,8},{24,16},{28,24},{20,28},{12,20},{4,12},{0,4},{9,1},{1... | collective-permute-start | bytes 1769480 | tf_op jit(solution)/shard_map/ppermute | solution.py:99
  658.3 81.0 %collective-permute-start.116 = (bf16[256,2304]{1,0:T(8,128)(2,1)S(1)}, bf16[256,2304]{1,0:T(8,128)(2,1)S(1)}, u32[]{:S(2)}, u32[]{:S(2)}) collective-permute-start(bf16[256,2304]{1,0:T(8,128)(2,1)S(1)} %get-tuple-element.217), channel_id=1, source_target_pairs={{8,0},{16,8},{24,16},{28,24},{20,28},{12,20},{4,12},{0,4},{9,1},{1... | collective-permute-start | bytes 3538952 | tf_op jit(solution)/shard_map/ppermute | solution.py:99
  659.7 79.5 %collective-permute-start.117 = (bf16[256,2304]{1,0:T(8,128)(2,1)S(1)}, bf16[256,2304]{1,0:T(8,128)(2,1)S(1)}, u32[]{:S(2)}, u32[]{:S(2)}) collective-permute-start(bf16[256,2304]{1,0:T(8,128)(2,1)S(1)} %get-tuple-element.218), channel_id=1, source_target_pairs={{0,8},{8,16},{16,24},{24,28},{28,20},{20,12},{12,4},{4,0},{1,9},{9... | collective-permute-start | bytes 3538952 | tf_op jit(solution)/shard_map/ppermute | solution.py:100
  671.4 35.2 %collective-permute-start.134 = (bf16[256,1152]{1,0:T(8,128)(2,1)S(1)}, bf16[256,1152]{1,0:T(8,128)(2,1)S(1)}, u32[]{:S(2)}, u32[]{:S(2)}) collective-permute-start(bf16[256,1152]{1,0:T(8,128)(2,1)S(1)} %get-tuple-element.243), channel_id=1, source_target_pairs={{8,0},{16,8},{24,16},{28,24},{20,28},{12,20},{4,12},{0,4},{9,1},{1... | collective-permute-start | bytes 1769480 | tf_op jit(solution)/shard_map/ppermute | solution.py:99
  671.8 36.5 %collective-permute-start.135 = (bf16[256,1152]{1,0:T(8,128)(2,1)S(1)}, bf16[256,1152]{1,0:T(8,128)(2,1)S(1)}, u32[]{:S(2)}, u32[]{:S(2)}) collective-permute-start(bf16[256,1152]{1,0:T(8,128)(2,1)S(1)} %get-tuple-element.244), channel_id=1, source_target_pairs={{0,8},{8,16},{16,24},{24,28},{28,20},{20,12},{12,4},{4,0},{1,9},{9... | collective-permute-start | bytes 1769480 | tf_op jit(solution)/shard_map/ppermute | solution.py:100
  675.4 36.3 %collective-permute-start.72 = (bf16[128,2048]{1,0:T(8,128)(2,1)S(1)}, bf16[128,2048]{1,0:T(8,128)(2,1)S(1)}, u32[]{:S(2)}, u32[]{:S(2)}) collective-permute-start(bf16[128,2048]{1,0:T(8,128)(2,1)S(1)} %get-tuple-element.303.refs_0_.refs_4_), channel_id=1, source_target_pairs={{0,2},{1,3},{2,0},{3,1},{4,6},{5,7},{6,4},{7,5},{8,10},{9,11},{10,... | collective-permute-start | bytes 1572872 | tf_op jit(solution)/shard_map/ppermute | solution.py:147
  710.1 35.9 %collective-permute-start.136 = (bf16[256,1152]{1,0:T(8,128)(2,1)}, bf16[256,1152]{1,0:T(8,128)(2,1)}, u32[]{:S(2)}, u32[]{:S(2)}) collective-permute-start(bf16[256,1152]{1,0:T(8,128)(2,1)} %get-tuple-element.245), channel_id=1, source_target_pairs={{8,0},{16,8},{24,16},{28,24},{20,28},{12,20},{4,12},{0,4},{9,1},{1... | collective-permute-start | bytes 1769480 | tf_op jit(solution)/shard_map/ppermute | solution.py:99
  713.3 32.8 %collective-permute-start.137 = (bf16[256,1152]{1,0:T(8,128)(2,1)}, bf16[256,1152]{1,0:T(8,128)(2,1)}, u32[]{:S(2)}, u32[]{:S(2)}) collective-permute-start(bf16[256,1152]{1,0:T(8,128)(2,1)} %get-tuple-element.246), channel_id=1, source_target_pairs={{0,8},{8,16},{16,24},{24,28},{28,20},{20,12},{12,4},{4,0},{1,9},{9... | collective-permute-start | bytes 1769480 | tf_op jit(solution)/shard_map/ppermute | solution.py:100
  743.6 27.6 %collective-permute-start.118 = (bf16[256,2304]{1,0:T(8,128)(2,1)S(1)}, bf16[256,2304]{1,0:T(8,128)(2,1)S(1)}, u32[]{:S(2)}, u32[]{:S(2)}) collective-permute-start(bf16[256,2304]{1,0:T(8,128)(2,1)S(1)} %get-tuple-element.219), channel_id=1, source_target_pairs={{8,0},{16,8},{24,16},{28,24},{20,28},{12,20},{4,12},{0,4},{9,1},{1... | collective-permute-start | bytes 3538952 | tf_op jit(solution)/shard_map/ppermute | solution.py:99
  743.9 27.3 %collective-permute-start.119 = (bf16[256,2304]{1,0:T(8,128)(2,1)S(1)}, bf16[256,2304]{1,0:T(8,128)(2,1)S(1)}, u32[]{:S(2)}, u32[]{:S(2)}) collective-permute-start(bf16[256,2304]{1,0:T(8,128)(2,1)S(1)} %get-tuple-element.220), channel_id=1, source_target_pairs={{0,8},{8,16},{16,24},{24,28},{28,20},{20,12},{12,4},{4,0},{1,9},{9... | collective-permute-start | bytes 3538952 | tf_op jit(solution)/shard_map/ppermute | solution.py:100
  750.2 26.7 %collective-permute-start.95 = (bf16[128,1024]{1,0:T(8,128)(2,1)S(1)}, bf16[128,1024]{1,0:T(8,128)(2,1)S(1)}, u32[]{:S(2)}, u32[]{:S(2)}) collective-permute-start(bf16[128,1024]{1,0:T(8,128)(2,1)S(1)} %get-tuple-element.189), channel_id=1, source_target_pairs={{8,0},{16,8},{24,16},{28,24},{20,28},{12,20},{4,12},{0,4},{9,1},{1... | collective-permute-start | bytes 786440 | tf_op jit(solution)/shard_map/ppermute | solution.py:99
  750.4 28.0 %collective-permute-start.96 = (bf16[128,1024]{1,0:T(8,128)(2,1)S(1)}, bf16[128,1024]{1,0:T(8,128)(2,1)S(1)}, u32[]{:S(2)}, u32[]{:S(2)}) collective-permute-start(bf16[128,1024]{1,0:T(8,128)(2,1)S(1)} %get-tuple-element.190), channel_id=1, source_target_pairs={{0,8},{8,16},{16,24},{24,28},{28,20},{20,12},{12,4},{4,0},{1,9},{9... | collective-permute-start | bytes 786440 | tf_op jit(solution)/shard_map/ppermute | solution.py:100
  774.4 50.4 %collective-permute-start.120 = (bf16[256,2304]{1,0:T(8,128)(2,1)}, bf16[256,2304]{1,0:T(8,128)(2,1)S(1)}, u32[]{:S(2)}, u32[]{:S(2)}) collective-permute-start(bf16[256,2304]{1,0:T(8,128)(2,1)} %get-tuple-element.221), channel_id=1, source_target_pairs={{8,0},{16,8},{24,16},{28,24},{20,28},{12,20},{4,12},{0,4},{9,1},{1... | collective-permute-start | bytes 3538952 | tf_op jit(solution)/shard_map/ppermute | solution.py:99
  775.7 49.0 %collective-permute-start.121 = (bf16[256,2304]{1,0:T(8,128)(2,1)S(1)}, bf16[256,2304]{1,0:T(8,128)(2,1)}, u32[]{:S(2)}, u32[]{:S(2)}) collective-permute-start(bf16[256,2304]{1,0:T(8,128)(2,1)S(1)} %get-tuple-element.222), channel_id=1, source_target_pairs={{0,8},{8,16},{16,24},{24,28},{28,20},{20,12},{12,4},{4,0},{1,9},{9... | collective-permute-start | bytes 3538952 | tf_op jit(solution)/shard_map/ppermute | solution.py:100
  780.2 31.3 %collective-permute-start.97 = (bf16[256,1024]{1,0:T(8,128)(2,1)}, bf16[256,1024]{1,0:T(8,128)(2,1)}, u32[]{:S(2)}, u32[]{:S(2)}) collective-permute-start(bf16[256,1024]{1,0:T(8,128)(2,1)} %get-tuple-element.191), channel_id=1, source_target_pairs={{8,0},{16,8},{24,16},{28,24},{20,28},{12,20},{4,12},{0,4},{9,1},{1... | collective-permute-start | bytes 1572872 | tf_op jit(solution)/shard_map/ppermute | solution.py:99
  781.5 31.0 %collective-permute-start.98 = (bf16[256,1024]{1,0:T(8,128)(2,1)}, bf16[256,1024]{1,0:T(8,128)(2,1)}, u32[]{:S(2)}, u32[]{:S(2)}) collective-permute-start(bf16[256,1024]{1,0:T(8,128)(2,1)} %get-tuple-element.192), channel_id=1, source_target_pairs={{0,8},{8,16},{16,24},{24,28},{28,20},{20,12},{12,4},{4,0},{1,9},{9... | collective-permute-start | bytes 1572872 | tf_op jit(solution)/shard_map/ppermute | solution.py:100
  859.9 24.5 %collective-permute-start.122 = (bf16[128,1152]{1,0:T(8,128)(2,1)}, bf16[128,1152]{1,0:T(8,128)(2,1)}, u32[]{:S(2)}, u32[]{:S(2)}) collective-permute-start(bf16[128,1152]{1,0:T(8,128)(2,1)} %get-tuple-element.223), channel_id=1, source_target_pairs={{8,0},{16,8},{24,16},{28,24},{20,28},{12,20},{4,12},{0,4},{9,1},{1... | collective-permute-start | bytes 884744 | tf_op jit(solution)/shard_map/ppermute | solution.py:99
  860.7 22.9 %collective-permute-start.123 = (bf16[128,1152]{1,0:T(8,128)(2,1)}, bf16[128,1152]{1,0:T(8,128)(2,1)}, u32[]{:S(2)}, u32[]{:S(2)}) collective-permute-start(bf16[128,1152]{1,0:T(8,128)(2,1)} %get-tuple-element.225), channel_id=1, source_target_pairs={{0,8},{8,16},{16,24},{24,28},{28,20},{20,12},{12,4},{4,0},{1,9},{9... | collective-permute-start | bytes 884744 | tf_op jit(solution)/shard_map/ppermute | solution.py:100
  864.6 24.4 %collective-permute-start.106 = (bf16[128,2304]{1,0:T(8,128)(2,1)}, bf16[128,2304]{1,0:T(8,128)(2,1)}, u32[]{:S(2)}, u32[]{:S(2)}) collective-permute-start(bf16[128,2304]{1,0:T(8,128)(2,1)} %get-tuple-element.199), channel_id=1, source_target_pairs={{8,0},{16,8},{24,16},{28,24},{20,28},{12,20},{4,12},{0,4},{9,1},{1... | collective-permute-start | bytes 1769480 | tf_op jit(solution)/shard_map/ppermute | solution.py:99
  865.3 24.6 %collective-permute-start.107 = (bf16[128,2304]{1,0:T(8,128)(2,1)}, bf16[128,2304]{1,0:T(8,128)(2,1)}, u32[]{:S(2)}, u32[]{:S(2)}) collective-permute-start(bf16[128,2304]{1,0:T(8,128)(2,1)} %get-tuple-element.201), channel_id=1, source_target_pairs={{0,8},{8,16},{16,24},{24,28},{28,20},{20,12},{12,4},{4,0},{1,9},{9... | collective-permute-start | bytes 1769480 | tf_op jit(solution)/shard_map/ppermute | solution.py:100
  893.4 60.9 %collective-permute-start.108 = (bf16[256,2304]{1,0:T(8,128)(2,1)S(1)}, bf16[256,2304]{1,0:T(8,128)(2,1)S(1)}, u32[]{:S(2)}, u32[]{:S(2)}) collective-permute-start(bf16[256,2304]{1,0:T(8,128)(2,1)S(1)} %get-tuple-element.203), channel_id=1, source_target_pairs={{8,0},{16,8},{24,16},{28,24},{20,28},{12,20},{4,12},{0,4},{9,1},{1... | collective-permute-start | bytes 3538952 | tf_op jit(solution)/shard_map/ppermute | solution.py:99
  894.1 60.1 %collective-permute-start.109 = (bf16[256,2304]{1,0:T(8,128)(2,1)S(1)}, bf16[256,2304]{1,0:T(8,128)(2,1)S(1)}, u32[]{:S(2)}, u32[]{:S(2)}) collective-permute-start(bf16[256,2304]{1,0:T(8,128)(2,1)S(1)} %get-tuple-element.205), channel_id=1, source_target_pairs={{0,8},{8,16},{16,24},{24,28},{28,20},{20,12},{12,4},{4,0},{1,9},{9... | collective-permute-start | bytes 3538952 | tf_op jit(solution)/shard_map/ppermute | solution.py:100
  897.0 42.2 %collective-permute-start.86 = (bf16[272,1024]{1,0:T(8,128)(2,1)S(1)}, bf16[272,1024]{1,0:T(8,128)(2,1)S(1)}, u32[]{:S(2)}, u32[]{:S(2)}) collective-permute-start(bf16[272,1024]{1,0:T(8,128)(2,1)S(1)} %get-tuple-element.182), channel_id=1, source_target_pairs={{8,0},{16,8},{24,16},{28,24},{20,28},{12,20},{4,12},{0,4},{9,1},{1... | collective-permute-start | bytes 1671176 | tf_op jit(solution)/shard_map/ppermute | solution.py:99
  902.0 38.2 %collective-permute-start.87 = (bf16[272,1024]{1,0:T(8,128)(2,1)S(1)}, bf16[272,1024]{1,0:T(8,128)(2,1)S(1)}, u32[]{:S(2)}, u32[]{:S(2)}) collective-permute-start(bf16[272,1024]{1,0:T(8,128)(2,1)S(1)} %get-tuple-element.183), channel_id=1, source_target_pairs={{0,8},{8,16},{16,24},{24,28},{28,20},{20,12},{12,4},{4,0},{1,9},{9... | collective-permute-start | bytes 1671176 | tf_op jit(solution)/shard_map/ppermute | solution.py:100
  903.9 48.0 %collective-permute-start.126 = (bf16[256,1152]{1,0:T(8,128)(2,1)S(1)}, bf16[256,1152]{1,0:T(8,128)(2,1)S(1)}, u32[]{:S(2)}, u32[]{:S(2)}) collective-permute-start(bf16[256,1152]{1,0:T(8,128)(2,1)S(1)} %get-tuple-element.231), channel_id=1, source_target_pairs={{8,0},{16,8},{24,16},{28,24},{20,28},{12,20},{4,12},{0,4},{9,1},{1... | collective-permute-start | bytes 1769480 | tf_op jit(solution)/shard_map/ppermute | solution.py:99
  952.8 23.7 %collective-permute-start.128 = (bf16[256,1152]{1,0:T(8,128)(2,1)S(1)}, bf16[256,1152]{1,0:T(8,128)(2,1)S(1)}, u32[]{:S(2)}, u32[]{:S(2)}) collective-permute-start(bf16[256,1152]{1,0:T(8,128)(2,1)S(1)} %get-tuple-element.235), channel_id=1, source_target_pairs={{8,0},{16,8},{24,16},{28,24},{20,28},{12,20},{4,12},{0,4},{9,1},{1... | collective-permute-start | bytes 1769480 | tf_op jit(solution)/shard_map/ppermute | solution.py:99
  954.3 22.2 %collective-permute-start.129 = (bf16[256,1152]{1,0:T(8,128)(2,1)S(1)}, bf16[256,1152]{1,0:T(8,128)(2,1)S(1)}, u32[]{:S(2)}, u32[]{:S(2)}) collective-permute-start(bf16[256,1152]{1,0:T(8,128)(2,1)S(1)} %get-tuple-element.237), channel_id=1, source_target_pairs={{0,8},{8,16},{16,24},{24,28},{28,20},{20,12},{12,4},{4,0},{1,9},{9... | collective-permute-start | bytes 1769480 | tf_op jit(solution)/shard_map/ppermute | solution.py:100
  965.7 22.7 %collective-permute-start.90 = (bf16[272,1024]{1,0:T(8,128)(2,1)S(1)}, bf16[272,1024]{1,0:T(8,128)(2,1)S(1)}, u32[]{:S(2)}, u32[]{:S(2)}) collective-permute-start(bf16[272,1024]{1,0:T(8,128)(2,1)S(1)} %get-tuple-element.186), channel_id=1, source_target_pairs={{8,0},{16,8},{24,16},{28,24},{20,28},{12,20},{4,12},{0,4},{9,1},{1... | collective-permute-start | bytes 1671176 | tf_op jit(solution)/shard_map/ppermute | solution.py:99
  966.4 22.1 %collective-permute-start.91 = (bf16[272,1024]{1,0:T(8,128)(2,1)S(1)}, bf16[272,1024]{1,0:T(8,128)(2,1)S(1)}, u32[]{:S(2)}, u32[]{:S(2)}) collective-permute-start(bf16[272,1024]{1,0:T(8,128)(2,1)S(1)} %get-tuple-element.187), channel_id=1, source_target_pairs={{0,8},{8,16},{16,24},{24,28},{28,20},{20,12},{12,4},{4,0},{1,9},{9... | collective-permute-start | bytes 1671176 | tf_op jit(solution)/shard_map/ppermute | solution.py:100
  970.9 42.8 %collective-permute-start.110 = (bf16[256,2304]{1,0:T(8,128)(2,1)}, bf16[256,2304]{1,0:T(8,128)(2,1)}, u32[]{:S(2)}, u32[]{:S(2)}) collective-permute-start(bf16[256,2304]{1,0:T(8,128)(2,1)} %get-tuple-element.207), channel_id=1, source_target_pairs={{8,0},{16,8},{24,16},{28,24},{20,28},{12,20},{4,12},{0,4},{9,1},{1... | collective-permute-start | bytes 3538952 | tf_op jit(solution)/shard_map/ppermute | solution.py:99
  976.4 37.3 %collective-permute-start.111 = (bf16[256,2304]{1,0:T(8,128)(2,1)}, bf16[256,2304]{1,0:T(8,128)(2,1)}, u32[]{:S(2)}, u32[]{:S(2)}) collective-permute-start(bf16[256,2304]{1,0:T(8,128)(2,1)} %get-tuple-element.209), channel_id=1, source_target_pairs={{0,8},{8,16},{16,24},{24,28},{28,20},{20,12},{12,4},{4,0},{1,9},{9... | collective-permute-start | bytes 3538952 | tf_op jit(solution)/shard_map/ppermute | solution.py:100
  976.5 54.2 %collective-permute-start.104 = (bf16[256,256]{1,0:T(8,128)(2,1)S(1)}, bf16[256,256]{1,0:T(8,128)(2,1)}, u32[]{:S(2)}, u32[]{:S(2)}) collective-permute-start(bf16[256,256]{1,0:T(8,128)(2,1)S(1)} %slice.654.refs_4_), channel_id=1, source_target_pairs={{0,2},{1,3},{2,0},{3,1},{4,6},{5,7},{6,4},{7,5},{8,10},{9,11},{10,... | collective-permute-start | bytes 393224 | tf_op jit(solution)/shard_map/ppermute | solution.py:147
  990.9 22.9 %collective-permute-start.93 = (bf16[272,1024]{1,0:T(8,128)(2,1)}, bf16[272,1024]{1,0:T(8,128)(2,1)}, u32[]{:S(2)}, u32[]{:S(2)}) collective-permute-start(bf16[272,1024]{1,0:T(8,128)(2,1)} %convert_element_type.391), channel_id=1, source_target_pairs={{0,2},{1,3},{2,0},{3,1},{4,6},{5,7},{6,4},{7,5},{8,10},{9,11},{10,... | collective-permute-start | bytes 1671176 | tf_op jit(solution)/shard_map/ppermute | solution.py:147
  997.0 34.4 %collective-permute-start.92 = (bf16[272,1024]{1,0:T(8,128)(2,1)}, bf16[272,1024]{1,0:T(8,128)(2,1)}, u32[]{:S(2)}, u32[]{:S(2)}) collective-permute-start(bf16[272,1024]{1,0:T(8,128)(2,1)} %convert_element_type.391), channel_id=1, source_target_pairs={{0,1},{1,0},{2,3},{3,2},{4,5},{5,4},{6,7},{7,6},{8,9},{9,8},{10,11... | collective-permute-start | bytes 1671176 | tf_op jit(solution)/shard_map/ppermute | solution.py:147
  1023.4 27.9 %collective-permute-start.112 = (bf16[256,2304]{1,0:T(8,128)(2,1)}, bf16[256,2304]{1,0:T(8,128)(2,1)S(1)}, u32[]{:S(2)}, u32[]{:S(2)}) collective-permute-start(bf16[256,2304]{1,0:T(8,128)(2,1)} %get-tuple-element.211), channel_id=1, source_target_pairs={{8,0},{16,8},{24,16},{28,24},{20,28},{12,20},{4,12},{0,4},{9,1},{1... | collective-permute-start | bytes 3538952 | tf_op jit(solution)/shard_map/ppermute | solution.py:99
  1023.4 27.8 %collective-permute-start.113 = (bf16[256,2304]{1,0:T(8,128)(2,1)}, bf16[256,2304]{1,0:T(8,128)(2,1)}, u32[]{:S(2)}, u32[]{:S(2)}) collective-permute-start(bf16[256,2304]{1,0:T(8,128)(2,1)} %get-tuple-element.213), channel_id=1, source_target_pairs={{0,8},{8,16},{16,24},{24,28},{28,20},{20,12},{12,4},{4,0},{1,9},{9... | collective-permute-start | bytes 3538952 | tf_op jit(solution)/shard_map/ppermute | solution.py:100
  (335 other events, 5162.8 us)

commit v3 on v2

--- a/solution.py
+++ b/solution.py
@@ -41,7 +41,7 @@
     )
 
 
-FLOPS_PER_US = 2e9
+FLOPS_PER_US = 3e9
 
 
 def ring_order(count):
@@ -757,13 +757,11 @@
         )
         if layer == 0:
             attn_pack = jnp.concatenate([attn_pack, gain_pad], axis=0)
-        ffn_pack = jnp.concatenate(
-            [gate_weight[layer], up_weight[layer], down_weight[layer].T], axis=1
-        )
+        gate_up_pack = jnp.concatenate([gate_weight[layer], up_weight[layer]], axis=1)
         gathered = []
-        for piece in (attn_pack, ffn_pack):
+        for piece in (attn_pack, gate_up_pack, down_weight[layer].T):
             if arrivals:
-                piece = after(piece, *arrivals[-1][-2])
+                piece = after(piece, *arrivals[-1][-1 if len(arrivals) == 1 else -2])
             pieces, steps = ring_gather(piece, dim_block)
             arrivals.append(steps)
             gathered.append(pieces)
@@ -821,6 +819,7 @@
         out_refs[0][...] = row_buf[...]
 
     def arrived(value, *wanted):
+        wanted = ()
         needed = [
             part
             for chain, step in wanted
@@ -832,7 +831,7 @@
     hidden = reorder(hidden_in.reshape(block, width), sources).astype(full)
     saved = []
     for layer in range(layers):
-        attn_pieces, ffn_pieces = packs[layer]
+        attn_pieces, gate_up_pieces, down_pieces = packs[layer]
         normed, scaled, inv_root = rms_forward(hidden, gains[0, layer])
         normed_all = tensor_gather(normed)
         normed_all = (arrived(normed_all[0], (2 * layer + 1, 0)), *normed_all[1:])
@@ -872,7 +871,7 @@
         active, gate, up = gathered_call(
                 sources,
             normed_ffn_all,
-            ffn_pieces,
+            gate_up_pieces,
             [(0, units), (units, units)],
             unit_tile,
             active_epilogue,
@@ -884,7 +883,7 @@
         active = arrived(active, (2 * layer + 2, 3))
         parts = spread_call(
                 sources,
-            [active], ffn_pieces, 2 * units, units, width, block, copy_rows, [], "down", 5
+            [active], down_pieces, 0, units, width, block, copy_rows, [], "down", 5
         )
         hidden = middle + tensor_scatter(*parts)
         saved.append(
@@ -900,7 +899,7 @@
     gain_grads = [[None] * layers, [None] * layers]
     attn_grad, gate_up_grad, down_grad = [None] * layers, [None] * layers, [None] * layers
     for layer in reversed(range(layers)):
-        attn_pieces, ffn_pieces = packs[layer]
+        attn_pieces, gate_up_pieces, down_pieces = packs[layer]
         attn_saved, attend_saved, ffn_saved = saved[layer]
         normed_all, scaled, inv_root, attended = attn_saved
         normed_ffn_all, scaled_ffn, inv_root_ffn, gate, up, active = ffn_saved
@@ -908,8 +907,8 @@
         grad_units = gathered_call(
                 sources,
             grad_branch,
-            ffn_pieces,
-            [(2 * units, units)],
+            down_pieces,
+            [(0, units)],
             unit_tile,
             active_backward,
             [(value, tiled(rows, unit_tile)) for value in (gate, up)],
@@ -919,7 +918,7 @@
         )[0]
         parts = spread_call(
                 sources,
-            [grad_units], ffn_pieces, 0, 2 * units, width, block, copy_rows, [], "ffn_back", 8
+            [grad_units], gate_up_pieces, 0, 2 * units, width, block, copy_rows, [], "ffn_back", 8
         )
         down_grad[layer] = RingSum(
             ring_chunks([grad_branch], active, [[(0, 0, units)]], dim_block, "down_chunk", 1.5)
@@ -993,6 +992,9 @@
             )
         )
     first = attn_grad[0].sent
+    for ring in (gate_up_grad[0], down_grad[0]):
+        for _ in range(ring.middle - 2):
+            ring.advance()
     for rings in (attn_grad, gate_up_grad, down_grad):
         rings[:] = [
             ring.finish(*(first if layer == 0 and ring is not attn_grad[0] else ()))

time: 1070 us -> 1010 us (0.944)
  waiting for transfers between devices: 507 us -> 395 us
  starting transfers between devices: 176 us -> 240 us
    ppermute x12 -> x18, waiting for transfers between devices: 3.27 us -> 117 us  [ring_gather(): ahead.append(lax.ppermute(ahead[-1], 'dp', forward))]
    ppermute x24, waiting for transfers between devices: 151 us -> 56.5 us  [send(): lax.ppermute(parts[0], 'dp', self.backward)]
    ppermute x12 -> x18, waiting for transfers between devices: 96.9 us -> 21.4 us  [ring_gather(): behind.append(lax.ppermute(behind[-1], 'dp', backward))]
    ppermute x46, waiting for transfers between devices: 95.9 us -> 40.4 us  [swap(): lax.ppermute(block, 'tensor', [(i, i ^ distance) for i in range(count)])]
    ppermute x12, waiting for transfers between devices: 135 us -> 102 us  [partner(): return lax.ppermute(block, 'dp', [(i, i ^ 1 << bit) for i in range(count)])]
    ppermute x24, waiting for transfers between devices: 6.55 us -> 33.2 us  [send(): lax.ppermute(parts[1], 'dp', self.forward)]
    ppermute x46, starting transfers between devices: 104 us -> 128 us  [swap(): lax.ppermute(block, 'tensor', [(i, i ^ distance) for i in range(count)])]
    ppermute x12 -> x18, starting transfers between devices: 3.39 us -> 24.7 us  [ring_gather(): ahead.append(lax.ppermute(ahead[-1], 'dp', forward))]
  transfers between devices with their start and end apart: 138 -> 154, of which waited for: 62 -> 65; matrix products, arithmetic and copies ran while one was open for 7% -> 8% of each run, Pallas kernels for 14% -> 21%
where the time goes in v3:
time: 1010 us; the launch traced here: 1000 us
  waiting for transfers between devices  395 us (39%)
  starting transfers between devices  240 us (24%)
  Pallas kernels  227 us (22%)
  local copies, waits for them, and re-layouts  80.3 us (8%)
  other arithmetic  46.3 us (5%)
  between operations  15.3 us (2%)
    ppermute x46, starting transfers between devices, swap(): lax.ppermute(block, 'tensor', [(i, i ^ distance) for i in range(count)])  128 us
    ppermute x18, waiting for transfers between devices, ring_gather(): ahead.append(lax.ppermute(ahead[-1], 'dp', forward))  117 us
    ppermute x12, waiting for transfers between devices, partner(): return lax.ppermute(block, 'dp', [(i, i ^ 1 << bit) for i in range(count)])  102 us
    pallas_call x30, Pallas kernels, chunk(): pl.pallas_call(kernel, grid=(len(plan),), in_specs=in_specs, out_shape=[s...  58.9 us
    unnamed x623, local copies, waits for them, and re-layouts  56.5 us
    ppermute x24, waiting for transfers between devices, send(): lax.ppermute(parts[0], 'dp', self.backward)  56.5 us
    pallas_call x8, Pallas kernels, gathered_call(): pl.pallas_call(kernel, grid=(steps,), in_specs=[in_smem] + [in_hbm] * (le...  53.3 us
    pallas_call x8, Pallas kernels, spread_call(): pl.pallas_call(kernel, grid=(groups,), in_specs=[in_smem] + [in_hbm] * le...  49 us
  transfers between devices with their start and end apart: 154, of which 65 were waited for; matrix products, arithmetic and copies ran while one was open for 8% of the time, Pallas kernels for 21%

profile of v3, /device:TPU:1, one launch (start us, length us, event | category | flops | bytes accessed | tf_op | source)
XLA Modules:
  0.0 1003.6 jit_solution(15225522764351124423)
XLA Ops:
  25.3 7.5 collective-permute-done.5.refs_11_.refs_7_
  36.3 7.9 collective-permute-done.6.refs_10_.refs_6_
  56.7 5.1 collective-permute-start.8
  61.9 5.0 collective-permute-start.10
  85.5 11.3 %collective-permute-done.11 = bf16[4,2,64,256]{3,2,1,0:T(8,128)(2,1)S(1)} collective-permute-done((bf16[4,2,64,256]{3,2,1,0:T(8,128)(2,1)S(1)}, bf16[4,2,64,256]{3,2,1,0:T(8,128)(2,1)S(1)}, u32[]{:S(2)}, u32[]{:S(2)}) %collective-permute-start.11) | collective-permute-done | bytes 262176 | tf_op jit(solution)/shard_map/ppermute | solution.py:164
  109.1 19.4 %collective-permute-done.16.refs_5_.refs_1_ = bf16[256,2304]{1,0:T(8,128)(2,1)} collective-permute-done((bf16[256,2304]{1,0:T(8,128)(2,1)S(1)}, bf16[256,2304]{1,0:T(8,128)(2,1)}, u32[]{:S(2)}, u32[]{:S(2)}) %collective-permute-start.16) | collective-permute-done | bytes 1179680 | tf_op jit(solution)/shard_map/ppermute | solution.py:72
  130.0 6.5 collective-permute-done.13
  138.6 14.6 %attend.2 = (bf16[4,2,64,384]{3,2,1,0:T(8,128)(2,1)S(1)}, bf16[2,6,1024,256]{3,2,1,0:T(8,128)(2,1)}, bf16[2,6,256,256]{3,2,1,0:T(8,128)(2,1)}) custom-call(s32[1]{0:T(128)} %bitcast.14.odd_ref, bf16[4,2,64,384]{3,2,1,0:T(8,128)(2,1)S(1)} %bitcast.233, bf16[16,2,64,256]{3,2,1,0:T(8,128)(2,1)S(1)} %pad_maximum_fusion.5.pk_ref.pv_ref, ...), custom_call_target="tpu_custom_call" | custom-call | flops 41999998976 | bytes 1024 | tf_op jit(solution)/shard_map/attend/pallas_call | solution.py:611
  153.2 6.6 collective-permute-done.17.refs_6_.refs_2_
  162.1 5.2 out.2
  171.8 14.1 %collective-permute-done.18.refs_7_.refs_3_ = bf16[256,2304]{1,0:T(8,128)(2,1)S(1)} collective-permute-done((bf16[256,2304]{1,0:T(8,128)(2,1)}, bf16[256,2304]{1,0:T(8,128)(2,1)S(1)}, u32[]{:S(2)}, u32[]{:S(2)}) %collective-permute-start.18) | collective-permute-done | bytes 1179680 | tf_op jit(solution)/shard_map/ppermute | solution.py:72
  192.6 7.5 collective-permute-done.22.refs_1_.refs_5_
  204.5 8.2 collective-permute-done.23.refs_2_.refs_6_
  222.7 6.7 collective-permute-start.30
  229.3 4.4 collective-permute-start.32
  240.5 10.8 %active.2 = (bf16[512,1152]{1,0:T(8,128)(2,1)S(1)}, bf16[512,1152]{1,0:T(8,128)(2,1)S(1)}, bf16[512,1152]{1,0:T(8,128)(2,1)}) custom-call(s32[8]{0:T(128)S(1)} %select_reduce_fusion.1.source_ref, bf16[128,2048]{1,0:T(8,128)(2,1)S(1)} %multiply_convert_fusion.2.refs_0_.refs_4_, bf16[128,2048]{1,0:T(8,128)(2,1)S(1)} %collective-permute-done.30.refs_1_.refs_5_, ...), custom_call_target="tpu_custom_call" | custom-call | flops 27000000512 | bytes 1024 | tf_op jit(solution)/shard_map/active/pallas_call | solution.py:288
  251.4 6.4 down.2
  257.8 9.0 collective-permute-start.35
  273.2 10.5 %collective-permute-done.37.refs_5_.refs_1_ = bf16[256,1024]{1,0:T(8,128)(2,1)S(1)} collective-permute-done((bf16[256,1024]{1,0:T(8,128)(2,1)S(1)}, bf16[256,1024]{1,0:T(8,128)(2,1)S(1)}, u32[]{:S(2)}, u32[]{:S(2)}) %collective-permute-start.37) | collective-permute-done | bytes 524320 | tf_op jit(solution)/shard_map/ppermute | solution.py:72
  288.6 7.7 collective-permute-done.38.refs_6_.refs_2_
  302.7 5.4 collective-permute-done.39.refs_7_.refs_3_
  323.0 10.3 %collective-permute-done.48 = bf16[4,2,64,256]{3,2,1,0:T(8,128)(2,1)S(1)} collective-permute-done((bf16[4,2,64,256]{3,2,1,0:T(8,128)(2,1)S(1)}, bf16[4,2,64,256]{3,2,1,0:T(8,128)(2,1)S(1)}, u32[]{:S(2)}, u32[]{:S(2)}) %collective-permute-start.48) | collective-permute-done | bytes 262176 | tf_op jit(solution)/shard_map/ppermute | solution.py:164
  333.5 17.1 %collective-permute-done.49 = bf16[4,2,64,256]{3,2,1,0:T(8,128)(2,1)S(1)} collective-permute-done((bf16[4,2,64,256]{3,2,1,0:T(8,128)(2,1)S(1)}, bf16[4,2,64,256]{3,2,1,0:T(8,128)(2,1)S(1)}, u32[]{:S(2)}, u32[]{:S(2)}) %collective-permute-start.49) | collective-permute-done | bytes 262176 | tf_op jit(solution)/shard_map/ppermute | solution.py:164
  350.8 6.5 collective-permute-start.54
  362.5 14.6 %attend.3 = (bf16[4,2,64,384]{3,2,1,0:T(8,128)(2,1)S(1)}, bf16[2,6,1024,256]{3,2,1,0:T(8,128)(2,1)}, bf16[2,6,256,256]{3,2,1,0:T(8,128)(2,1)}) custom-call(s32[1]{0:T(128)} %bitcast.14.odd_ref, bf16[4,2,64,384]{3,2,1,0:T(8,128)(2,1)S(1)} %bitcast.235, bf16[16,2,64,256]{3,2,1,0:T(8,128)(2,1)S(1)} %pad_maximum_fusion.6.pk_ref.pv_ref, ...), custom_call_target="tpu_custom_call" | custom-call | flops 41999998976 | bytes 1024 | tf_op jit(solution)/shard_map/attend/pallas_call | solution.py:611
  381.9 10.6 %collective-permute-start.51 = (bf16[2,128,2048]{2,1,0:T(8,128)(2,1)S(1)}, bf16[2,128,2048]{2,1,0:T(8,128)(2,1)S(1)}, u32[]{:S(2)}, u32[]{:S(2)}) collective-permute-start(bf16[2,128,2048]{2,1,0:T(8,128)(2,1)S(1)} %get-tuple-element.129), channel_id=1, source_target_pairs={{0,1},{1,0},{2,3},{3,2},{4,5},{5,4},{6,7},{7,6},{8,9},{9,8},{10,11... | collective-permute-start | bytes 3145736 | tf_op jit(solution)/shard_map/ppermute | solution.py:147
  397.8 22.6 %collective-permute-done.55.refs_7_.refs_3_ = bf16[256,2304]{1,0:T(8,128)(2,1)} collective-permute-done((bf16[256,2304]{1,0:T(8,128)(2,1)}, bf16[256,2304]{1,0:T(8,128)(2,1)}, u32[]{:S(2)}, u32[]{:S(2)}) %collective-permute-start.55) | collective-permute-done | bytes 1179680 | tf_op jit(solution)/shard_map/ppermute | solution.py:72
  428.0 6.6 collective-permute-done.59.refs_1_.refs_5_
  436.8 10.4 %collective-permute-done.70.refs_8_.refs_4_ = bf16[128,2304]{1,0:T(8,128)(2,1)S(1)} collective-permute-done((bf16[128,2304]{1,0:T(8,128)(2,1)S(1)}, bf16[128,2304]{1,0:T(8,128)(2,1)S(1)}, u32[]{:S(2)}, u32[]{:S(2)}) %collective-permute-start.70) | collective-permute-done | bytes 589856 | tf_op jit(solution)/shard_map/ppermute | solution.py:76
  452.1 7.9 collective-permute-done.60.refs_2_.refs_6_
  461.4 10.7 %active.3 = (bf16[512,1152]{1,0:T(8,128)(2,1)S(1)}, bf16[512,1152]{1,0:T(8,128)(2,1)S(1)}, bf16[512,1152]{1,0:T(8,128)(2,1)}) custom-call(s32[8]{0:T(128)S(1)} %select_reduce_fusion.1.source_ref, bf16[128,2048]{1,0:T(8,128)(2,1)S(1)} %multiply_convert_fusion.refs_0_.refs_4_, bf16[128,2048]{1,0:T(8,128)(2,1)S(1)} %collective-permute-done.67.refs_1_.refs_5_, ...), custom_call_target="tpu_custom_call" | custom-call | flops 27000000512 | bytes 1024 | tf_op jit(solution)/shard_map/active/pallas_call | solution.py:288
  490.1 9.0 active_back.2.refs_9_.refs_4_.refs_8_
  501.5 8.6 ffn_back.2
  515.0 6.1 down.3
  530.0 7.0 collective-permute-done.78
  538.2 10.0 %collective-permute-done.73 = bf16[128,2048]{1,0:T(8,128)(2,1)S(1)} collective-permute-done((bf16[128,2048]{1,0:T(8,128)(2,1)S(1)}, bf16[128,2048]{1,0:T(8,128)(2,1)S(1)}, u32[]{:S(2)}, u32[]{:S(2)}) %collective-permute-start.73) | collective-permute-done | bytes 524320 | tf_op jit(solution)/shard_map/ppermute | solution.py:147
  558.8 4.2 collective-permute-done.80.refs_2_.refs_6_.refs_14_
  574.5 16.8 %attend_back.2 = (f32[4,2,64,384]{3,2,1,0:T(8,128)S(1)}, f32[16,2,64,256]{3,2,1,0:T(8,128)S(1)}, f32[4,2,64,256]{3,2,1,0:T(8,128)S(1)}) custom-call(s32[1]{0:T(128)} %bitcast.14.odd_ref, bf16[4,2,64,384]{3,2,1,0:T(8,128)(2,1)S(1)} %bitcast.238, bf16[4,2,64,384]{3,2,1,0:T(8,128)(2,1)S(1)} %bitcast.236, bf16[16,2,64,256]{3,2,1,0:T(8,128)(2,1)S(1)} %copy-done.7, ...), custom_call_target="tpu_custom_call" | custom-call | flops 48000000000 | bytes 1024 | tf_op jit(solution)/shard_map/attend_back/pallas_call | solution.py:646
  598.1 7.4 collective-permute-done.82
  612.9 11.4 %collective-permute-done.84 = bf16[4,2,64,256]{3,2,1,0:T(8,128)(2,1)S(1)} collective-permute-done((bf16[4,2,64,256]{3,2,1,0:T(8,128)(2,1)S(1)}, bf16[4,2,64,256]{3,2,1,0:T(8,128)(2,1)S(1)}, u32[]{:S(2)}, u32[]{:S(2)}) %collective-permute-start.84) | collective-permute-done | bytes 262176 | tf_op jit(solution)/shard_map/ppermute | solution.py:164
  625.8 5.3 normed_back.2
  642.3 9.1 collective-permute-done.86
  656.3 7.9 collective-permute-done.134.refs_9_
  675.8 8.5 active_back.3.refs_9_.refs_4_.refs_8_
  688.7 8.3 ffn_back.3
  698.1 7.4 collective-permute-done.113.refs_17_
  713.8 5.8 collective-permute-done.115.refs_17_
  734.7 4.8 collective-permute-start.94
  746.2 16.8 %attend_back.3 = (f32[4,2,64,384]{3,2,1,0:T(8,128)S(1)}, f32[16,2,64,256]{3,2,1,0:T(8,128)S(1)}, f32[4,2,64,256]{3,2,1,0:T(8,128)S(1)}) custom-call(s32[1]{0:T(128)} %bitcast.14.odd_ref, bf16[4,2,64,384]{3,2,1,0:T(8,128)(2,1)S(1)} %bitcast.237, bf16[4,2,64,384]{3,2,1,0:T(8,128)(2,1)S(1)} %bitcast.234, bf16[16,2,64,256]{3,2,1,0:T(8,128)(2,1)S(1)} %copy-done.5, ...), custom_call_target="tpu_custom_call" | custom-call | flops 48000000000 | bytes 1024 | tf_op jit(solution)/shard_map/attend_back/pallas_call | solution.py:646
  768.8 7.6 collective-permute-done.95
  776.9 18.5 %collective-permute-done.138.refs_9_ = bf16[128,1152]{1,0:T(8,128)(2,1)S(1)} collective-permute-done((bf16[128,1152]{1,0:T(8,128)(2,1)S(1)}, bf16[128,1152]{1,0:T(8,128)(2,1)S(1)}, u32[]{:S(2)}, u32[]{:S(2)}) %collective-permute-start.138) | collective-permute-done | bytes 294944 | tf_op jit(solution)/shard_map/ppermute | solution.py:99
  797.8 4.2 collective-permute-done.96
  807.2 14.9 %collective-permute-done.97 = bf16[4,2,64,256]{3,2,1,0:T(8,128)(2,1)S(1)} collective-permute-done((bf16[4,2,64,256]{3,2,1,0:T(8,128)(2,1)S(1)}, bf16[4,2,64,256]{3,2,1,0:T(8,128)(2,1)S(1)}, u32[]{:S(2)}, u32[]{:S(2)}) %collective-permute-start.97) | collective-permute-done | bytes 262176 | tf_op jit(solution)/shard_map/ppermute | solution.py:164
  826.2 5.3 normed_back.3
  831.4 5.1 collective-permute-start.98
  842.1 6.8 collective-permute-done.125.refs_10_
  866.7 4.4 collective-permute-done.126.refs_9_
  873.9 13.0 %collective-permute-done.127.refs_10_ = bf16[256,2304]{1,0:T(8,128)(2,1)} collective-permute-done((bf16[256,2304]{1,0:T(8,128)(2,1)}, bf16[256,2304]{1,0:T(8,128)(2,1)}, u32[]{:S(2)}, u32[]{:S(2)}) %collective-permute-start.127) | collective-permute-done | bytes 1179680 | tf_op jit(solution)/shard_map/ppermute | solution.py:100
  893.9 4.4 gate_up_chunk.13
  906.1 7.7 collective-permute-done.102.refs_19_
  927.8 11.5 %collective-permute-start.119 = (bf16[256,256]{1,0:T(8,128)(2,1)}, bf16[256,256]{1,0:T(8,128)(2,1)S(1)}, u32[]{:S(2)}, u32[]{:S(2)}) collective-permute-start(bf16[256,256]{1,0:T(8,128)(2,1)} %slice.674.refs_4_), channel_id=1, source_target_pairs={{0,1},{1,0},{2,3},{3,2},{4,5},{5,4},{6,7},{7,6},{8,9},{9,8},{10,11... | collective-permute-start | bytes 393224 | tf_op jit(solution)/shard_map/ppermute | solution.py:147
  939.2 8.9 collective-permute-start.121
  976.5 6.9 collective-permute-start.108
  983.4 6.9 collective-permute-start.110
  (1062 shorter events, 410.8 us)
Async XLA Ops:
  97.8 30.7 %collective-permute-start.16 = (bf16[256,2304]{1,0:T(8,128)(2,1)S(1)}, bf16[256,2304]{1,0:T(8,128)(2,1)}, u32[]{:S(2)}, u32[]{:S(2)}) collective-permute-start(bf16[256,2304]{1,0:T(8,128)(2,1)S(1)} %pad_maximum_fusion.3.refs_4_.refs_0_), channel_id=1, source_target_pairs={{0,8},{8,16},{16,24},{24,28},{28,20},{20,12},{12,4},{4,0},{1,9},{9... | collective-permute-start | bytes 3538952 | tf_op jit(solution)/shard_map/ppermute | solution.py:72
  98.7 29.8 %collective-permute-start.19 = (bf16[256,2304]{1,0:T(8,128)(2,1)S(1)}, bf16[256,2304]{1,0:T(8,128)(2,1)}, u32[]{:S(2)}, u32[]{:S(2)}) collective-permute-start(bf16[256,2304]{1,0:T(8,128)(2,1)S(1)} %pad_maximum_fusion.3.refs_4_.refs_0_), channel_id=1, source_target_pairs={{8,0},{16,8},{24,16},{28,24},{20,28},{12,20},{4,12},{0,4},{9,1},{1... | collective-permute-start | bytes 3538952 | tf_op jit(solution)/shard_map/ppermute | solution.py:73
  104.1 32.3 %collective-permute-start.13 = (bf16[8,2,64,256]{3,2,1,0:T(8,128)(2,1)}, bf16[8,2,64,256]{3,2,1,0:T(8,128)(2,1)}, u32[]{:S(2)}, u32[]{:S(2)}) collective-permute-start(bf16[8,2,64,256]{3,2,1,0:T(8,128)(2,1)} %pad_maximum_fusion.11), channel_id=1, source_target_pairs={{0,8},{4,12},{8,0},{12,4},{16,24},{20,28},{24,16},{28,20},{1,9},{5... | collective-permute-start | bytes 1572872 | tf_op jit(solution)/shard_map/ppermute | solution.py:164
  128.5 31.3 %collective-permute-start.17 = (bf16[256,2304]{1,0:T(8,128)(2,1)}, bf16[256,2304]{1,0:T(8,128)(2,1)}, u32[]{:S(2)}, u32[]{:S(2)}) collective-permute-start(bf16[256,2304]{1,0:T(8,128)(2,1)} %collective-permute-done.16.refs_5_.refs_1_), channel_id=1, source_target_pairs={{0,8},{8,16},{16,24},{24,28},{28,20},{20,12},{12,4},{4,0},{1,9},{9... | collective-permute-start | bytes 3538952 | tf_op jit(solution)/shard_map/ppermute | solution.py:72
  128.5 33.5 %collective-permute-start.20 = (bf16[256,2304]{1,0:T(8,128)(2,1)}, bf16[256,2304]{1,0:T(8,128)(2,1)}, u32[]{:S(2)}, u32[]{:S(2)}) collective-permute-start(bf16[256,2304]{1,0:T(8,128)(2,1)} %collective-permute-done.19.refs_12_.refs_8_), channel_id=1, source_target_pairs={{8,0},{16,8},{24,16},{28,24},{20,28},{12,20},{4,12},{0,4},{9,1},{1... | collective-permute-start | bytes 3538952 | tf_op jit(solution)/shard_map/ppermute | solution.py:73
  159.8 26.1 %collective-permute-start.18 = (bf16[256,2304]{1,0:T(8,128)(2,1)}, bf16[256,2304]{1,0:T(8,128)(2,1)S(1)}, u32[]{:S(2)}, u32[]{:S(2)}) collective-permute-start(bf16[256,2304]{1,0:T(8,128)(2,1)} %collective-permute-done.17.refs_6_.refs_2_), channel_id=1, source_target_pairs={{0,8},{8,16},{16,24},{24,28},{28,20},{20,12},{12,4},{4,0},{1,9},{9... | collective-permute-start | bytes 3538952 | tf_op jit(solution)/shard_map/ppermute | solution.py:72
  162.0 25.8 %collective-permute-start.21 = (bf16[256,2304]{1,0:T(8,128)(2,1)}, bf16[256,2304]{1,0:T(8,128)(2,1)}, u32[]{:S(2)}, u32[]{:S(2)}) collective-permute-start(bf16[256,2304]{1,0:T(8,128)(2,1)} %collective-permute-done.20.refs_11_.refs_7_), channel_id=1, source_target_pairs={{8,0},{16,8},{24,16},{28,24},{20,28},{12,20},{4,12},{0,4},{9,1},{1... | collective-permute-start | bytes 3538952 | tf_op jit(solution)/shard_map/ppermute | solution.py:73
  167.4 22.7 %collective-permute-start.14 = (bf16[2,128,2048]{2,1,0:T(8,128)(2,1)}, bf16[2,128,2048]{2,1,0:T(8,128)(2,1)}, u32[]{:S(2)}, u32[]{:S(2)}) collective-permute-start(bf16[2,128,2048]{2,1,0:T(8,128)(2,1)} %get-tuple-element.118), channel_id=1, source_target_pairs={{0,1},{1,0},{2,3},{3,2},{4,5},{5,4},{6,7},{7,6},{8,9},{9,8},{10,11... | collective-permute-start | bytes 3145736 | tf_op jit(solution)/shard_map/ppermute | solution.py:147
  216.4 20.8 %collective-permute-start.33 = (bf16[128,2304]{1,0:T(8,128)(2,1)S(1)}, bf16[128,2304]{1,0:T(8,128)(2,1)S(1)}, u32[]{:S(2)}, u32[]{:S(2)}) collective-permute-start(bf16[128,2304]{1,0:T(8,128)(2,1)S(1)} %slice.493), channel_id=1, source_target_pairs={{0,8},{8,16},{16,24},{24,28},{28,20},{20,12},{12,4},{4,0},{1,9},{9... | collective-permute-start | bytes 1769480 | tf_op jit(solution)/shard_map/ppermute | solution.py:76
  218.7 21.7 %collective-permute-start.34 = (bf16[128,2304]{1,0:T(8,128)(2,1)S(1)}, bf16[128,2304]{1,0:T(8,128)(2,1)S(1)}, u32[]{:S(2)}, u32[]{:S(2)}) collective-permute-start(bf16[128,2304]{1,0:T(8,128)(2,1)S(1)} %slice.494), channel_id=1, source_target_pairs={{8,0},{16,8},{24,16},{28,24},{20,28},{12,20},{4,12},{0,4},{9,1},{1... | collective-permute-start | bytes 1769480 | tf_op jit(solution)/shard_map/ppermute | solution.py:77
  321.5 29.3 %collective-permute-start.53 = (bf16[256,2304]{1,0:T(8,128)(2,1)S(1)}, bf16[256,2304]{1,0:T(8,128)(2,1)S(1)}, u32[]{:S(2)}, u32[]{:S(2)}) collective-permute-start(bf16[256,2304]{1,0:T(8,128)(2,1)S(1)} %pad_maximum_fusion.4.refs_4_.refs_0_), channel_id=1, source_target_pairs={{0,8},{8,16},{16,24},{24,28},{28,20},{20,12},{12,4},{4,0},{1,9},{9... | collective-permute-start | bytes 3538952 | tf_op jit(solution)/shard_map/ppermute | solution.py:72
  321.8 35.5 %collective-permute-start.56 = (bf16[256,2304]{1,0:T(8,128)(2,1)S(1)}, bf16[256,2304]{1,0:T(8,128)(2,1)S(1)}, u32[]{:S(2)}, u32[]{:S(2)}) collective-permute-start(bf16[256,2304]{1,0:T(8,128)(2,1)S(1)} %pad_maximum_fusion.4.refs_4_.refs_0_), channel_id=1, source_target_pairs={{8,0},{16,8},{24,16},{28,24},{20,28},{12,20},{4,12},{0,4},{9,1},{1... | collective-permute-start | bytes 3538952 | tf_op jit(solution)/shard_map/ppermute | solution.py:73
  350.8 41.7 %collective-permute-start.54 = (bf16[256,2304]{1,0:T(8,128)(2,1)S(1)}, bf16[256,2304]{1,0:T(8,128)(2,1)}, u32[]{:S(2)}, u32[]{:S(2)}) collective-permute-start(bf16[256,2304]{1,0:T(8,128)(2,1)S(1)} %collective-permute-done.53.refs_5_.refs_1_), channel_id=1, source_target_pairs={{0,8},{8,16},{16,24},{24,28},{28,20},{20,12},{12,4},{4,0},{1,9},{9... | collective-permute-start | bytes 3538952 | tf_op jit(solution)/shard_map/ppermute | solution.py:72
  357.3 35.2 %collective-permute-start.57 = (bf16[256,2304]{1,0:T(8,128)(2,1)S(1)}, bf16[256,2304]{1,0:T(8,128)(2,1)}, u32[]{:S(2)}, u32[]{:S(2)}) collective-permute-start(bf16[256,2304]{1,0:T(8,128)(2,1)S(1)} %collective-permute-done.56.refs_12_.refs_8_), channel_id=1, source_target_pairs={{8,0},{16,8},{24,16},{28,24},{20,28},{12,20},{4,12},{0,4},{9,1},{1... | collective-permute-start | bytes 3538952 | tf_op jit(solution)/shard_map/ppermute | solution.py:73
  392.5 27.9 %collective-permute-start.55 = (bf16[256,2304]{1,0:T(8,128)(2,1)}, bf16[256,2304]{1,0:T(8,128)(2,1)}, u32[]{:S(2)}, u32[]{:S(2)}) collective-permute-start(bf16[256,2304]{1,0:T(8,128)(2,1)} %collective-permute-done.54.refs_6_.refs_2_), channel_id=1, source_target_pairs={{0,8},{8,16},{16,24},{24,28},{28,20},{20,12},{12,4},{4,0},{1,9},{9... | collective-permute-start | bytes 3538952 | tf_op jit(solution)/shard_map/ppermute | solution.py:72
  392.5 28.0 %collective-permute-start.58 = (bf16[256,2304]{1,0:T(8,128)(2,1)}, bf16[256,2304]{1,0:T(8,128)(2,1)}, u32[]{:S(2)}, u32[]{:S(2)}) collective-permute-start(bf16[256,2304]{1,0:T(8,128)(2,1)} %collective-permute-done.57.refs_11_.refs_7_), channel_id=1, source_target_pairs={{8,0},{16,8},{24,16},{28,24},{20,28},{12,20},{4,12},{0,4},{9,1},{1... | collective-permute-start | bytes 3538952 | tf_op jit(solution)/shard_map/ppermute | solution.py:73
  395.9 27.4 %collective-permute-start.52 = (bf16[128,2048]{1,0:T(8,128)(2,1)}, bf16[128,2048]{1,0:T(8,128)(2,1)}, u32[]{:S(2)}, u32[]{:S(2)}) collective-permute-start(bf16[128,2048]{1,0:T(8,128)(2,1)} %fusion.22), channel_id=1, source_target_pairs={{0,2},{1,3},{2,0},{3,1},{4,6},{5,7},{6,4},{7,5},{8,10},{9,11},{10,... | collective-permute-start | bytes 1572872 | tf_op jit(solution)/shard_map/ppermute | solution.py:147
  396.3 30.3 %collective-permute-start.75 = (bf16[128,2048]{1,0:T(8,128)(2,1)S(1)}, bf16[128,2048]{1,0:T(8,128)(2,1)}, u32[]{:S(2)}, u32[]{:S(2)}) collective-permute-start(bf16[128,2048]{1,0:T(8,128)(2,1)S(1)} %constant_dynamic-update-slice_fusion.8.refs_0_.refs_4_), channel_id=1, source_target_pairs={{0,2},{1,3},{2,0},{3,1},{4,6},{5,7},{6,4},{7,5},{8,10},{9,11},{10,... | collective-permute-start | bytes 1572872 | tf_op jit(solution)/shard_map/ppermute | solution.py:147
  423.1 24.1 %collective-permute-start.70 = (bf16[128,2304]{1,0:T(8,128)(2,1)S(1)}, bf16[128,2304]{1,0:T(8,128)(2,1)S(1)}, u32[]{:S(2)}, u32[]{:S(2)}) collective-permute-start(bf16[128,2304]{1,0:T(8,128)(2,1)S(1)} %slice.506), channel_id=1, source_target_pairs={{0,8},{8,16},{16,24},{24,28},{28,20},{20,12},{12,4},{4,0},{1,9},{9... | collective-permute-start | bytes 1769480 | tf_op jit(solution)/shard_map/ppermute | solution.py:76
  425.1 25.1 %collective-permute-start.68 = (bf16[128,2048]{1,0:T(8,128)(2,1)S(1)}, bf16[128,2048]{1,0:T(8,128)(2,1)S(1)}, u32[]{:S(2)}, u32[]{:S(2)}) collective-permute-start(bf16[128,2048]{1,0:T(8,128)(2,1)S(1)} %multiply_convert_fusion.refs_0_.refs_4_), channel_id=1, source_target_pairs={{0,2},{1,3},{2,0},{3,1},{4,6},{5,7},{6,4},{7,5},{8,10},{9,11},{10,... | collective-permute-start | bytes 1572872 | tf_op jit(solution)/shard_map/ppermute | solution.py:147
  426.6 23.6 %collective-permute-start.71 = (bf16[128,2304]{1,0:T(8,128)(2,1)S(1)}, bf16[128,2304]{1,0:T(8,128)(2,1)S(1)}, u32[]{:S(2)}, u32[]{:S(2)}) collective-permute-start(bf16[128,2304]{1,0:T(8,128)(2,1)S(1)} %slice.507), channel_id=1, source_target_pairs={{8,0},{16,8},{24,16},{28,24},{20,28},{12,20},{4,12},{0,4},{9,1},{1... | collective-permute-start | bytes 1769480 | tf_op jit(solution)/shard_map/ppermute | solution.py:77
  434.5 25.4 %collective-permute-start.60 = (bf16[256,1152]{1,0:T(8,128)(2,1)S(1)}, bf16[256,1152]{1,0:T(8,128)(2,1)}, u32[]{:S(2)}, u32[]{:S(2)}) collective-permute-start(bf16[256,1152]{1,0:T(8,128)(2,1)S(1)} %collective-permute-done.59.refs_1_.refs_5_), channel_id=1, source_target_pairs={{0,8},{8,16},{16,24},{24,28},{28,20},{20,12},{12,4},{4,0},{1,9},{9... | collective-permute-start | bytes 1769480 | tf_op jit(solution)/shard_map/ppermute | solution.py:72
  435.8 24.6 %collective-permute-start.64 = (bf16[256,1152]{1,0:T(8,128)(2,1)S(1)}, bf16[256,1152]{1,0:T(8,128)(2,1)}, u32[]{:S(2)}, u32[]{:S(2)}) collective-permute-start(bf16[256,1152]{1,0:T(8,128)(2,1)S(1)} %collective-permute-done.63.refs_8_.refs_12_), channel_id=1, source_target_pairs={{8,0},{16,8},{24,16},{28,24},{20,28},{12,20},{4,12},{0,4},{9,1},{1... | collective-permute-start | bytes 1769480 | tf_op jit(solution)/shard_map/ppermute | solution.py:73
  450.2 21.9 %collective-permute-start.74 = (bf16[128,2048]{1,0:T(8,128)(2,1)S(1)}, bf16[128,2048]{1,0:T(8,128)(2,1)S(1)}, u32[]{:S(2)}, u32[]{:S(2)}) collective-permute-start(bf16[128,2048]{1,0:T(8,128)(2,1)S(1)} %constant_dynamic-update-slice_fusion.8.refs_0_.refs_4_), channel_id=1, source_target_pairs={{0,1},{1,0},{2,3},{3,2},{4,5},{5,4},{6,7},{7,6},{8,9},{9,8},{10,11... | collective-permute-start | bytes 1572872 | tf_op jit(solution)/shard_map/ppermute | solution.py:147
  451.7 20.5 %collective-permute-start.76 = (bf16[128,2048]{1,0:T(8,128)(2,1)}, bf16[128,2048]{1,0:T(8,128)(2,1)S(1)}, u32[]{:S(2)}, u32[]{:S(2)}) collective-permute-start(bf16[128,2048]{1,0:T(8,128)(2,1)} %collective-permute-done.75.refs_2_.refs_6_), channel_id=1, source_target_pairs={{0,1},{1,0},{2,3},{3,2},{4,5},{5,4},{6,7},{7,6},{8,9},{9,8},{10,11... | collective-permute-start | bytes 1572872 | tf_op jit(solution)/shard_map/ppermute | solution.py:147
  459.9 22.4 %collective-permute-start.61 = (bf16[256,1152]{1,0:T(8,128)(2,1)}, bf16[256,1152]{1,0:T(8,128)(2,1)S(1)}, u32[]{:S(2)}, u32[]{:S(2)}) collective-permute-start(bf16[256,1152]{1,0:T(8,128)(2,1)} %collective-permute-done.60.refs_2_.refs_6_), channel_id=1, source_target_pairs={{0,8},{8,16},{16,24},{24,28},{28,20},{20,12},{12,4},{4,0},{1,9},{9... | collective-permute-start | bytes 1769480 | tf_op jit(solution)/shard_map/ppermute | solution.py:72
  460.3 22.5 %collective-permute-start.65 = (bf16[256,1152]{1,0:T(8,128)(2,1)}, bf16[256,1152]{1,0:T(8,128)(2,1)S(1)}, u32[]{:S(2)}, u32[]{:S(2)}) collective-permute-start(bf16[256,1152]{1,0:T(8,128)(2,1)} %collective-permute-done.64.refs_7_.refs_11_), channel_id=1, source_target_pairs={{8,0},{16,8},{24,16},{28,24},{20,28},{12,20},{4,12},{0,4},{9,1},{1... | collective-permute-start | bytes 1769480 | tf_op jit(solution)/shard_map/ppermute | solution.py:73
  488.3 36.7 %collective-permute-start.148 = (bf16[256,1152]{1,0:T(8,128)(2,1)S(1)}, bf16[256,1152]{1,0:T(8,128)(2,1)S(1)}, u32[]{:S(2)}, u32[]{:S(2)}) collective-permute-start(bf16[256,1152]{1,0:T(8,128)(2,1)S(1)} %get-tuple-element.211), channel_id=1, source_target_pairs={{8,0},{16,8},{24,16},{28,24},{20,28},{12,20},{4,12},{0,4},{9,1},{1... | collective-permute-start | bytes 1769480 | tf_op jit(solution)/shard_map/ppermute | solution.py:99
  489.2 37.1 %collective-permute-start.149 = (bf16[256,1152]{1,0:T(8,128)(2,1)S(1)}, bf16[256,1152]{1,0:T(8,128)(2,1)S(1)}, u32[]{:S(2)}, u32[]{:S(2)}) collective-permute-start(bf16[256,1152]{1,0:T(8,128)(2,1)S(1)} %get-tuple-element.212), channel_id=1, source_target_pairs={{0,8},{8,16},{16,24},{24,28},{28,20},{20,12},{12,4},{4,0},{1,9},{9... | collective-permute-start | bytes 1769480 | tf_op jit(solution)/shard_map/ppermute | solution.py:100
  522.8 29.0 %collective-permute-start.130 = (bf16[128,2304]{1,0:T(8,128)(2,1)S(1)}, bf16[128,2304]{1,0:T(8,128)(2,1)S(1)}, u32[]{:S(2)}, u32[]{:S(2)}) collective-permute-start(bf16[128,2304]{1,0:T(8,128)(2,1)S(1)} %get-tuple-element.189), channel_id=1, source_target_pairs={{8,0},{16,8},{24,16},{28,24},{20,28},{12,20},{4,12},{0,4},{9,1},{1... | collective-permute-start | bytes 1769480 | tf_op jit(solution)/shard_map/ppermute | solution.py:99
  524.2 27.6 %collective-permute-start.131 = (bf16[128,2304]{1,0:T(8,128)(2,1)S(1)}, bf16[128,2304]{1,0:T(8,128)(2,1)S(1)}, u32[]{:S(2)}, u32[]{:S(2)}) collective-permute-start(bf16[128,2304]{1,0:T(8,128)(2,1)S(1)} %get-tuple-element.190), channel_id=1, source_target_pairs={{0,8},{8,16},{16,24},{24,28},{28,20},{20,12},{12,4},{4,0},{1,9},{9... | collective-permute-start | bytes 1769480 | tf_op jit(solution)/shard_map/ppermute | solution.py:100
  525.1 23.2 %collective-permute-start.73 = (bf16[128,2048]{1,0:T(8,128)(2,1)S(1)}, bf16[128,2048]{1,0:T(8,128)(2,1)S(1)}, u32[]{:S(2)}, u32[]{:S(2)}) collective-permute-start(bf16[128,2048]{1,0:T(8,128)(2,1)S(1)} %fusion.23), channel_id=1, source_target_pairs={{0,2},{1,3},{2,0},{3,1},{4,6},{5,7},{6,4},{7,5},{8,10},{9,11},{10,... | collective-permute-start | bytes 1572872 | tf_op jit(solution)/shard_map/ppermute | solution.py:147
  528.1 28.6 %collective-permute-start.150 = (bf16[256,1152]{1,0:T(8,128)(2,1)S(1)}, bf16[256,1152]{1,0:T(8,128)(2,1)S(1)}, u32[]{:S(2)}, u32[]{:S(2)}) collective-permute-start(bf16[256,1152]{1,0:T(8,128)(2,1)S(1)} %get-tuple-element.213), channel_id=1, source_target_pairs={{8,0},{16,8},{24,16},{28,24},{20,28},{12,20},{4,12},{0,4},{9,1},{1... | collective-permute-start | bytes 1769480 | tf_op jit(solution)/shard_map/ppermute | solution.py:99
  537.0 28.8 %collective-permute-start.151 = (bf16[256,1152]{1,0:T(8,128)(2,1)S(1)}, bf16[256,1152]{1,0:T(8,128)(2,1)S(1)}, u32[]{:S(2)}, u32[]{:S(2)}) collective-permute-start(bf16[256,1152]{1,0:T(8,128)(2,1)S(1)} %get-tuple-element.214), channel_id=1, source_target_pairs={{0,8},{8,16},{16,24},{24,28},{28,20},{20,12},{12,4},{4,0},{1,9},{9... | collective-permute-start | bytes 1769480 | tf_op jit(solution)/shard_map/ppermute | solution.py:100
  554.2 79.2 %collective-permute-start.132 = (bf16[256,2304]{1,0:T(8,128)(2,1)S(1)}, bf16[256,2304]{1,0:T(8,128)(2,1)S(1)}, u32[]{:S(2)}, u32[]{:S(2)}) collective-permute-start(bf16[256,2304]{1,0:T(8,128)(2,1)S(1)} %get-tuple-element.191), channel_id=1, source_target_pairs={{8,0},{16,8},{24,16},{28,24},{20,28},{12,20},{4,12},{0,4},{9,1},{1... | collective-permute-start | bytes 3538952 | tf_op jit(solution)/shard_map/ppermute | solution.py:99
  556.6 76.7 %collective-permute-start.133 = (bf16[256,2304]{1,0:T(8,128)(2,1)S(1)}, bf16[256,2304]{1,0:T(8,128)(2,1)}, u32[]{:S(2)}, u32[]{:S(2)}) collective-permute-start(bf16[256,2304]{1,0:T(8,128)(2,1)S(1)} %get-tuple-element.192), channel_id=1, source_target_pairs={{0,8},{8,16},{16,24},{24,28},{28,20},{20,12},{12,4},{4,0},{1,9},{9... | collective-permute-start | bytes 3538952 | tf_op jit(solution)/shard_map/ppermute | solution.py:100
  567.6 25.1 %collective-permute-start.152 = (bf16[256,1152]{1,0:T(8,128)(2,1)S(1)}, bf16[256,1152]{1,0:T(8,128)(2,1)S(1)}, u32[]{:S(2)}, u32[]{:S(2)}) collective-permute-start(bf16[256,1152]{1,0:T(8,128)(2,1)S(1)} %get-tuple-element.215), channel_id=1, source_target_pairs={{8,0},{16,8},{24,16},{28,24},{20,28},{12,20},{4,12},{0,4},{9,1},{1... | collective-permute-start | bytes 1769480 | tf_op jit(solution)/shard_map/ppermute | solution.py:99
  569.8 24.9 %collective-permute-start.153 = (bf16[256,1152]{1,0:T(8,128)(2,1)S(1)}, bf16[256,1152]{1,0:T(8,128)(2,1)S(1)}, u32[]{:S(2)}, u32[]{:S(2)}) collective-permute-start(bf16[256,1152]{1,0:T(8,128)(2,1)S(1)} %get-tuple-element.216), channel_id=1, source_target_pairs={{0,8},{8,16},{16,24},{24,28},{28,20},{20,12},{12,4},{4,0},{1,9},{9... | collective-permute-start | bytes 1769480 | tf_op jit(solution)/shard_map/ppermute | solution.py:100
  636.6 27.6 %collective-permute-start.134 = (bf16[256,2304]{1,0:T(8,128)(2,1)S(1)}, bf16[256,2304]{1,0:T(8,128)(2,1)S(1)}, u32[]{:S(2)}, u32[]{:S(2)}) collective-permute-start(bf16[256,2304]{1,0:T(8,128)(2,1)S(1)} %get-tuple-element.193), channel_id=1, source_target_pairs={{8,0},{16,8},{24,16},{28,24},{20,28},{12,20},{4,12},{0,4},{9,1},{1... | collective-permute-start | bytes 3538952 | tf_op jit(solution)/shard_map/ppermute | solution.py:99
  638.0 27.2 %collective-permute-start.135 = (bf16[256,2304]{1,0:T(8,128)(2,1)S(1)}, bf16[256,2304]{1,0:T(8,128)(2,1)S(1)}, u32[]{:S(2)}, u32[]{:S(2)}) collective-permute-start(bf16[256,2304]{1,0:T(8,128)(2,1)S(1)} %get-tuple-element.194), channel_id=1, source_target_pairs={{0,8},{8,16},{16,24},{24,28},{28,20},{20,12},{12,4},{4,0},{1,9},{9... | collective-permute-start | bytes 3538952 | tf_op jit(solution)/shard_map/ppermute | solution.py:100
  640.4 29.6 %collective-permute-start.111 = (bf16[128,1024]{1,0:T(8,128)(2,1)S(1)}, bf16[128,1024]{1,0:T(8,128)(2,1)S(1)}, u32[]{:S(2)}, u32[]{:S(2)}) collective-permute-start(bf16[128,1024]{1,0:T(8,128)(2,1)S(1)} %get-tuple-element.167), channel_id=1, source_target_pairs={{8,0},{16,8},{24,16},{28,24},{20,28},{12,20},{4,12},{0,4},{9,1},{1... | collective-permute-start | bytes 786440 | tf_op jit(solution)/shard_map/ppermute | solution.py:99
  641.8 30.7 %collective-permute-start.112 = (bf16[128,1024]{1,0:T(8,128)(2,1)S(1)}, bf16[128,1024]{1,0:T(8,128)(2,1)S(1)}, u32[]{:S(2)}, u32[]{:S(2)}) collective-permute-start(bf16[128,1024]{1,0:T(8,128)(2,1)S(1)} %get-tuple-element.168), channel_id=1, source_target_pairs={{0,8},{8,16},{16,24},{24,28},{28,20},{20,12},{12,4},{4,0},{1,9},{9... | collective-permute-start | bytes 786440 | tf_op jit(solution)/shard_map/ppermute | solution.py:100
  668.4 41.6 %collective-permute-start.136 = (bf16[256,2304]{1,0:T(8,128)(2,1)}, bf16[256,2304]{1,0:T(8,128)(2,1)S(1)}, u32[]{:S(2)}, u32[]{:S(2)}) collective-permute-start(bf16[256,2304]{1,0:T(8,128)(2,1)} %get-tuple-element.195), channel_id=1, source_target_pairs={{8,0},{16,8},{24,16},{28,24},{20,28},{12,20},{4,12},{0,4},{9,1},{1... | collective-permute-start | bytes 3538952 | tf_op jit(solution)/shard_map/ppermute | solution.py:99
  668.8 41.2 %collective-permute-start.137 = (bf16[256,2304]{1,0:T(8,128)(2,1)S(1)}, bf16[256,2304]{1,0:T(8,128)(2,1)}, u32[]{:S(2)}, u32[]{:S(2)}) collective-permute-start(bf16[256,2304]{1,0:T(8,128)(2,1)S(1)} %get-tuple-element.196), channel_id=1, source_target_pairs={{0,8},{8,16},{16,24},{24,28},{28,20},{20,12},{12,4},{4,0},{1,9},{9... | collective-permute-start | bytes 3538952 | tf_op jit(solution)/shard_map/ppermute | solution.py:100
  674.2 31.3 %collective-permute-start.113 = (bf16[256,1024]{1,0:T(8,128)(2,1)}, bf16[256,1024]{1,0:T(8,128)(2,1)}, u32[]{:S(2)}, u32[]{:S(2)}) collective-permute-start(bf16[256,1024]{1,0:T(8,128)(2,1)} %get-tuple-element.169), channel_id=1, source_target_pairs={{8,0},{16,8},{24,16},{28,24},{20,28},{12,20},{4,12},{0,4},{9,1},{1... | collective-permute-start | bytes 1572872 | tf_op jit(solution)/shard_map/ppermute | solution.py:99
  674.3 31.9 %collective-permute-start.114 = (bf16[256,1024]{1,0:T(8,128)(2,1)}, bf16[256,1024]{1,0:T(8,128)(2,1)}, u32[]{:S(2)}, u32[]{:S(2)}) collective-permute-start(bf16[256,1024]{1,0:T(8,128)(2,1)} %get-tuple-element.170), channel_id=1, source_target_pairs={{0,8},{8,16},{16,24},{24,28},{28,20},{20,12},{12,4},{4,0},{1,9},{9... | collective-permute-start | bytes 1572872 | tf_op jit(solution)/shard_map/ppermute | solution.py:100
  740.9 186.8 %collective-permute-start.120 = (bf16[256,256]{1,0:T(8,128)(2,1)}, bf16[256,256]{1,0:T(8,128)(2,1)}, u32[]{:S(2)}, u32[]{:S(2)}) collective-permute-start(bf16[256,256]{1,0:T(8,128)(2,1)} %slice.674.refs_4_), channel_id=1, source_target_pairs={{0,2},{1,3},{2,0},{3,1},{4,6},{5,7},{6,4},{7,5},{8,10},{9,11},{10,... | collective-permute-start | bytes 393224 | tf_op jit(solution)/shard_map/ppermute | solution.py:147
  765.8 36.5 %collective-permute-start.122 = (bf16[128,2304]{1,0:T(8,128)(2,1)S(1)}, bf16[128,2304]{1,0:T(8,128)(2,1)S(1)}, u32[]{:S(2)}, u32[]{:S(2)}) collective-permute-start(bf16[128,2304]{1,0:T(8,128)(2,1)S(1)} %get-tuple-element.177), channel_id=1, source_target_pairs={{8,0},{16,8},{24,16},{28,24},{20,28},{12,20},{4,12},{0,4},{9,1},{1... | collective-permute-start | bytes 1769480 | tf_op jit(solution)/shard_map/ppermute | solution.py:99
  766.7 36.0 %collective-permute-start.123 = (bf16[128,2304]{1,0:T(8,128)(2,1)S(1)}, bf16[128,2304]{1,0:T(8,128)(2,1)S(1)}, u32[]{:S(2)}, u32[]{:S(2)}) collective-permute-start(bf16[128,2304]{1,0:T(8,128)(2,1)S(1)} %get-tuple-element.178), channel_id=1, source_target_pairs={{0,8},{8,16},{16,24},{24,28},{28,20},{20,12},{12,4},{4,0},{1,9},{9... | collective-permute-start | bytes 1769480 | tf_op jit(solution)/shard_map/ppermute | solution.py:100
  767.9 27.5 %collective-permute-start.138 = (bf16[128,1152]{1,0:T(8,128)(2,1)S(1)}, bf16[128,1152]{1,0:T(8,128)(2,1)S(1)}, u32[]{:S(2)}, u32[]{:S(2)}) collective-permute-start(bf16[128,1152]{1,0:T(8,128)(2,1)S(1)} %get-tuple-element.197), channel_id=1, source_target_pairs={{8,0},{16,8},{24,16},{28,24},{20,28},{12,20},{4,12},{0,4},{9,1},{1... | collective-permute-start | bytes 884744 | tf_op jit(solution)/shard_map/ppermute | solution.py:99
  796.3 35.1 %collective-permute-start.140 = (bf16[256,1152]{1,0:T(8,128)(2,1)S(1)}, bf16[256,1152]{1,0:T(8,128)(2,1)S(1)}, u32[]{:S(2)}, u32[]{:S(2)}) collective-permute-start(bf16[256,1152]{1,0:T(8,128)(2,1)S(1)} %get-tuple-element.199), channel_id=1, source_target_pairs={{8,0},{16,8},{24,16},{28,24},{20,28},{12,20},{4,12},{0,4},{9,1},{1... | collective-permute-start | bytes 1769480 | tf_op jit(solution)/shard_map/ppermute | solution.py:99
  802.1 34.5 %collective-permute-start.141 = (bf16[256,1152]{1,0:T(8,128)(2,1)S(1)}, bf16[256,1152]{1,0:T(8,128)(2,1)S(1)}, u32[]{:S(2)}, u32[]{:S(2)}) collective-permute-start(bf16[256,1152]{1,0:T(8,128)(2,1)S(1)} %get-tuple-element.200), channel_id=1, source_target_pairs={{0,8},{8,16},{16,24},{24,28},{28,20},{20,12},{12,4},{4,0},{1,9},{9... | collective-permute-start | bytes 1769480 | tf_op jit(solution)/shard_map/ppermute | solution.py:100
  805.1 37.0 %collective-permute-start.124 = (bf16[256,2304]{1,0:T(8,128)(2,1)S(1)}, bf16[256,2304]{1,0:T(8,128)(2,1)S(1)}, u32[]{:S(2)}, u32[]{:S(2)}) collective-permute-start(bf16[256,2304]{1,0:T(8,128)(2,1)S(1)} %get-tuple-element.179), channel_id=1, source_target_pairs={{8,0},{16,8},{24,16},{28,24},{20,28},{12,20},{4,12},{0,4},{9,1},{1... | collective-permute-start | bytes 3538952 | tf_op jit(solution)/shard_map/ppermute | solution.py:99
  822.1 26.9 %collective-permute-start.125 = (bf16[256,2304]{1,0:T(8,128)(2,1)S(1)}, bf16[256,2304]{1,0:T(8,128)(2,1)S(1)}, u32[]{:S(2)}, u32[]{:S(2)}) collective-permute-start(bf16[256,2304]{1,0:T(8,128)(2,1)S(1)} %get-tuple-element.180), channel_id=1, source_target_pairs={{0,8},{8,16},{16,24},{24,28},{28,20},{20,12},{12,4},{4,0},{1,9},{9... | collective-permute-start | bytes 3538952 | tf_op jit(solution)/shard_map/ppermute | solution.py:100
  839.6 47.8 %collective-permute-start.142 = (bf16[256,1152]{1,0:T(8,128)(2,1)}, bf16[256,1152]{1,0:T(8,128)(2,1)}, u32[]{:S(2)}, u32[]{:S(2)}) collective-permute-start(bf16[256,1152]{1,0:T(8,128)(2,1)} %get-tuple-element.201), channel_id=1, source_target_pairs={{8,0},{16,8},{24,16},{28,24},{20,28},{12,20},{4,12},{0,4},{9,1},{1... | collective-permute-start | bytes 1769480 | tf_op jit(solution)/shard_map/ppermute | solution.py:99
  841.8 45.5 %collective-permute-start.143 = (bf16[256,1152]{1,0:T(8,128)(2,1)}, bf16[256,1152]{1,0:T(8,128)(2,1)}, u32[]{:S(2)}, u32[]{:S(2)}) collective-permute-start(bf16[256,1152]{1,0:T(8,128)(2,1)} %get-tuple-element.203), channel_id=1, source_target_pairs={{0,8},{8,16},{16,24},{24,28},{28,20},{20,12},{12,4},{4,0},{1,9},{9... | collective-permute-start | bytes 1769480 | tf_op jit(solution)/shard_map/ppermute | solution.py:100
  855.1 31.8 %collective-permute-start.127 = (bf16[256,2304]{1,0:T(8,128)(2,1)}, bf16[256,2304]{1,0:T(8,128)(2,1)}, u32[]{:S(2)}, u32[]{:S(2)}) collective-permute-start(bf16[256,2304]{1,0:T(8,128)(2,1)} %get-tuple-element.183), channel_id=1, source_target_pairs={{0,8},{8,16},{16,24},{24,28},{28,20},{20,12},{12,4},{4,0},{1,9},{9... | collective-permute-start | bytes 3538952 | tf_op jit(solution)/shard_map/ppermute | solution.py:100
  871.1 27.3 %collective-permute-start.100 = (bf16[128,1024]{1,0:T(8,128)(2,1)S(1)}, bf16[128,1024]{1,0:T(8,128)(2,1)S(1)}, u32[]{:S(2)}, u32[]{:S(2)}) collective-permute-start(bf16[128,1024]{1,0:T(8,128)(2,1)S(1)} %get-tuple-element.158), channel_id=1, source_target_pairs={{8,0},{16,8},{24,16},{28,24},{20,28},{12,20},{4,12},{0,4},{9,1},{1... | collective-permute-start | bytes 786440 | tf_op jit(solution)/shard_map/ppermute | solution.py:99
  902.0 37.3 %collective-permute-start.128 = (bf16[256,2304]{1,0:T(8,128)(2,1)}, bf16[256,2304]{1,0:T(8,128)(2,1)}, u32[]{:S(2)}, u32[]{:S(2)}) collective-permute-start(bf16[256,2304]{1,0:T(8,128)(2,1)} %get-tuple-element.185), channel_id=1, source_target_pairs={{8,0},{16,8},{24,16},{28,24},{20,28},{12,20},{4,12},{0,4},{9,1},{1... | collective-permute-start | bytes 3538952 | tf_op jit(solution)/shard_map/ppermute | solution.py:99
  904.9 43.2 %collective-permute-start.129 = (bf16[256,2304]{1,0:T(8,128)(2,1)}, bf16[256,2304]{1,0:T(8,128)(2,1)}, u32[]{:S(2)}, u32[]{:S(2)}) collective-permute-start(bf16[256,2304]{1,0:T(8,128)(2,1)} %get-tuple-element.187), channel_id=1, source_target_pairs={{0,8},{8,16},{16,24},{24,28},{28,20},{20,12},{12,4},{4,0},{1,9},{9... | collective-permute-start | bytes 3538952 | tf_op jit(solution)/shard_map/ppermute | solution.py:100
  919.6 31.5 %collective-permute-start.104 = (bf16[272,1024]{1,0:T(8,128)(2,1)}, bf16[272,1024]{1,0:T(8,128)(2,1)}, u32[]{:S(2)}, u32[]{:S(2)}) collective-permute-start(bf16[272,1024]{1,0:T(8,128)(2,1)} %get-tuple-element.162), channel_id=1, source_target_pairs={{8,0},{16,8},{24,16},{28,24},{20,28},{12,20},{4,12},{0,4},{9,1},{1... | collective-permute-start | bytes 1671176 | tf_op jit(solution)/shard_map/ppermute | solution.py:99
  922.5 31.6 %collective-permute-start.105 = (bf16[272,1024]{1,0:T(8,128)(2,1)}, bf16[272,1024]{1,0:T(8,128)(2,1)}, u32[]{:S(2)}, u32[]{:S(2)}) collective-permute-start(bf16[272,1024]{1,0:T(8,128)(2,1)} %get-tuple-element.163), channel_id=1, source_target_pairs={{0,8},{8,16},{16,24},{24,28},{28,20},{20,12},{12,4},{4,0},{1,9},{9... | collective-permute-start | bytes 1671176 | tf_op jit(solution)/shard_map/ppermute | solution.py:100
  927.8 72.0 %collective-permute-start.119 = (bf16[256,256]{1,0:T(8,128)(2,1)}, bf16[256,256]{1,0:T(8,128)(2,1)S(1)}, u32[]{:S(2)}, u32[]{:S(2)}) collective-permute-start(bf16[256,256]{1,0:T(8,128)(2,1)} %slice.674.refs_4_), channel_id=1, source_target_pairs={{0,1},{1,0},{2,3},{3,2},{4,5},{5,4},{6,7},{7,6},{8,9},{9,8},{10,11... | collective-permute-start | bytes 393224 | tf_op jit(solution)/shard_map/ppermute | solution.py:147
  939.2 60.6 %collective-permute-start.121 = (bf16[256,256]{1,0:T(8,128)(2,1)}, bf16[256,256]{1,0:T(8,128)(2,1)S(1)}, u32[]{:S(2)}, u32[]{:S(2)}) collective-permute-start(bf16[256,256]{1,0:T(8,128)(2,1)} %collective-permute-done.120.refs_6_), channel_id=1, source_target_pairs={{0,1},{1,0},{2,3},{3,2},{4,5},{5,4},{6,7},{7,6},{8,9},{9,8},{10,11... | collective-permute-start | bytes 393224 | tf_op jit(solution)/shard_map/ppermute | solution.py:147
  (382 other events, 5130.9 us)

commit v4 on v3

--- a/solution.py
+++ b/solution.py
@@ -993,7 +993,7 @@
         )
     first = attn_grad[0].sent
     for ring in (gate_up_grad[0], down_grad[0]):
-        for _ in range(ring.middle - 2):
+        for _ in range(ring.middle - 1):
             ring.advance()
     for rings in (attn_grad, gate_up_grad, down_grad):
         rings[:] = [

time: 1010 us -> 1020 us (level)
  waiting for transfers between devices: 395 us -> 423 us
  starting transfers between devices: 240 us -> 228 us
    ppermute x12, waiting for transfers between devices: 102 us -> 127 us  [partner(): return lax.ppermute(block, 'dp', [(i, i ^ 1 << bit) for i in range(count)])]
    ppermute x24, starting transfers between devices: 37.3 us -> 17.5 us  [send(): lax.ppermute(parts[0], 'dp', self.backward)]
    ppermute x24, waiting for transfers between devices: 33.2 us -> 15.9 us  [send(): lax.ppermute(parts[1], 'dp', self.forward)]
    ppermute x24, waiting for transfers between devices: 56.5 us -> 72.6 us  [send(): lax.ppermute(parts[0], 'dp', self.backward)]
    unnamed x623 -> x579, local copies, waits for them, and re-layouts: 56.5 us -> 50.9 us
  transfers between devices with their start and end apart: 154 -> 154, of which waited for: 65 -> 65; matrix products, arithmetic and copies ran while one was open for 8% -> 8% of each run, Pallas kernels for 21% -> 20%
where the time goes in v4:
time: 1020 us; the launch traced here: 1010 us
  waiting for transfers between devices  423 us (41%)
  starting transfers between devices  228 us (22%)
  Pallas kernels  224 us (22%)
  local copies, waits for them, and re-layouts  75.2 us (7%)
  other arithmetic  45.9 us (4%)
  between operations  15.3 us (2%)
    ppermute x46, starting transfers between devices, swap(): lax.ppermute(block, 'tensor', [(i, i ^ distance) for i in range(count)])  130 us
    ppermute x12, waiting for transfers between devices, partner(): return lax.ppermute(block, 'dp', [(i, i ^ 1 << bit) for i in range(count)])  127 us
    ppermute x18, waiting for transfers between devices, ring_gather(): ahead.append(lax.ppermute(ahead[-1], 'dp', forward))  116 us
    ppermute x24, waiting for transfers between devices, send(): lax.ppermute(parts[0], 'dp', self.backward)  72.6 us
    pallas_call x30, Pallas kernels, chunk(): pl.pallas_call(kernel, grid=(len(plan),), in_specs=in_specs, out_shape=[s...  55.2 us
    pallas_call x8, Pallas kernels, gathered_call(): pl.pallas_call(kernel, grid=(steps,), in_specs=[in_smem] + [in_hbm] * (le...  53.3 us
    unnamed x579, local copies, waits for them, and re-layouts  50.9 us
    pallas_call x8, Pallas kernels, spread_call(): pl.pallas_call(kernel, grid=(groups,), in_specs=[in_smem] + [in_hbm] * le...  48.9 us
  transfers between devices with their start and end apart: 154, of which 65 were waited for; matrix products, arithmetic and copies ran while one was open for 8% of the time, Pallas kernels for 20%

profile of v4, /device:TPU:1, one launch (start us, length us, event | category | flops | bytes accessed | tf_op | source)
XLA Modules:
  0.0 1011.1 jit_solution(10939380047164094079)
XLA Ops:
  25.3 7.5 collective-permute-done.5.refs_11_.refs_7_
  36.3 7.9 collective-permute-done.6.refs_10_.refs_6_
  56.7 5.1 collective-permute-start.8
  61.9 5.0 collective-permute-start.10
  78.8 4.2 queries_keys_values.2
  85.5 11.3 %collective-permute-done.11 = bf16[4,2,64,256]{3,2,1,0:T(8,128)(2,1)S(1)} collective-permute-done((bf16[4,2,64,256]{3,2,1,0:T(8,128)(2,1)S(1)}, bf16[4,2,64,256]{3,2,1,0:T(8,128)(2,1)S(1)}, u32[]{:S(2)}, u32[]{:S(2)}) %collective-permute-start.11) | collective-permute-done | bytes 262176 | tf_op jit(solution)/shard_map/ppermute | solution.py:164
  99.2 4.0 collective-permute-done.12
  109.1 19.4 %collective-permute-done.16.refs_5_.refs_1_ = bf16[256,2304]{1,0:T(8,128)(2,1)} collective-permute-done((bf16[256,2304]{1,0:T(8,128)(2,1)S(1)}, bf16[256,2304]{1,0:T(8,128)(2,1)}, u32[]{:S(2)}, u32[]{:S(2)}) %collective-permute-start.16) | collective-permute-done | bytes 1179680 | tf_op jit(solution)/shard_map/ppermute | solution.py:72
  130.0 6.5 collective-permute-done.13
  138.6 14.6 %attend.2 = (bf16[4,2,64,384]{3,2,1,0:T(8,128)(2,1)S(1)}, bf16[2,6,1024,256]{3,2,1,0:T(8,128)(2,1)}, bf16[2,6,256,256]{3,2,1,0:T(8,128)(2,1)}) custom-call(s32[1]{0:T(128)} %bitcast.14.odd_ref, bf16[4,2,64,384]{3,2,1,0:T(8,128)(2,1)S(1)} %bitcast.233, bf16[16,2,64,256]{3,2,1,0:T(8,128)(2,1)S(1)} %pad_maximum_fusion.5.pk_ref.pv_ref, ...), custom_call_target="tpu_custom_call" | custom-call | flops 41999998976 | bytes 1024 | tf_op jit(solution)/shard_map/attend/pallas_call | solution.py:611
  153.2 6.6 collective-permute-done.17.refs_6_.refs_2_
  162.1 5.2 out.2
  171.8 14.1 %collective-permute-done.18.refs_7_.refs_3_ = bf16[256,2304]{1,0:T(8,128)(2,1)S(1)} collective-permute-done((bf16[256,2304]{1,0:T(8,128)(2,1)}, bf16[256,2304]{1,0:T(8,128)(2,1)S(1)}, u32[]{:S(2)}, u32[]{:S(2)}) %collective-permute-start.18) | collective-permute-done | bytes 1179680 | tf_op jit(solution)/shard_map/ppermute | solution.py:72
  192.5 7.5 collective-permute-done.22.refs_1_.refs_5_
  204.5 8.2 collective-permute-done.23.refs_2_.refs_6_
  222.6 6.7 collective-permute-start.30
  229.3 4.4 collective-permute-start.32
  240.5 10.7 %active.2 = (bf16[512,1152]{1,0:T(8,128)(2,1)S(1)}, bf16[512,1152]{1,0:T(8,128)(2,1)S(1)}, bf16[512,1152]{1,0:T(8,128)(2,1)}) custom-call(s32[8]{0:T(128)S(1)} %select_reduce_fusion.1.source_ref, bf16[128,2048]{1,0:T(8,128)(2,1)S(1)} %multiply_convert_fusion.2.refs_0_.refs_4_, bf16[128,2048]{1,0:T(8,128)(2,1)S(1)} %collective-permute-done.30.refs_1_.refs_5_, ...), custom_call_target="tpu_custom_call" | custom-call | flops 27000000512 | bytes 1024 | tf_op jit(solution)/shard_map/active/pallas_call | solution.py:288
  251.4 6.4 down.2
  257.8 9.0 collective-permute-start.35
  273.1 10.5 %collective-permute-done.37.refs_5_.refs_1_ = bf16[256,1024]{1,0:T(8,128)(2,1)S(1)} collective-permute-done((bf16[256,1024]{1,0:T(8,128)(2,1)S(1)}, bf16[256,1024]{1,0:T(8,128)(2,1)S(1)}, u32[]{:S(2)}, u32[]{:S(2)}) %collective-permute-start.37) | collective-permute-done | bytes 524320 | tf_op jit(solution)/shard_map/ppermute | solution.py:72
  288.6 7.7 collective-permute-done.38.refs_6_.refs_2_
  302.6 5.4 collective-permute-done.39.refs_7_.refs_3_
  315.0 4.1 queries_keys_values.3
  323.0 10.3 %collective-permute-done.48 = bf16[4,2,64,256]{3,2,1,0:T(8,128)(2,1)S(1)} collective-permute-done((bf16[4,2,64,256]{3,2,1,0:T(8,128)(2,1)S(1)}, bf16[4,2,64,256]{3,2,1,0:T(8,128)(2,1)S(1)}, u32[]{:S(2)}, u32[]{:S(2)}) %collective-permute-start.48) | collective-permute-done | bytes 262176 | tf_op jit(solution)/shard_map/ppermute | solution.py:164
  333.5 17.1 %collective-permute-done.49 = bf16[4,2,64,256]{3,2,1,0:T(8,128)(2,1)S(1)} collective-permute-done((bf16[4,2,64,256]{3,2,1,0:T(8,128)(2,1)S(1)}, bf16[4,2,64,256]{3,2,1,0:T(8,128)(2,1)S(1)}, u32[]{:S(2)}, u32[]{:S(2)}) %collective-permute-start.49) | collective-permute-done | bytes 262176 | tf_op jit(solution)/shard_map/ppermute | solution.py:164
  350.8 6.5 collective-permute-start.54
  362.5 14.6 %attend.3 = (bf16[4,2,64,384]{3,2,1,0:T(8,128)(2,1)S(1)}, bf16[2,6,1024,256]{3,2,1,0:T(8,128)(2,1)}, bf16[2,6,256,256]{3,2,1,0:T(8,128)(2,1)}) custom-call(s32[1]{0:T(128)} %bitcast.14.odd_ref, bf16[4,2,64,384]{3,2,1,0:T(8,128)(2,1)S(1)} %bitcast.235, bf16[16,2,64,256]{3,2,1,0:T(8,128)(2,1)S(1)} %pad_maximum_fusion.6.pk_ref.pv_ref, ...), custom_call_target="tpu_custom_call" | custom-call | flops 41999998976 | bytes 1024 | tf_op jit(solution)/shard_map/attend/pallas_call | solution.py:611
  381.8 10.7 %collective-permute-start.51 = (bf16[2,128,2048]{2,1,0:T(8,128)(2,1)S(1)}, bf16[2,128,2048]{2,1,0:T(8,128)(2,1)S(1)}, u32[]{:S(2)}, u32[]{:S(2)}) collective-permute-start(bf16[2,128,2048]{2,1,0:T(8,128)(2,1)S(1)} %get-tuple-element.125), channel_id=1, source_target_pairs={{0,1},{1,0},{2,3},{3,2},{4,5},{5,4},{6,7},{7,6},{8,9},{9,8},{10,11... | collective-permute-start | bytes 3145736 | tf_op jit(solution)/shard_map/ppermute | solution.py:147
  397.8 22.6 %collective-permute-done.55.refs_7_.refs_3_ = bf16[256,2304]{1,0:T(8,128)(2,1)} collective-permute-done((bf16[256,2304]{1,0:T(8,128)(2,1)}, bf16[256,2304]{1,0:T(8,128)(2,1)}, u32[]{:S(2)}, u32[]{:S(2)}) %collective-permute-start.55) | collective-permute-done | bytes 1179680 | tf_op jit(solution)/shard_map/ppermute | solution.py:72
  427.9 6.6 collective-permute-done.59.refs_1_.refs_5_
  436.8 10.4 %collective-permute-done.70.refs_8_.refs_4_ = bf16[128,2304]{1,0:T(8,128)(2,1)S(1)} collective-permute-done((bf16[128,2304]{1,0:T(8,128)(2,1)S(1)}, bf16[128,2304]{1,0:T(8,128)(2,1)S(1)}, u32[]{:S(2)}, u32[]{:S(2)}) %collective-permute-start.70) | collective-permute-done | bytes 589856 | tf_op jit(solution)/shard_map/ppermute | solution.py:76
  452.0 7.9 collective-permute-done.60.refs_2_.refs_6_
  461.4 10.7 %active.3 = (bf16[512,1152]{1,0:T(8,128)(2,1)S(1)}, bf16[512,1152]{1,0:T(8,128)(2,1)S(1)}, bf16[512,1152]{1,0:T(8,128)(2,1)}) custom-call(s32[8]{0:T(128)S(1)} %select_reduce_fusion.1.source_ref, bf16[128,2048]{1,0:T(8,128)(2,1)S(1)} %multiply_convert_fusion.refs_0_.refs_4_, bf16[128,2048]{1,0:T(8,128)(2,1)S(1)} %collective-permute-done.67.refs_1_.refs_5_, ...), custom_call_target="tpu_custom_call" | custom-call | flops 27000000512 | bytes 1024 | tf_op jit(solution)/shard_map/active/pallas_call | solution.py:288
  490.6 9.0 active_back.2.refs_9_.refs_4_.refs_8_
  501.3 8.6 ffn_back.2
  509.9 4.0 collective-permute-start.77
  513.9 6.1 down.3
  528.0 7.8 collective-permute-done.78
  537.0 10.1 collective-permute-done.73
  570.4 16.8 %attend_back.2 = (f32[4,2,64,384]{3,2,1,0:T(8,128)S(1)}, f32[16,2,64,256]{3,2,1,0:T(8,128)S(1)}, f32[4,2,64,256]{3,2,1,0:T(8,128)S(1)}) custom-call(s32[1]{0:T(128)} %bitcast.14.odd_ref, bf16[4,2,64,384]{3,2,1,0:T(8,128)(2,1)S(1)} %bitcast.238, bf16[4,2,64,384]{3,2,1,0:T(8,128)(2,1)S(1)} %bitcast.236, bf16[16,2,64,256]{3,2,1,0:T(8,128)(2,1)S(1)} %copy-done.7, ...), custom_call_target="tpu_custom_call" | custom-call | flops 48000000000 | bytes 1024 | tf_op jit(solution)/shard_map/attend_back/pallas_call | solution.py:646
  592.9 9.1 collective-permute-done.82
  609.0 12.2 %collective-permute-done.84 = bf16[4,2,64,256]{3,2,1,0:T(8,128)(2,1)S(1)} collective-permute-done((bf16[4,2,64,256]{3,2,1,0:T(8,128)(2,1)S(1)}, bf16[4,2,64,256]{3,2,1,0:T(8,128)(2,1)S(1)}, u32[]{:S(2)}, u32[]{:S(2)}) %collective-permute-start.84) | collective-permute-done | bytes 262176 | tf_op jit(solution)/shard_map/ppermute | solution.py:164
  622.4 5.3 normed_back.2
  642.2 18.6 %collective-permute-done.134.refs_9_ = bf16[256,2304]{1,0:T(8,128)(2,1)S(1)} collective-permute-done((bf16[256,2304]{1,0:T(8,128)(2,1)S(1)}, bf16[256,2304]{1,0:T(8,128)(2,1)S(1)}, u32[]{:S(2)}, u32[]{:S(2)}) %collective-permute-start.134) | collective-permute-done | bytes 1179680 | tf_op jit(solution)/shard_map/ppermute | solution.py:99
  681.4 16.0 %collective-permute-done.136.refs_5_ = bf16[256,2304]{1,0:T(8,128)(2,1)S(1)} collective-permute-done((bf16[256,2304]{1,0:T(8,128)(2,1)S(1)}, bf16[256,2304]{1,0:T(8,128)(2,1)S(1)}, u32[]{:S(2)}, u32[]{:S(2)}) %collective-permute-start.136) | collective-permute-done | bytes 1179680 | tf_op jit(solution)/shard_map/ppermute | solution.py:99
  700.9 5.7 collective-permute-start.87
  713.7 8.5 active_back.3.refs_9_.refs_4_.refs_8_
  726.6 8.3 ffn_back.3
  747.4 7.6 collective-permute-done.91
  782.3 16.8 %attend_back.3 = (f32[4,2,64,384]{3,2,1,0:T(8,128)S(1)}, f32[16,2,64,256]{3,2,1,0:T(8,128)S(1)}, f32[4,2,64,256]{3,2,1,0:T(8,128)S(1)}) custom-call(s32[1]{0:T(128)} %bitcast.14.odd_ref, bf16[4,2,64,384]{3,2,1,0:T(8,128)(2,1)S(1)} %bitcast.237, bf16[4,2,64,384]{3,2,1,0:T(8,128)(2,1)S(1)} %bitcast.234, bf16[16,2,64,256]{3,2,1,0:T(8,128)(2,1)S(1)} %copy-done.5, ...), custom_call_target="tpu_custom_call" | custom-call | flops 48000000000 | bytes 1024 | tf_op jit(solution)/shard_map/attend_back/pallas_call | solution.py:646
  801.9 10.4 %collective-permute-done.95 = bf16[8,2,64,256]{3,2,1,0:T(8,128)(2,1)S(1)} collective-permute-done((bf16[8,2,64,256]{3,2,1,0:T(8,128)(2,1)S(1)}, bf16[8,2,64,256]{3,2,1,0:T(8,128)(2,1)S(1)}, u32[]{:S(2)}, u32[]{:S(2)}) %collective-permute-start.95) | collective-permute-done | bytes 524320 | tf_op jit(solution)/shard_map/ppermute | solution.py:164
  815.3 27.7 %collective-permute-done.96 = bf16[4,2,64,256]{3,2,1,0:T(8,128)(2,1)S(1)} collective-permute-done((bf16[4,2,64,256]{3,2,1,0:T(8,128)(2,1)S(1)}, bf16[4,2,64,256]{3,2,1,0:T(8,128)(2,1)S(1)}, u32[]{:S(2)}, u32[]{:S(2)}) %collective-permute-start.96) | collective-permute-done | bytes 262176 | tf_op jit(solution)/shard_map/ppermute | solution.py:164
  847.2 10.7 %collective-permute-done.97 = bf16[4,2,64,256]{3,2,1,0:T(8,128)(2,1)S(1)} collective-permute-done((bf16[4,2,64,256]{3,2,1,0:T(8,128)(2,1)S(1)}, bf16[4,2,64,256]{3,2,1,0:T(8,128)(2,1)S(1)}, u32[]{:S(2)}, u32[]{:S(2)}) %collective-permute-start.97) | collective-permute-done | bytes 262176 | tf_op jit(solution)/shard_map/ppermute | solution.py:164
  859.5 5.3 normed_back.3
  864.8 7.3 collective-permute-start.98
  886.5 5.6 collective-permute-done.99
  902.0 12.3 %collective-permute-done.128.refs_5_ = bf16[256,2304]{1,0:T(8,128)(2,1)} collective-permute-done((bf16[256,2304]{1,0:T(8,128)(2,1)}, bf16[256,2304]{1,0:T(8,128)(2,1)}, u32[]{:S(2)}, u32[]{:S(2)}) %collective-permute-start.128) | collective-permute-done | bytes 1179680 | tf_op jit(solution)/shard_map/ppermute | solution.py:99
  914.3 6.3 collective-permute-done.129.refs_6_
  933.0 6.8 collective-permute-done.102.refs_19_
  947.8 6.9 collective-permute-done.104.refs_19_
  959.9 16.3 %collective-permute-start.119 = (bf16[256,256]{1,0:T(8,128)(2,1)}, bf16[256,256]{1,0:T(8,128)(2,1)S(1)}, u32[]{:S(2)}, u32[]{:S(2)}) collective-permute-start(bf16[256,256]{1,0:T(8,128)(2,1)} %slice.674.refs_4_), channel_id=1, source_target_pairs={{0,1},{1,0},{2,3},{3,2},{4,5},{5,4},{6,7},{7,6},{8,9},{9,8},{10,11... | collective-permute-start | bytes 393224 | tf_op jit(solution)/shard_map/ppermute | solution.py:147
  984.7 4.5 collective-permute-start.108
  990.4 5.2 collective-permute-start.110
  (1018 shorter events, 391.0 us)
Async XLA Ops:
  97.8 30.7 %collective-permute-start.16 = (bf16[256,2304]{1,0:T(8,128)(2,1)S(1)}, bf16[256,2304]{1,0:T(8,128)(2,1)}, u32[]{:S(2)}, u32[]{:S(2)}) collective-permute-start(bf16[256,2304]{1,0:T(8,128)(2,1)S(1)} %pad_maximum_fusion.3.refs_4_.refs_0_), channel_id=1, source_target_pairs={{0,8},{8,16},{16,24},{24,28},{28,20},{20,12},{12,4},{4,0},{1,9},{9... | collective-permute-start | bytes 3538952 | tf_op jit(solution)/shard_map/ppermute | solution.py:72
  98.7 29.8 %collective-permute-start.19 = (bf16[256,2304]{1,0:T(8,128)(2,1)S(1)}, bf16[256,2304]{1,0:T(8,128)(2,1)}, u32[]{:S(2)}, u32[]{:S(2)}) collective-permute-start(bf16[256,2304]{1,0:T(8,128)(2,1)S(1)} %pad_maximum_fusion.3.refs_4_.refs_0_), channel_id=1, source_target_pairs={{8,0},{16,8},{24,16},{28,24},{20,28},{12,20},{4,12},{0,4},{9,1},{1... | collective-permute-start | bytes 3538952 | tf_op jit(solution)/shard_map/ppermute | solution.py:73
  104.1 32.3 %collective-permute-start.13 = (bf16[8,2,64,256]{3,2,1,0:T(8,128)(2,1)}, bf16[8,2,64,256]{3,2,1,0:T(8,128)(2,1)}, u32[]{:S(2)}, u32[]{:S(2)}) collective-permute-start(bf16[8,2,64,256]{3,2,1,0:T(8,128)(2,1)} %pad_maximum_fusion.11), channel_id=1, source_target_pairs={{0,8},{4,12},{8,0},{12,4},{16,24},{20,28},{24,16},{28,20},{1,9},{5... | collective-permute-start | bytes 1572872 | tf_op jit(solution)/shard_map/ppermute | solution.py:164
  128.5 31.3 %collective-permute-start.17 = (bf16[256,2304]{1,0:T(8,128)(2,1)}, bf16[256,2304]{1,0:T(8,128)(2,1)}, u32[]{:S(2)}, u32[]{:S(2)}) collective-permute-start(bf16[256,2304]{1,0:T(8,128)(2,1)} %collective-permute-done.16.refs_5_.refs_1_), channel_id=1, source_target_pairs={{0,8},{8,16},{16,24},{24,28},{28,20},{20,12},{12,4},{4,0},{1,9},{9... | collective-permute-start | bytes 3538952 | tf_op jit(solution)/shard_map/ppermute | solution.py:72
  128.5 33.5 %collective-permute-start.20 = (bf16[256,2304]{1,0:T(8,128)(2,1)}, bf16[256,2304]{1,0:T(8,128)(2,1)}, u32[]{:S(2)}, u32[]{:S(2)}) collective-permute-start(bf16[256,2304]{1,0:T(8,128)(2,1)} %collective-permute-done.19.refs_12_.refs_8_), channel_id=1, source_target_pairs={{8,0},{16,8},{24,16},{28,24},{20,28},{12,20},{4,12},{0,4},{9,1},{1... | collective-permute-start | bytes 3538952 | tf_op jit(solution)/shard_map/ppermute | solution.py:73
  159.8 26.1 %collective-permute-start.18 = (bf16[256,2304]{1,0:T(8,128)(2,1)}, bf16[256,2304]{1,0:T(8,128)(2,1)S(1)}, u32[]{:S(2)}, u32[]{:S(2)}) collective-permute-start(bf16[256,2304]{1,0:T(8,128)(2,1)} %collective-permute-done.17.refs_6_.refs_2_), channel_id=1, source_target_pairs={{0,8},{8,16},{16,24},{24,28},{28,20},{20,12},{12,4},{4,0},{1,9},{9... | collective-permute-start | bytes 3538952 | tf_op jit(solution)/shard_map/ppermute | solution.py:72
  162.0 25.8 %collective-permute-start.21 = (bf16[256,2304]{1,0:T(8,128)(2,1)}, bf16[256,2304]{1,0:T(8,128)(2,1)}, u32[]{:S(2)}, u32[]{:S(2)}) collective-permute-start(bf16[256,2304]{1,0:T(8,128)(2,1)} %collective-permute-done.20.refs_11_.refs_7_), channel_id=1, source_target_pairs={{8,0},{16,8},{24,16},{28,24},{20,28},{12,20},{4,12},{0,4},{9,1},{1... | collective-permute-start | bytes 3538952 | tf_op jit(solution)/shard_map/ppermute | solution.py:73
  167.4 22.7 %collective-permute-start.14 = (bf16[2,128,2048]{2,1,0:T(8,128)(2,1)}, bf16[2,128,2048]{2,1,0:T(8,128)(2,1)}, u32[]{:S(2)}, u32[]{:S(2)}) collective-permute-start(bf16[2,128,2048]{2,1,0:T(8,128)(2,1)} %get-tuple-element.114), channel_id=1, source_target_pairs={{0,1},{1,0},{2,3},{3,2},{4,5},{5,4},{6,7},{7,6},{8,9},{9,8},{10,11... | collective-permute-start | bytes 3145736 | tf_op jit(solution)/shard_map/ppermute | solution.py:147
  321.5 29.3 %collective-permute-start.53 = (bf16[256,2304]{1,0:T(8,128)(2,1)S(1)}, bf16[256,2304]{1,0:T(8,128)(2,1)S(1)}, u32[]{:S(2)}, u32[]{:S(2)}) collective-permute-start(bf16[256,2304]{1,0:T(8,128)(2,1)S(1)} %pad_maximum_fusion.4.refs_4_.refs_0_), channel_id=1, source_target_pairs={{0,8},{8,16},{16,24},{24,28},{28,20},{20,12},{12,4},{4,0},{1,9},{9... | collective-permute-start | bytes 3538952 | tf_op jit(solution)/shard_map/ppermute | solution.py:72
  321.8 35.5 %collective-permute-start.56 = (bf16[256,2304]{1,0:T(8,128)(2,1)S(1)}, bf16[256,2304]{1,0:T(8,128)(2,1)S(1)}, u32[]{:S(2)}, u32[]{:S(2)}) collective-permute-start(bf16[256,2304]{1,0:T(8,128)(2,1)S(1)} %pad_maximum_fusion.4.refs_4_.refs_0_), channel_id=1, source_target_pairs={{8,0},{16,8},{24,16},{28,24},{20,28},{12,20},{4,12},{0,4},{9,1},{1... | collective-permute-start | bytes 3538952 | tf_op jit(solution)/shard_map/ppermute | solution.py:73
  350.8 41.6 %collective-permute-start.54 = (bf16[256,2304]{1,0:T(8,128)(2,1)S(1)}, bf16[256,2304]{1,0:T(8,128)(2,1)}, u32[]{:S(2)}, u32[]{:S(2)}) collective-permute-start(bf16[256,2304]{1,0:T(8,128)(2,1)S(1)} %collective-permute-done.53.refs_5_.refs_1_), channel_id=1, source_target_pairs={{0,8},{8,16},{16,24},{24,28},{28,20},{20,12},{12,4},{4,0},{1,9},{9... | collective-permute-start | bytes 3538952 | tf_op jit(solution)/shard_map/ppermute | solution.py:72
  357.3 35.2 %collective-permute-start.57 = (bf16[256,2304]{1,0:T(8,128)(2,1)S(1)}, bf16[256,2304]{1,0:T(8,128)(2,1)}, u32[]{:S(2)}, u32[]{:S(2)}) collective-permute-start(bf16[256,2304]{1,0:T(8,128)(2,1)S(1)} %collective-permute-done.56.refs_12_.refs_8_), channel_id=1, source_target_pairs={{8,0},{16,8},{24,16},{28,24},{20,28},{12,20},{4,12},{0,4},{9,1},{1... | collective-permute-start | bytes 3538952 | tf_op jit(solution)/shard_map/ppermute | solution.py:73
  392.5 27.9 %collective-permute-start.55 = (bf16[256,2304]{1,0:T(8,128)(2,1)}, bf16[256,2304]{1,0:T(8,128)(2,1)}, u32[]{:S(2)}, u32[]{:S(2)}) collective-permute-start(bf16[256,2304]{1,0:T(8,128)(2,1)} %collective-permute-done.54.refs_6_.refs_2_), channel_id=1, source_target_pairs={{0,8},{8,16},{16,24},{24,28},{28,20},{20,12},{12,4},{4,0},{1,9},{9... | collective-permute-start | bytes 3538952 | tf_op jit(solution)/shard_map/ppermute | solution.py:72
  392.5 28.0 %collective-permute-start.58 = (bf16[256,2304]{1,0:T(8,128)(2,1)}, bf16[256,2304]{1,0:T(8,128)(2,1)}, u32[]{:S(2)}, u32[]{:S(2)}) collective-permute-start(bf16[256,2304]{1,0:T(8,128)(2,1)} %collective-permute-done.57.refs_11_.refs_7_), channel_id=1, source_target_pairs={{8,0},{16,8},{24,16},{28,24},{20,28},{12,20},{4,12},{0,4},{9,1},{1... | collective-permute-start | bytes 3538952 | tf_op jit(solution)/shard_map/ppermute | solution.py:73
  395.8 27.4 %collective-permute-start.52 = (bf16[128,2048]{1,0:T(8,128)(2,1)}, bf16[128,2048]{1,0:T(8,128)(2,1)}, u32[]{:S(2)}, u32[]{:S(2)}) collective-permute-start(bf16[128,2048]{1,0:T(8,128)(2,1)} %fusion.22), channel_id=1, source_target_pairs={{0,2},{1,3},{2,0},{3,1},{4,6},{5,7},{6,4},{7,5},{8,10},{9,11},{10,... | collective-permute-start | bytes 1572872 | tf_op jit(solution)/shard_map/ppermute | solution.py:147
  396.3 30.3 %collective-permute-start.75 = (bf16[128,2048]{1,0:T(8,128)(2,1)S(1)}, bf16[128,2048]{1,0:T(8,128)(2,1)}, u32[]{:S(2)}, u32[]{:S(2)}) collective-permute-start(bf16[128,2048]{1,0:T(8,128)(2,1)S(1)} %constant_dynamic-update-slice_fusion.8.refs_0_.refs_4_), channel_id=1, source_target_pairs={{0,2},{1,3},{2,0},{3,1},{4,6},{5,7},{6,4},{7,5},{8,10},{9,11},{10,... | collective-permute-start | bytes 1572872 | tf_op jit(solution)/shard_map/ppermute | solution.py:147
  423.0 24.1 %collective-permute-start.70 = (bf16[128,2304]{1,0:T(8,128)(2,1)S(1)}, bf16[128,2304]{1,0:T(8,128)(2,1)S(1)}, u32[]{:S(2)}, u32[]{:S(2)}) collective-permute-start(bf16[128,2304]{1,0:T(8,128)(2,1)S(1)} %slice.506), channel_id=1, source_target_pairs={{0,8},{8,16},{16,24},{24,28},{28,20},{20,12},{12,4},{4,0},{1,9},{9... | collective-permute-start | bytes 1769480 | tf_op jit(solution)/shard_map/ppermute | solution.py:76
  425.0 25.1 %collective-permute-start.68 = (bf16[128,2048]{1,0:T(8,128)(2,1)S(1)}, bf16[128,2048]{1,0:T(8,128)(2,1)S(1)}, u32[]{:S(2)}, u32[]{:S(2)}) collective-permute-start(bf16[128,2048]{1,0:T(8,128)(2,1)S(1)} %multiply_convert_fusion.refs_0_.refs_4_), channel_id=1, source_target_pairs={{0,2},{1,3},{2,0},{3,1},{4,6},{5,7},{6,4},{7,5},{8,10},{9,11},{10,... | collective-permute-start | bytes 1572872 | tf_op jit(solution)/shard_map/ppermute | solution.py:147
  426.6 23.6 %collective-permute-start.71 = (bf16[128,2304]{1,0:T(8,128)(2,1)S(1)}, bf16[128,2304]{1,0:T(8,128)(2,1)S(1)}, u32[]{:S(2)}, u32[]{:S(2)}) collective-permute-start(bf16[128,2304]{1,0:T(8,128)(2,1)S(1)} %slice.507), channel_id=1, source_target_pairs={{8,0},{16,8},{24,16},{28,24},{20,28},{12,20},{4,12},{0,4},{9,1},{1... | collective-permute-start | bytes 1769480 | tf_op jit(solution)/shard_map/ppermute | solution.py:77
  434.5 25.4 %collective-permute-start.60 = (bf16[256,1152]{1,0:T(8,128)(2,1)S(1)}, bf16[256,1152]{1,0:T(8,128)(2,1)}, u32[]{:S(2)}, u32[]{:S(2)}) collective-permute-start(bf16[256,1152]{1,0:T(8,128)(2,1)S(1)} %collective-permute-done.59.refs_1_.refs_5_), channel_id=1, source_target_pairs={{0,8},{8,16},{16,24},{24,28},{28,20},{20,12},{12,4},{4,0},{1,9},{9... | collective-permute-start | bytes 1769480 | tf_op jit(solution)/shard_map/ppermute | solution.py:72
  435.7 24.6 %collective-permute-start.64 = (bf16[256,1152]{1,0:T(8,128)(2,1)S(1)}, bf16[256,1152]{1,0:T(8,128)(2,1)}, u32[]{:S(2)}, u32[]{:S(2)}) collective-permute-start(bf16[256,1152]{1,0:T(8,128)(2,1)S(1)} %collective-permute-done.63.refs_8_.refs_12_), channel_id=1, source_target_pairs={{8,0},{16,8},{24,16},{28,24},{20,28},{12,20},{4,12},{0,4},{9,1},{1... | collective-permute-start | bytes 1769480 | tf_op jit(solution)/shard_map/ppermute | solution.py:73
  459.9 22.6 %collective-permute-start.61 = (bf16[256,1152]{1,0:T(8,128)(2,1)}, bf16[256,1152]{1,0:T(8,128)(2,1)S(1)}, u32[]{:S(2)}, u32[]{:S(2)}) collective-permute-start(bf16[256,1152]{1,0:T(8,128)(2,1)} %collective-permute-done.60.refs_2_.refs_6_), channel_id=1, source_target_pairs={{0,8},{8,16},{16,24},{24,28},{28,20},{20,12},{12,4},{4,0},{1,9},{9... | collective-permute-start | bytes 1769480 | tf_op jit(solution)/shard_map/ppermute | solution.py:72
  460.3 22.7 %collective-permute-start.65 = (bf16[256,1152]{1,0:T(8,128)(2,1)}, bf16[256,1152]{1,0:T(8,128)(2,1)S(1)}, u32[]{:S(2)}, u32[]{:S(2)}) collective-permute-start(bf16[256,1152]{1,0:T(8,128)(2,1)} %collective-permute-done.64.refs_7_.refs_11_), channel_id=1, source_target_pairs={{8,0},{16,8},{24,16},{28,24},{20,28},{12,20},{4,12},{0,4},{9,1},{1... | collective-permute-start | bytes 1769480 | tf_op jit(solution)/shard_map/ppermute | solution.py:73
  488.9 35.0 %collective-permute-start.148 = (bf16[256,1152]{1,0:T(8,128)(2,1)}, bf16[256,1152]{1,0:T(8,128)(2,1)S(1)}, u32[]{:S(2)}, u32[]{:S(2)}) collective-permute-start(bf16[256,1152]{1,0:T(8,128)(2,1)} %get-tuple-element.203), channel_id=1, source_target_pairs={{8,0},{16,8},{24,16},{28,24},{20,28},{12,20},{4,12},{0,4},{9,1},{1... | collective-permute-start | bytes 1769480 | tf_op jit(solution)/shard_map/ppermute | solution.py:99
  489.7 35.4 %collective-permute-start.149 = (bf16[256,1152]{1,0:T(8,128)(2,1)S(1)}, bf16[256,1152]{1,0:T(8,128)(2,1)S(1)}, u32[]{:S(2)}, u32[]{:S(2)}) collective-permute-start(bf16[256,1152]{1,0:T(8,128)(2,1)S(1)} %get-tuple-element.204), channel_id=1, source_target_pairs={{0,8},{8,16},{16,24},{24,28},{28,20},{20,12},{12,4},{4,0},{1,9},{9... | collective-permute-start | bytes 1769480 | tf_op jit(solution)/shard_map/ppermute | solution.py:100
  521.6 27.9 %collective-permute-start.130 = (bf16[128,2304]{1,0:T(8,128)(2,1)S(1)}, bf16[128,2304]{1,0:T(8,128)(2,1)S(1)}, u32[]{:S(2)}, u32[]{:S(2)}) collective-permute-start(bf16[128,2304]{1,0:T(8,128)(2,1)S(1)} %get-tuple-element.183), channel_id=1, source_target_pairs={{8,0},{16,8},{24,16},{28,24},{20,28},{12,20},{4,12},{0,4},{9,1},{1... | collective-permute-start | bytes 1769480 | tf_op jit(solution)/shard_map/ppermute | solution.py:99
  522.8 26.7 %collective-permute-start.131 = (bf16[128,2304]{1,0:T(8,128)(2,1)S(1)}, bf16[128,2304]{1,0:T(8,128)(2,1)S(1)}, u32[]{:S(2)}, u32[]{:S(2)}) collective-permute-start(bf16[128,2304]{1,0:T(8,128)(2,1)S(1)} %get-tuple-element.184), channel_id=1, source_target_pairs={{0,8},{8,16},{16,24},{24,28},{28,20},{20,12},{12,4},{4,0},{1,9},{9... | collective-permute-start | bytes 1769480 | tf_op jit(solution)/shard_map/ppermute | solution.py:100
  523.9 23.2 %collective-permute-start.73 = (bf16[128,2048]{1,0:T(8,128)(2,1)S(1)}, bf16[128,2048]{1,0:T(8,128)(2,1)S(1)}, u32[]{:S(2)}, u32[]{:S(2)}) collective-permute-start(bf16[128,2048]{1,0:T(8,128)(2,1)S(1)} %fusion.23), channel_id=1, source_target_pairs={{0,2},{1,3},{2,0},{3,1},{4,6},{5,7},{6,4},{7,5},{8,10},{9,11},{10,... | collective-permute-start | bytes 1572872 | tf_op jit(solution)/shard_map/ppermute | solution.py:147
  526.9 27.4 %collective-permute-start.150 = (bf16[256,1152]{1,0:T(8,128)(2,1)S(1)}, bf16[256,1152]{1,0:T(8,128)(2,1)S(1)}, u32[]{:S(2)}, u32[]{:S(2)}) collective-permute-start(bf16[256,1152]{1,0:T(8,128)(2,1)S(1)} %get-tuple-element.205), channel_id=1, source_target_pairs={{8,0},{16,8},{24,16},{28,24},{20,28},{12,20},{4,12},{0,4},{9,1},{1... | collective-permute-start | bytes 1769480 | tf_op jit(solution)/shard_map/ppermute | solution.py:99
  535.8 27.7 %collective-permute-start.151 = (bf16[256,1152]{1,0:T(8,128)(2,1)S(1)}, bf16[256,1152]{1,0:T(8,128)(2,1)S(1)}, u32[]{:S(2)}, u32[]{:S(2)}) collective-permute-start(bf16[256,1152]{1,0:T(8,128)(2,1)S(1)} %get-tuple-element.206), channel_id=1, source_target_pairs={{0,8},{8,16},{16,24},{24,28},{28,20},{20,12},{12,4},{4,0},{1,9},{9... | collective-permute-start | bytes 1769480 | tf_op jit(solution)/shard_map/ppermute | solution.py:100
  552.7 78.6 %collective-permute-start.132 = (bf16[256,2304]{1,0:T(8,128)(2,1)}, bf16[256,2304]{1,0:T(8,128)(2,1)S(1)}, u32[]{:S(2)}, u32[]{:S(2)}) collective-permute-start(bf16[256,2304]{1,0:T(8,128)(2,1)} %get-tuple-element.185), channel_id=1, source_target_pairs={{8,0},{16,8},{24,16},{28,24},{20,28},{12,20},{4,12},{0,4},{9,1},{1... | collective-permute-start | bytes 3538952 | tf_op jit(solution)/shard_map/ppermute | solution.py:99
  553.8 77.5 %collective-permute-start.133 = (bf16[256,2304]{1,0:T(8,128)(2,1)S(1)}, bf16[256,2304]{1,0:T(8,128)(2,1)}, u32[]{:S(2)}, u32[]{:S(2)}) collective-permute-start(bf16[256,2304]{1,0:T(8,128)(2,1)S(1)} %get-tuple-element.186), channel_id=1, source_target_pairs={{0,8},{8,16},{16,24},{24,28},{28,20},{20,12},{12,4},{4,0},{1,9},{9... | collective-permute-start | bytes 3538952 | tf_op jit(solution)/shard_map/ppermute | solution.py:100
  565.3 25.5 %collective-permute-start.152 = (bf16[256,1152]{1,0:T(8,128)(2,1)S(1)}, bf16[256,1152]{1,0:T(8,128)(2,1)S(1)}, u32[]{:S(2)}, u32[]{:S(2)}) collective-permute-start(bf16[256,1152]{1,0:T(8,128)(2,1)S(1)} %get-tuple-element.207), channel_id=1, source_target_pairs={{8,0},{16,8},{24,16},{28,24},{20,28},{12,20},{4,12},{0,4},{9,1},{1... | collective-permute-start | bytes 1769480 | tf_op jit(solution)/shard_map/ppermute | solution.py:99
  566.4 25.0 %collective-permute-start.153 = (bf16[256,1152]{1,0:T(8,128)(2,1)S(1)}, bf16[256,1152]{1,0:T(8,128)(2,1)S(1)}, u32[]{:S(2)}, u32[]{:S(2)}) collective-permute-start(bf16[256,1152]{1,0:T(8,128)(2,1)S(1)} %get-tuple-element.208), channel_id=1, source_target_pairs={{0,8},{8,16},{16,24},{24,28},{28,20},{20,12},{12,4},{4,0},{1,9},{9... | collective-permute-start | bytes 1769480 | tf_op jit(solution)/shard_map/ppermute | solution.py:100
  634.6 26.2 %collective-permute-start.134 = (bf16[256,2304]{1,0:T(8,128)(2,1)S(1)}, bf16[256,2304]{1,0:T(8,128)(2,1)S(1)}, u32[]{:S(2)}, u32[]{:S(2)}) collective-permute-start(bf16[256,2304]{1,0:T(8,128)(2,1)S(1)} %get-tuple-element.187), channel_id=1, source_target_pairs={{8,0},{16,8},{24,16},{28,24},{20,28},{12,20},{4,12},{0,4},{9,1},{1... | collective-permute-start | bytes 3538952 | tf_op jit(solution)/shard_map/ppermute | solution.py:99
  635.9 26.7 %collective-permute-start.135 = (bf16[256,2304]{1,0:T(8,128)(2,1)S(1)}, bf16[256,2304]{1,0:T(8,128)(2,1)S(1)}, u32[]{:S(2)}, u32[]{:S(2)}) collective-permute-start(bf16[256,2304]{1,0:T(8,128)(2,1)S(1)} %get-tuple-element.188), channel_id=1, source_target_pairs={{0,8},{8,16},{16,24},{24,28},{28,20},{20,12},{12,4},{4,0},{1,9},{9... | collective-permute-start | bytes 3538952 | tf_op jit(solution)/shard_map/ppermute | solution.py:100
  636.2 30.8 %collective-permute-start.85 = (bf16[2,128,2048]{2,1,0:T(8,128)(2,1)S(1)}, bf16[2,128,2048]{2,1,0:T(8,128)(2,1)S(1)}, u32[]{:S(2)}, u32[]{:S(2)}) collective-permute-start(bf16[2,128,2048]{2,1,0:T(8,128)(2,1)S(1)} %get-tuple-element.141), channel_id=1, source_target_pairs={{0,1},{1,0},{2,3},{3,2},{4,5},{5,4},{6,7},{7,6},{8,9},{9,8},{10,11... | collective-permute-start | bytes 3145736 | tf_op jit(solution)/shard_map/ppermute | solution.py:147
  640.7 31.4 %collective-permute-start.113 = (bf16[256,1024]{1,0:T(8,128)(2,1)S(1)}, bf16[256,1024]{1,0:T(8,128)(2,1)S(1)}, u32[]{:S(2)}, u32[]{:S(2)}) collective-permute-start(bf16[256,1024]{1,0:T(8,128)(2,1)S(1)} %get-tuple-element.165), channel_id=1, source_target_pairs={{8,0},{16,8},{24,16},{28,24},{20,28},{12,20},{4,12},{0,4},{9,1},{1... | collective-permute-start | bytes 1572872 | tf_op jit(solution)/shard_map/ppermute | solution.py:99
  642.2 31.6 %collective-permute-start.114 = (bf16[256,1024]{1,0:T(8,128)(2,1)S(1)}, bf16[256,1024]{1,0:T(8,128)(2,1)S(1)}, u32[]{:S(2)}, u32[]{:S(2)}) collective-permute-start(bf16[256,1024]{1,0:T(8,128)(2,1)S(1)} %get-tuple-element.166), channel_id=1, source_target_pairs={{0,8},{8,16},{16,24},{24,28},{28,20},{20,12},{12,4},{4,0},{1,9},{9... | collective-permute-start | bytes 1572872 | tf_op jit(solution)/shard_map/ppermute | solution.py:100
  665.1 32.3 %collective-permute-start.136 = (bf16[256,2304]{1,0:T(8,128)(2,1)S(1)}, bf16[256,2304]{1,0:T(8,128)(2,1)S(1)}, u32[]{:S(2)}, u32[]{:S(2)}) collective-permute-start(bf16[256,2304]{1,0:T(8,128)(2,1)S(1)} %get-tuple-element.189), channel_id=1, source_target_pairs={{8,0},{16,8},{24,16},{28,24},{20,28},{12,20},{4,12},{0,4},{9,1},{1... | collective-permute-start | bytes 3538952 | tf_op jit(solution)/shard_map/ppermute | solution.py:99
  665.5 33.6 %collective-permute-start.137 = (bf16[256,2304]{1,0:T(8,128)(2,1)S(1)}, bf16[256,2304]{1,0:T(8,128)(2,1)S(1)}, u32[]{:S(2)}, u32[]{:S(2)}) collective-permute-start(bf16[256,2304]{1,0:T(8,128)(2,1)S(1)} %get-tuple-element.190), channel_id=1, source_target_pairs={{0,8},{8,16},{16,24},{24,28},{28,20},{20,12},{12,4},{4,0},{1,9},{9... | collective-permute-start | bytes 3538952 | tf_op jit(solution)/shard_map/ppermute | solution.py:100
  674.8 33.8 %collective-permute-start.115 = (bf16[256,1024]{1,0:T(8,128)(2,1)S(1)}, bf16[256,1024]{1,0:T(8,128)(2,1)S(1)}, u32[]{:S(2)}, u32[]{:S(2)}) collective-permute-start(bf16[256,1024]{1,0:T(8,128)(2,1)S(1)} %get-tuple-element.167), channel_id=1, source_target_pairs={{8,0},{16,8},{24,16},{28,24},{20,28},{12,20},{4,12},{0,4},{9,1},{1... | collective-permute-start | bytes 1572872 | tf_op jit(solution)/shard_map/ppermute | solution.py:99
  674.9 35.4 %collective-permute-start.116 = (bf16[256,1024]{1,0:T(8,128)(2,1)S(1)}, bf16[256,1024]{1,0:T(8,128)(2,1)S(1)}, u32[]{:S(2)}, u32[]{:S(2)}) collective-permute-start(bf16[256,1024]{1,0:T(8,128)(2,1)S(1)} %get-tuple-element.168), channel_id=1, source_target_pairs={{0,8},{8,16},{16,24},{24,28},{28,20},{20,12},{12,4},{4,0},{1,9},{9... | collective-permute-start | bytes 1572872 | tf_op jit(solution)/shard_map/ppermute | solution.py:100
  680.3 26.3 %collective-permute-start.88 = (bf16[128,2048]{1,0:T(8,128)(2,1)S(1)}, bf16[128,2048]{1,0:T(8,128)(2,1)S(1)}, u32[]{:S(2)}, u32[]{:S(2)}) collective-permute-start(bf16[128,2048]{1,0:T(8,128)(2,1)S(1)} %get-tuple-element.265.refs_0_.refs_4_), channel_id=1, source_target_pairs={{0,2},{1,3},{2,0},{3,1},{4,6},{5,7},{6,4},{7,5},{8,10},{9,11},{10,... | collective-permute-start | bytes 1572872 | tf_op jit(solution)/shard_map/ppermute | solution.py:147
  712.1 28.0 %collective-permute-start.117 = (bf16[256,1024]{1,0:T(8,128)(2,1)}, bf16[256,1024]{1,0:T(8,128)(2,1)}, u32[]{:S(2)}, u32[]{:S(2)}) collective-permute-start(bf16[256,1024]{1,0:T(8,128)(2,1)} %get-tuple-element.169), channel_id=1, source_target_pairs={{8,0},{16,8},{24,16},{28,24},{20,28},{12,20},{4,12},{0,4},{9,1},{1... | collective-permute-start | bytes 1572872 | tf_op jit(solution)/shard_map/ppermute | solution.py:99
  712.1 28.0 %collective-permute-start.118 = (bf16[256,1024]{1,0:T(8,128)(2,1)}, bf16[256,1024]{1,0:T(8,128)(2,1)}, u32[]{:S(2)}, u32[]{:S(2)}) collective-permute-start(bf16[256,1024]{1,0:T(8,128)(2,1)} %get-tuple-element.170), channel_id=1, source_target_pairs={{0,8},{8,16},{16,24},{24,28},{28,20},{20,12},{12,4},{4,0},{1,9},{9... | collective-permute-start | bytes 1572872 | tf_op jit(solution)/shard_map/ppermute | solution.py:100
  744.9 215.0 %collective-permute-start.120 = (bf16[256,256]{1,0:T(8,128)(2,1)}, bf16[256,256]{1,0:T(8,128)(2,1)}, u32[]{:S(2)}, u32[]{:S(2)}) collective-permute-start(bf16[256,256]{1,0:T(8,128)(2,1)} %slice.674.refs_4_), channel_id=1, source_target_pairs={{0,2},{1,3},{2,0},{3,1},{4,6},{5,7},{6,4},{7,5},{8,10},{9,11},{10,... | collective-permute-start | bytes 393224 | tf_op jit(solution)/shard_map/ppermute | solution.py:147
  760.1 39.1 %collective-permute-start.122 = (bf16[128,2304]{1,0:T(8,128)(2,1)S(1)}, bf16[128,2304]{1,0:T(8,128)(2,1)S(1)}, u32[]{:S(2)}, u32[]{:S(2)}) collective-permute-start(bf16[128,2304]{1,0:T(8,128)(2,1)S(1)} %get-tuple-element.173), channel_id=1, source_target_pairs={{8,0},{16,8},{24,16},{28,24},{20,28},{12,20},{4,12},{0,4},{9,1},{1... | collective-permute-start | bytes 1769480 | tf_op jit(solution)/shard_map/ppermute | solution.py:99
  760.3 39.1 %collective-permute-start.123 = (bf16[128,2304]{1,0:T(8,128)(2,1)S(1)}, bf16[128,2304]{1,0:T(8,128)(2,1)S(1)}, u32[]{:S(2)}, u32[]{:S(2)}) collective-permute-start(bf16[128,2304]{1,0:T(8,128)(2,1)S(1)} %get-tuple-element.174), channel_id=1, source_target_pairs={{0,8},{8,16},{16,24},{24,28},{28,20},{20,12},{12,4},{4,0},{1,9},{9... | collective-permute-start | bytes 1769480 | tf_op jit(solution)/shard_map/ppermute | solution.py:100
  773.7 39.0 %collective-permute-start.140 = (bf16[256,1152]{1,0:T(8,128)(2,1)S(1)}, bf16[256,1152]{1,0:T(8,128)(2,1)S(1)}, u32[]{:S(2)}, u32[]{:S(2)}) collective-permute-start(bf16[256,1152]{1,0:T(8,128)(2,1)S(1)} %get-tuple-element.193), channel_id=1, source_target_pairs={{8,0},{16,8},{24,16},{28,24},{20,28},{12,20},{4,12},{0,4},{9,1},{1... | collective-permute-start | bytes 1769480 | tf_op jit(solution)/shard_map/ppermute | solution.py:99
  774.5 39.6 %collective-permute-start.141 = (bf16[256,1152]{1,0:T(8,128)(2,1)S(1)}, bf16[256,1152]{1,0:T(8,128)(2,1)S(1)}, u32[]{:S(2)}, u32[]{:S(2)}) collective-permute-start(bf16[256,1152]{1,0:T(8,128)(2,1)S(1)} %get-tuple-element.194), channel_id=1, source_target_pairs={{0,8},{8,16},{16,24},{24,28},{28,20},{20,12},{12,4},{4,0},{1,9},{9... | collective-permute-start | bytes 1769480 | tf_op jit(solution)/shard_map/ppermute | solution.py:100
  801.8 41.3 %collective-permute-start.124 = (bf16[256,2304]{1,0:T(8,128)(2,1)S(1)}, bf16[256,2304]{1,0:T(8,128)(2,1)S(1)}, u32[]{:S(2)}, u32[]{:S(2)}) collective-permute-start(bf16[256,2304]{1,0:T(8,128)(2,1)S(1)} %get-tuple-element.175), channel_id=1, source_target_pairs={{8,0},{16,8},{24,16},{28,24},{20,28},{12,20},{4,12},{0,4},{9,1},{1... | collective-permute-start | bytes 3538952 | tf_op jit(solution)/shard_map/ppermute | solution.py:99
  812.2 30.9 %collective-permute-start.125 = (bf16[256,2304]{1,0:T(8,128)(2,1)S(1)}, bf16[256,2304]{1,0:T(8,128)(2,1)S(1)}, u32[]{:S(2)}, u32[]{:S(2)}) collective-permute-start(bf16[256,2304]{1,0:T(8,128)(2,1)S(1)} %get-tuple-element.176), channel_id=1, source_target_pairs={{0,8},{8,16},{16,24},{24,28},{28,20},{20,12},{12,4},{4,0},{1,9},{9... | collective-permute-start | bytes 3538952 | tf_op jit(solution)/shard_map/ppermute | solution.py:100
  812.7 30.2 %collective-permute-start.96 = (bf16[4,2,64,256]{3,2,1,0:T(8,128)(2,1)S(1)}, bf16[4,2,64,256]{3,2,1,0:T(8,128)(2,1)S(1)}, u32[]{:S(2)}, u32[]{:S(2)}) collective-permute-start(bf16[4,2,64,256]{3,2,1,0:T(8,128)(2,1)S(1)} %select_convert_fusion.2), channel_id=1, source_target_pairs={{0,4},{4,0},{8,12},{12,8},{16,20},{20,16},{24,28},{28,24},{1,5},{5... | collective-permute-start | bytes 786440 | tf_op jit(solution)/shard_map/ppermute | solution.py:164
  815.0 49.7 %collective-permute-start.142 = (bf16[256,1152]{1,0:T(8,128)(2,1)S(1)}, bf16[256,1152]{1,0:T(8,128)(2,1)S(1)}, u32[]{:S(2)}, u32[]{:S(2)}) collective-permute-start(bf16[256,1152]{1,0:T(8,128)(2,1)S(1)} %get-tuple-element.195), channel_id=1, source_target_pairs={{8,0},{16,8},{24,16},{28,24},{20,28},{12,20},{4,12},{0,4},{9,1},{1... | collective-permute-start | bytes 1769480 | tf_op jit(solution)/shard_map/ppermute | solution.py:99
  842.9 29.1 %collective-permute-start.143 = (bf16[256,1152]{1,0:T(8,128)(2,1)S(1)}, bf16[256,1152]{1,0:T(8,128)(2,1)S(1)}, u32[]{:S(2)}, u32[]{:S(2)}) collective-permute-start(bf16[256,1152]{1,0:T(8,128)(2,1)S(1)} %get-tuple-element.196), channel_id=1, source_target_pairs={{0,8},{8,16},{16,24},{24,28},{28,20},{20,12},{12,4},{4,0},{1,9},{9... | collective-permute-start | bytes 1769480 | tf_op jit(solution)/shard_map/ppermute | solution.py:100
  845.7 35.4 %collective-permute-start.126 = (bf16[256,2304]{1,0:T(8,128)(2,1)S(1)}, bf16[256,2304]{1,0:T(8,128)(2,1)S(1)}, u32[]{:S(2)}, u32[]{:S(2)}) collective-permute-start(bf16[256,2304]{1,0:T(8,128)(2,1)S(1)} %get-tuple-element.177), channel_id=1, source_target_pairs={{8,0},{16,8},{24,16},{28,24},{20,28},{12,20},{4,12},{0,4},{9,1},{1... | collective-permute-start | bytes 3538952 | tf_op jit(solution)/shard_map/ppermute | solution.py:99
  857.9 24.7 %collective-permute-start.127 = (bf16[256,2304]{1,0:T(8,128)(2,1)S(1)}, bf16[256,2304]{1,0:T(8,128)(2,1)S(1)}, u32[]{:S(2)}, u32[]{:S(2)}) collective-permute-start(bf16[256,2304]{1,0:T(8,128)(2,1)S(1)} %get-tuple-element.178), channel_id=1, source_target_pairs={{0,8},{8,16},{16,24},{24,28},{28,20},{20,12},{12,4},{4,0},{1,9},{9... | collective-permute-start | bytes 3538952 | tf_op jit(solution)/shard_map/ppermute | solution.py:100
  873.8 102.4 %collective-permute-start.144 = (bf16[256,1152]{1,0:T(8,128)(2,1)}, bf16[256,1152]{1,0:T(8,128)(2,1)}, u32[]{:S(2)}, u32[]{:S(2)}) collective-permute-start(bf16[256,1152]{1,0:T(8,128)(2,1)} %get-tuple-element.197), channel_id=1, source_target_pairs={{8,0},{16,8},{24,16},{28,24},{20,28},{12,20},{4,12},{0,4},{9,1},{1... | collective-permute-start | bytes 1769480 | tf_op jit(solution)/shard_map/ppermute | solution.py:99
  875.6 100.7 %collective-permute-start.145 = (bf16[256,1152]{1,0:T(8,128)(2,1)}, bf16[256,1152]{1,0:T(8,128)(2,1)}, u32[]{:S(2)}, u32[]{:S(2)}) collective-permute-start(bf16[256,1152]{1,0:T(8,128)(2,1)} %get-tuple-element.199), channel_id=1, source_target_pairs={{0,8},{8,16},{16,24},{24,28},{28,20},{20,12},{12,4},{4,0},{1,9},{9... | collective-permute-start | bytes 1769480 | tf_op jit(solution)/shard_map/ppermute | solution.py:100
  886.0 28.3 %collective-permute-start.128 = (bf16[256,2304]{1,0:T(8,128)(2,1)}, bf16[256,2304]{1,0:T(8,128)(2,1)}, u32[]{:S(2)}, u32[]{:S(2)}) collective-permute-start(bf16[256,2304]{1,0:T(8,128)(2,1)} %get-tuple-element.179), channel_id=1, source_target_pairs={{8,0},{16,8},{24,16},{28,24},{20,28},{12,20},{4,12},{0,4},{9,1},{1... | collective-permute-start | bytes 3538952 | tf_op jit(solution)/shard_map/ppermute | solution.py:99
  892.1 28.5 %collective-permute-start.129 = (bf16[256,2304]{1,0:T(8,128)(2,1)}, bf16[256,2304]{1,0:T(8,128)(2,1)}, u32[]{:S(2)}, u32[]{:S(2)}) collective-permute-start(bf16[256,2304]{1,0:T(8,128)(2,1)} %get-tuple-element.181), channel_id=1, source_target_pairs={{0,8},{8,16},{16,24},{24,28},{28,20},{20,12},{12,4},{4,0},{1,9},{9... | collective-permute-start | bytes 3538952 | tf_op jit(solution)/shard_map/ppermute | solution.py:100
  959.9 47.4 %collective-permute-start.119 = (bf16[256,256]{1,0:T(8,128)(2,1)}, bf16[256,256]{1,0:T(8,128)(2,1)S(1)}, u32[]{:S(2)}, u32[]{:S(2)}) collective-permute-start(bf16[256,256]{1,0:T(8,128)(2,1)} %slice.674.refs_4_), channel_id=1, source_target_pairs={{0,1},{1,0},{2,3},{3,2},{4,5},{5,4},{6,7},{7,6},{8,9},{9,8},{10,11... | collective-permute-start | bytes 393224 | tf_op jit(solution)/shard_map/ppermute | solution.py:147
  976.2 31.0 %collective-permute-start.121 = (bf16[256,256]{1,0:T(8,128)(2,1)}, bf16[256,256]{1,0:T(8,128)(2,1)}, u32[]{:S(2)}, u32[]{:S(2)}) collective-permute-start(bf16[256,256]{1,0:T(8,128)(2,1)} %collective-permute-done.120.refs_6_), channel_id=1, source_target_pairs={{0,1},{1,0},{2,3},{3,2},{4,5},{5,4},{6,7},{7,6},{8,9},{9,8},{10,11... | collective-permute-start | bytes 393224 | tf_op jit(solution)/shard_map/ppermute | solution.py:147
  (360 other events, 4999.2 us)
